TPU v7x, 128 devices: a whole 4x4x4 slice. The times are simulated.
128 devices in a mesh: replica: 16 (over z_lo, x, core), shard: 8 (over y, z_hi).
Axes of the slice: x: 4, y: 4, z: 4 (z_hi: 2, z_lo: 2; z = z_hi * 2 + z_lo), core: 2. Of those that a mesh axis runs over, the one named last changes fastest.
Arguments:
- params: float32 [16, 128, 28672], P('replica', 'shard'), may hold values from -6 to 6
- first_moment: float32 [16, 128, 28672], P('replica', 'shard'), may hold values from -3 to 3
- second_moment: float32 [16, 128, 28672], P('replica', 'shard'), may hold values from 0.25 to 4
- grads: bfloat16 [4, 16, 128, 28672], P(None, 'replica', 'shard'), may hold values from -6 to 6
- push_weight: float32 [16], P('replica'), may hold values from 0.5 to 2
Outputs:
- final_weights: bfloat16 [16, 128, 28672], P('replica')
All inputs are finite; a program needn't handle non-finite values.
Results may differ from a plain program's by a relative error of at most 0.001.
Values may be sent and summed in bfloat16 or wider, within the bound.
No kernel may reach another device: no remote copies, remote signals or barrier semaphores. Data moves between devices by JAX's collectives and lax.ppermute only.
A program may use at most 64 MiB of HBM per device.

v0:
```python
import jax
import jax.numpy as jnp
from jax import lax
from jax.sharding import PartitionSpec as P

STEPS = 4


beta_one = 0.9
beta_two = 0.95
learn_rate = 0.1
decay_rate = 0.1
epsilon = 1e-08
adam_offset = 101


def passed_along(value, axis, steps):
    count = lax.axis_size(axis)
    pairs = [(source, (source + steps) % count) for source in range(count)]
    return lax.ppermute(value, axis, pairs)


def adam_block(numer, first_moment, second_moment, gradient, weight, first_fix, second_fix):
    scale = weight[:, None, None]
    current = numer / scale
    gradient = gradient.astype(jnp.float32)
    first_moment = beta_one * first_moment + (1.0 - beta_one) * gradient
    second_moment = beta_two * second_moment + (1.0 - beta_two) * gradient * gradient
    update = first_moment / first_fix / (jnp.sqrt(second_moment / second_fix) + epsilon)
    current = current - learn_rate * (update + decay_rate * current)
    return (current * scale, first_moment, second_moment)


def per_device(params, first_moment, second_moment, grads, push_weight):
    replicas = lax.axis_size("replica")
    levels = replicas.bit_length() - 1
    weight = push_weight
    numer = params * weight[:, None, None]
    for iteration in range(STEPS):
        distance = 2 ** (iteration % levels)
        count = adam_offset + iteration
        first_fix = 1.0 - beta_one**count
        second_fix = 1.0 - beta_two**count
        gradient = grads[iteration]
        numer, first_moment, second_moment = adam_block(
            numer, first_moment, second_moment, gradient, weight, first_fix, second_fix
        )
        arrived, arrived_weight = passed_along((numer, weight), "replica", distance)
        numer = 0.5 * numer + 0.5 * arrived
        weight = 0.5 * weight + 0.5 * arrived_weight
    result = (numer / weight[:, None, None]).astype(jnp.bfloat16)
    return lax.all_gather(result, "shard", axis=1, tiled=True)


def solution(mesh):
    return jax.shard_map(
        per_device,
        mesh=mesh,
        in_specs=(
            P("replica", "shard", None),
            P("replica", "shard", None),
            P("replica", "shard", None),
            P(None, "replica", "shard", None),
            P("replica"),
        ),
        out_specs=P("replica", None, None),
        check_vma=False,
    )
```

profile of v0, /device:TPU:0, one launch (start us, length us, event | category | flops | bytes accessed | tf_op | source)
XLA Modules:
  0.0 283.4 jit_solution(8978683002006352249)
XLA Ops:
  6.5 0.0 all-gather.2.cloned.1.call-start
  7.2 0.0 copy-start
  7.2 0.0 copy-start.1
  7.2 0.0 copy-start.2
  7.2 4.6 %subtract_multiply_fusion.2 = f32[1,16,28672]{2,1,0:T(8,128)S(1)} fusion(f32[1,16,28672]{2,1,0:T(8,128)} %param.5, f32[1,16,28672]{2,1,0:T(8,128)} %param.6, f32[1,16,28672]{2,1,0:T(8,128)} %param.7, f32[]{:T(128)} %bitcast.45, bf16[4,1,16,28672]{3,2,1,0:T(8,128)(2,1)} %param.8), kind=kLoop, calls=%fused_computation.32 | loop fusion | flops 8716288 | bytes 8257540 | tf_op jit(solution)/shard_map/mul | solution.py:31
  11.8 0.1 collective-permute-start
  11.9 1.7 collective-permute-start.1
  13.6 23.2 %collective-permute-done.1 = f32[1]{0:T(128)} collective-permute-done((f32[1]{0:T(128)}, f32[1]{0:T(128)}, u32[]{:S(2)}, u32[]{:S(2)}) %collective-permute-start.1) | collective-permute-done | bytes 36 | tf_op jit(solution)/shard_map/ppermute | solution.py:20
  37.4 0.0 collective-permute-done
  37.4 0.0 copy-done
  37.4 0.0 copy-done.1
  37.4 0.0 copy-done.2
  37.4 2.2 subtract_multiply_fusion.1
  39.6 0.1 collective-permute-start.2
  39.7 37.9 %collective-permute-start.3 = (f32[1]{0:T(128)}, f32[1]{0:T(128)}, u32[]{:S(2)}, u32[]{:S(2)}) collective-permute-start(f32[1]{0:T(128)} %add.83), channel_id=1, source_target_pairs={{0,16},{8,24},{16,32},{24,40},{32,48},{40,56},{48,64},{56,72},{64,... | collective-permute-start | bytes 20 | tf_op jit(solution)/shard_map/ppermute | solution.py:20
  77.6 3.2 %collective-permute-done.3 = f32[1]{0:T(128)} collective-permute-done((f32[1]{0:T(128)}, f32[1]{0:T(128)}, u32[]{:S(2)}, u32[]{:S(2)}) %collective-permute-start.3) | collective-permute-done | bytes 36 | tf_op jit(solution)/shard_map/ppermute | solution.py:20
  81.4 0.0 collective-permute-done.2
  81.5 2.7 subtract_multiply_fusion
  84.1 0.7 collective-permute-start.4
  84.8 37.1 %collective-permute-start.5 = (f32[1]{0:T(128)}, f32[1]{0:T(128)}, u32[]{:S(2)}, u32[]{:S(2)}) collective-permute-start(f32[1]{0:T(128)} %add.89), channel_id=1, source_target_pairs={{0,32},{8,40},{16,48},{24,56},{32,64},{40,72},{48,80},{56,88},{64,... | collective-permute-start | bytes 20 | tf_op jit(solution)/shard_map/ppermute | solution.py:20
  121.9 2.6 collective-permute-done.5
  125.1 0.0 collective-permute-done.4
  125.2 3.1 %fusion.12 = f32[1,16,28672]{2,1,0:T(8,128)S(1)} fusion(f32[1,16,28672]{2,1,0:T(8,128)S(1)} %subtract_multiply_fusion, f32[1,16,28672]{2,1,0:T(8,128)S(1)} %collective-permute-done.4, bf16[4,1,16,28672]{3,2,1,0:T(8,128)(2,1)S(1)} %copy-done.2, f32[]{:T(128)} %bitcast.9, f32[1,16,28672]{2,1,0:T(8,128)S(1)} %copy-done, f32[1,16,28672]{2,1,0:T(8,128)S(1)} %copy-done.1), kind=kLoop, calls=%fused_computation.24 | loop fusion | flops 20185088 | bytes 12845060 | tf_op jit(solution)/shard_map/mul | solution.py:31
  128.3 1.9 collective-permute-start.6
  130.2 34.2 %collective-permute-start.7 = (f32[1]{0:T(128)}, f32[1]{0:T(128)}, u32[]{:S(2)}, u32[]{:S(2)}) collective-permute-start(f32[1]{0:T(128)} %add.95), channel_id=1, source_target_pairs={{0,64},{8,72},{16,80},{24,88},{32,96},{40,104},{48,112},{56,120},{... | collective-permute-start | bytes 20 | tf_op jit(solution)/shard_map/ppermute | solution.py:20
  164.4 0.9 collective-permute-done.7
  165.8 0.0 collective-permute-done.6
  165.8 1.2 divide_convert_fusion
  167.1 0.0 all-gather.2.cloned.1.call-update
  167.1 102.6 %all-gather.2.cloned.1.call-done = bf16[1,128,28672]{2,1,0:T(8,128)(2,1)} async-done(((bf16[1,16,28672]{2,1,0:T(8,128)(2,1)}), bf16[1,128,28672]{2,1,0:T(8,128)(2,1)}) %all-gather.2.cloned.1.call-update) | async-done | bytes 7340048 | tf_op jit(solution)/shard_map/all_gather | solution.py:52
  269.7 6.8 %copy.8 = bf16[1,128,28672]{2,1,0:T(8,128)(2,1)} copy(bf16[1,128,28672]{2,1,0:T(8,128)(2,1)} %all-gather.2.cloned.1.call-done) | data formatting | bytes 14680064
Async XLA Ops:
  6.5 263.2 %all-gather.2.cloned.1.call-start = ((), (), s32[]{:S(2)}) async-start(), calls=%async_computation | async-start | bytes 8257536 | tf_op jit(solution)/shard_map/all_gather | solution.py:52
  7.2 30.2 %copy-start = (f32[1,16,28672]{2,1,0:T(8,128)S(1)}, f32[1,16,28672]{2,1,0:T(8,128)}, u32[]{:S(2)}) copy-start(f32[1,16,28672]{2,1,0:T(8,128)} %param.6) | copy-start | bytes 5505028
  7.2 30.2 %copy-start.1 = (f32[1,16,28672]{2,1,0:T(8,128)S(1)}, f32[1,16,28672]{2,1,0:T(8,128)}, u32[]{:S(2)}) copy-start(f32[1,16,28672]{2,1,0:T(8,128)} %param.7) | copy-start | bytes 5505028
  7.2 30.2 %copy-start.2 = (bf16[4,1,16,28672]{3,2,1,0:T(8,128)(2,1)S(1)}, bf16[4,1,16,28672]{3,2,1,0:T(8,128)(2,1)}, u32[]{:S(2)}) copy-start(bf16[4,1,16,28672]{3,2,1,0:T(8,128)(2,1)} %param.8) | copy-start | bytes 11010052
  11.8 25.6 %collective-permute-start = (f32[1,16,28672]{2,1,0:T(8,128)S(1)}, f32[1,16,28672]{2,1,0:T(8,128)S(1)}, u32[]{:S(2)}, u32[]{:S(2)}) collective-permute-start(f32[1,16,28672]{2,1,0:T(8,128)S(1)} %subtract_multiply_fusion.2), channel_id=1, source_target_pairs={{0,8},{8,16},{16,24},{24,32},{32,40},{40,48},{48,56},{56,64},{64,7... | collective-permute-start | bytes 5505032 | tf_op jit(solution)/shard_map/ppermute | solution.py:20
  11.9 24.9 %collective-permute-start.1 = (f32[1]{0:T(128)}, f32[1]{0:T(128)}, u32[]{:S(2)}, u32[]{:S(2)}) collective-permute-start(f32[1]{0:T(128)} %param.9), channel_id=1, source_target_pairs={{0,8},{8,16},{16,24},{24,32},{32,40},{40,48},{48,56},{56,64},{64,7... | collective-permute-start | bytes 20 | tf_op jit(solution)/shard_map/ppermute | solution.py:20
  39.6 41.8 %collective-permute-start.2 = (f32[1,16,28672]{2,1,0:T(8,128)S(1)}, f32[1,16,28672]{2,1,0:T(8,128)S(1)}, u32[]{:S(2)}, u32[]{:S(2)}) collective-permute-start(f32[1,16,28672]{2,1,0:T(8,128)S(1)} %subtract_multiply_fusion.1), channel_id=1, source_target_pairs={{0,16},{8,24},{16,32},{24,40},{32,48},{40,56},{48,64},{56,72},{64,... | collective-permute-start | bytes 5505032 | tf_op jit(solution)/shard_map/ppermute | solution.py:20
  39.7 41.2 %collective-permute-start.3 = (f32[1]{0:T(128)}, f32[1]{0:T(128)}, u32[]{:S(2)}, u32[]{:S(2)}) collective-permute-start(f32[1]{0:T(128)} %add.83), channel_id=1, source_target_pairs={{0,16},{8,24},{16,32},{24,40},{32,48},{40,56},{48,64},{56,72},{64,... | collective-permute-start | bytes 20 | tf_op jit(solution)/shard_map/ppermute | solution.py:20
  84.1 41.0 %collective-permute-start.4 = (f32[1,16,28672]{2,1,0:T(8,128)S(1)}, f32[1,16,28672]{2,1,0:T(8,128)S(1)}, u32[]{:S(2)}, u32[]{:S(2)}) collective-permute-start(f32[1,16,28672]{2,1,0:T(8,128)S(1)} %subtract_multiply_fusion), channel_id=1, source_target_pairs={{0,32},{8,40},{16,48},{24,56},{32,64},{40,72},{48,80},{56,88},{64,... | collective-permute-start | bytes 5505032 | tf_op jit(solution)/shard_map/ppermute | solution.py:20
  84.8 39.7 %collective-permute-start.5 = (f32[1]{0:T(128)}, f32[1]{0:T(128)}, u32[]{:S(2)}, u32[]{:S(2)}) collective-permute-start(f32[1]{0:T(128)} %add.89), channel_id=1, source_target_pairs={{0,32},{8,40},{16,48},{24,56},{32,64},{40,72},{48,80},{56,88},{64,... | collective-permute-start | bytes 20 | tf_op jit(solution)/shard_map/ppermute | solution.py:20
  128.3 37.5 %collective-permute-start.6 = (f32[1,16,28672]{2,1,0:T(8,128)S(1)}, f32[1,16,28672]{2,1,0:T(8,128)S(1)}, u32[]{:S(2)}, u32[]{:S(2)}) collective-permute-start(f32[1,16,28672]{2,1,0:T(8,128)S(1)} %fusion.12), channel_id=1, source_target_pairs={{0,64},{8,72},{16,80},{24,88},{32,96},{40,104},{48,112},{56,120},{... | collective-permute-start | bytes 5505032 | tf_op jit(solution)/shard_map/ppermute | solution.py:20
  130.2 35.0 %collective-permute-start.7 = (f32[1]{0:T(128)}, f32[1]{0:T(128)}, u32[]{:S(2)}, u32[]{:S(2)}) collective-permute-start(f32[1]{0:T(128)} %add.95), channel_id=1, source_target_pairs={{0,64},{8,72},{16,80},{24,88},{32,96},{40,104},{48,112},{56,120},{... | collective-permute-start | bytes 20 | tf_op jit(solution)/shard_map/ppermute | solution.py:20
Sparse Core Ops, SparseCore 0:
  167.2 102.4 all-gather.1
where the time goes:
time: 284 us; the launch traced here: 283 us
  waiting for transfers between devices  133 us (47%)
  starting transfers between devices  114 us (40%)
  between operations  16.4 us (6%)
  other arithmetic  13.8 us (5%)
  local copies, waits for them, and re-layouts  6.79 us (2%)
    ppermute x8, starting transfers between devices, passed_along(): return lax.ppermute(value, axis, pairs)  114 us
    all_gather x1, waiting for transfers between devices, per_device(): return lax.all_gather(result, 'shard', axis=1, tiled=True)  103 us
    ppermute x8, waiting for transfers between devices, passed_along(): return lax.ppermute(value, axis, pairs)  30 us
    mul x4, other arithmetic, adam_block(): return (current * scale, first_moment, second_moment)  12.6 us
    unnamed x7, local copies, waits for them, and re-layouts  6.79 us
  transfers between devices with their start and end apart: 9, of which 5 were waited for; matrix products, arithmetic and copies ran while one was open for 0% of the time, Pallas kernels for 0%

commit v1 on v0

v1 whole, which is shorter than its diff:
```python
import jax
import jax.numpy as jnp
import numpy as np
from jax import lax
from jax.sharding import PartitionSpec as P

STEPS = 4
REPLICAS = 16
beta_one = 0.9
beta_two = 0.95
learn_rate = 0.1
decay_rate = 0.1
epsilon = 1e-08
adam_offset = 101

AXES = ("replica", "shard")
DIMS = (2, 4, 2, 4, 2)


def moved(value, to):
    pairs = []
    for place in np.ndindex(*DIMS):
        z_lo, x, core, y, z_hi = place
        x, y, z, core = to(x, y, 2 * z_hi + z_lo, core)
        x, y, z = x % 4, y % 4, z % 4
        target = (z % 2, x, core, y, z // 2)
        pairs.append((int(np.ravel_multi_index(place, DIMS)), int(np.ravel_multi_index(target, DIMS))))
    return lax.ppermute(value, AXES, pairs)


def updates(first_moment, second_moment, grads):
    out = []
    for step in range(STEPS):
        count = adam_offset + step
        gradient = grads[step].astype(jnp.float32)
        first_moment = beta_one * first_moment + (1.0 - beta_one) * gradient
        second_moment = beta_two * second_moment + (1.0 - beta_two) * gradient * gradient
        first_fix = 1.0 - beta_one**count
        second_fix = 1.0 - beta_two**count
        out.append(first_moment / first_fix / (jnp.sqrt(second_moment / second_fix) + epsilon))
    return out


POWER = 15


def coded(value, bound):
    value = value * (2.0**8.5 / bound)
    second = value * value
    fourth = second * second
    return (value * second * fourth * (fourth * fourth)).astype(jnp.bfloat16)


def decoded(code, bound):
    code = code.astype(jnp.float32)
    root = jnp.exp(jnp.log(jnp.abs(code)) * (1.0 / POWER)) * (bound / 2.0**8.5)
    return jnp.where(code < 0, -root, root)


def gathered(piece, y, z):
    rows, cols = piece.shape
    half = cols // 2
    one, two = piece[:, :half], piece[:, half:]
    core = lax.axis_index("replica") % 2
    way = 1 - 2 * core
    along_y = lambda v: moved(v, lambda x, yy, zz, c: (x, yy + 1 - 2 * c, zz, c))
    along_z = lambda v: moved(v, lambda x, yy, zz, c: (x, yy, zz + 1 - 2 * c, c))
    out = jnp.zeros((4, 4, rows, cols), piece.dtype)

    def put(out, part, y_back, z_back, at):
        return lax.dynamic_update_slice(out, part[None, None], ((y - y_back * way) % 4, (z - z_back * way) % 4, 0, at))

    ones, twos = [one], [two]
    for step in range(1, 4):
        ones.append(along_y(ones[-1]))
        twos.append(along_z(twos[-1]))
    for group in ((0,), (1, 2), (3,)):
        block_one = jnp.concatenate([ones[k] for k in group]) if len(group) > 1 else ones[group[0]]
        block_two = jnp.concatenate([twos[k] for k in group]) if len(group) > 1 else twos[group[0]]
        for step in range(4):
            if step:
                block_one = along_z(block_one)
                block_two = along_y(block_two)
            for at, k in enumerate(group):
                out = put(out, block_one[rows * at : rows * at + rows], k, step, 0)
                out = put(out, block_two[rows * at : rows * at + rows], step, k, half)
    return out


def per_device(params, first_moment, second_moment, grads, push_weight):
    replica = lax.axis_index("replica")
    shard = lax.axis_index("shard")
    z_lo, y, z = replica // 8, shard // 2, 2 * (shard % 2) + replica // 8
    cols = params.shape[-1]
    keep = 1.0 - learn_rate * decay_rate

    behind = lambda v, steps: lax.ppermute(v, "replica", [(r, (r + steps) % REPLICAS) for r in range(REPLICAS)])
    one_behind = behind(push_weight, 1)
    four = push_weight + one_behind + behind(push_weight, 2) + behind(push_weight, 3)
    eight = four + behind(four, 4)
    sixteen = eight + behind(four, 8) + behind(four, 12)
    means = [v[0] for v in (push_weight, (push_weight + one_behind) / 2, four / 4, eight / 8, sixteen / 16)]

    halves = lambda v: v.reshape(2, 8, cols)
    u = [halves(v) for v in updates(first_moment[0], second_moment[0], grads[:, 0])]
    a = (keep**4 * halves(params[0]) - learn_rate * keep**3 * u[0]) * (push_weight[0] / 16.0)
    b = (-learn_rate * keep**2 / 8.0 * means[1]) * u[1]
    c = (-learn_rate * keep / 4.0 * means[2]) * u[2]
    d = (-learn_rate / 2.0 * means[3]) * u[3]

    mine = lambda v: jnp.where(z_lo == 0, v[0], v[1])
    other = lambda v: jnp.where(z_lo == 0, v[1], v[0])
    cores = lambda v: moved(v, lambda x, yy, zz, cc: (x, yy, zz, cc ^ 1))

    sent = lambda v, bound, to: decoded(moved(coded(v, bound), to), bound)
    out_a, own_a = other(a), mine(a)
    ab = mine(b) + own_a + cores(own_a) + sent(other(b) + out_a + cores(out_a), 2.0, lambda x, yy, zz, cc: (x, yy, zz ^ 1, cc))
    cz = mine(c) + sent(other(c), 0.5, lambda x, yy, zz, cc: (x, yy, zz ^ 1, cc))
    dz = mine(d) + sent(other(d), 1.0, lambda x, yy, zz, cc: (x, yy, zz ^ 1, cc))
    left, right = ab[:, : cols // 2], ab[:, cols // 2 :]
    left = left + sent(left, 4.0, lambda x, yy, zz, cc: (x ^ 1, yy, zz, cc))
    right = right + sent(right, 4.0, lambda x, yy, zz, cc: (3 - x, yy, zz, cc))
    total = jnp.concatenate([left, right], axis=1) + cz
    total = total + sent(total, 8.0, lambda x, yy, zz, cc: (x ^ 2, yy, zz, cc)) + dz
    piece = (total / means[4]).astype(jnp.bfloat16)
    return gathered(piece, y, z).reshape(1, 128, cols)


def solution(mesh):
    return jax.shard_map(
        per_device,
        mesh=mesh,
        in_specs=(
            P("replica", "shard", None),
            P("replica", "shard", None),
            P("replica", "shard", None),
            P(None, "replica", "shard", None),
            P("replica"),
        ),
        out_specs=P("replica", None, None),
        check_vma=False,
    )
```

time: 284 us -> 136 us (0.48)
  starting transfers between devices: 114 us -> 46.4 us
  waiting for transfers between devices: 133 us -> 66.7 us
  between operations: 16.4 us -> 4.79 us
    all_gather x1 -> x0, waiting for transfers between devices: 103 us -> none  [per_device(): return lax.all_gather(result, 'shard', axis=1, tiled=True)]
    ppermute x8 -> x38, starting transfers between devices: 114 us -> 46.4 us  [the longest x32 30.4 us: moved(): return lax.ppermute(value, AXES, pairs)]
    ppermute x8 -> x38, waiting for transfers between devices: 30 us -> 66.7 us  [the longest x32 59.8 us: moved(): return lax.ppermute(value, AXES, pairs)]
    mul x4 -> x1, other arithmetic: 12.6 us -> 7.5 us  [per_device(): b = -learn_rate * keep ** 2 / 8.0 * means[1] * u[1]]
    convert_element_type x1 -> x6, other arithmetic: 1.22 us -> 5.15 us  [the longest x5 3.3 us: coded(): return (value * second * fourth * (fourth * fourth)).astype(jnp.bfloat16)]
    unnamed x7 -> x2, local copies, waits for them, and re-layouts: 6.79 us -> 3.04 us
  transfers between devices with their start and end apart: 9 -> 38, of which waited for: 5 -> 20; matrix products, arithmetic and copies ran while one was open for 0% -> 4% of each run, Pallas kernels for 0% -> 0%
where the time goes in v1:
time: 136 us
  waiting for transfers between devices  66.7 us (49%)
  starting transfers between devices  46.4 us (34%)
  other arithmetic  13.7 us (10%)
  between operations  4.79 us (4%)
  local copies, waits for them, and re-layouts  4.52 us (3%)
    ppermute x32, waiting for transfers between devices, moved(): return lax.ppermute(value, AXES, pairs)  59.8 us
    ppermute x32, starting transfers between devices, moved(): return lax.ppermute(value, AXES, pairs)  30.4 us
    ppermute x6, starting transfers between devices, per_device(): lax.ppermute(v, 'replica', [(r, (r + steps) % REPLICAS) for r in range(RE...  16 us
    mul x1, other arithmetic, per_device(): b = -learn_rate * keep ** 2 / 8.0 * means[1] * u[1]  7.5 us
    ppermute x6, waiting for transfers between devices, per_device(): lax.ppermute(v, 'replica', [(r, (r + steps) % REPLICAS) for r in range(RE...  6.88 us
    convert_element_type x5, other arithmetic, coded(): return (value * second * fourth * (fourth * fourth)).astype(jnp.bfloat16)  3.3 us
    unnamed x2, local copies, waits for them, and re-layouts  3.04 us
  transfers between devices with their start and end apart: 38, of which 20 were waited for; matrix products, arithmetic and copies ran while one was open for 4% of the time, Pallas kernels for 0%

profile of v1, /device:TPU:0, one launch (start us, length us, event | category | flops | bytes accessed | tf_op | source)
XLA Modules:
  0.0 136.0 jit_solution(14146670618975457340)
XLA Ops:
  1.6 2.1 %collective-permute-start.7 = (f32[1]{0:T(128)}, f32[1]{0:T(128)}, u32[]{:S(2)}, u32[]{:S(2)}) collective-permute-start(f32[1]{0:T(128)} %param.9), channel_id=1, source_target_pairs={{0,24},{8,32},{16,40},{24,48},{32,56},{40,64},{48,72},{56,80},{64,... | collective-permute-start | bytes 20 | tf_op jit(solution)/shard_map/ppermute | solution.py:97
  7.7 3.3 %collective-permute-start.10 = (f32[1]{0:T(128)}, f32[1]{0:T(128)}, u32[]{:S(2)}, u32[]{:S(2)}) collective-permute-start(f32[1]{0:T(128)} %add.302), channel_id=1, source_target_pairs={{0,32},{8,40},{16,48},{24,56},{32,64},{40,72},{48,80},{56,88},{64,... | collective-permute-start | bytes 20 | tf_op jit(solution)/shard_map/ppermute | solution.py:97
  11.0 2.8 %collective-permute-done.10 = f32[1]{0:T(128)} collective-permute-done((f32[1]{0:T(128)}, f32[1]{0:T(128)}, u32[]{:S(2)}, u32[]{:S(2)}) %collective-permute-start.10) | collective-permute-done | bytes 36 | tf_op jit(solution)/shard_map/ppermute | solution.py:97
  14.4 7.5 %divide_multiply_fusion.1 = (f32[2,8,28672]{2,1,0:T(8,128)S(1)}, f32[2,8,28672]{2,1,0:T(8,128)S(1)}, f32[2,8,28672]{2,1,0:T(8,128)S(1)}, f32[2,8,28672]{2,1,0:T(8,128)S(1)}) fusion(f32[]{:T(128)} %bitcast, bf16[4,1,16,28672]{3,2,1,0:T(8,128)(2,1)} %param.8, f32[1,16,28672]{2,1,0:T(8,128)} %param.6, f32[1,16,28672]{2,1,0:T(8,128)} %param.7, f32[]{:T(128)} %bitcast.9, ...), kind=kLoop, calls=%fused_computation.29 | loop fusion | flops 25231360 | bytes 16515088 | tf_op jit(solution)/shard_map/mul | solution.py:107
  22.6 2.0 %collective-permute-done.2 = f32[8,28672]{1,0:T(8,128)S(1)} collective-permute-done((f32[8,28672]{1,0:T(8,128)S(1)}, f32[8,28672]{1,0:T(8,128)S(1)}, u32[]{:S(2)}, u32[]{:S(2)}) %collective-permute-start.2) | collective-permute-done | bytes 917536 | tf_op jit(solution)/shard_map/ppermute | solution.py:28
  25.0 2.0 %collective-permute-start.3 = (bf16[8,28672]{1,0:T(8,128)(2,1)S(1)}, bf16[8,28672]{1,0:T(8,128)(2,1)S(1)}, u32[]{:S(2)}, u32[]{:S(2)}) collective-permute-start(bf16[8,28672]{1,0:T(8,128)(2,1)S(1)} %fusion.33), channel_id=1, source_target_pairs={{0,64},{1,65},{2,66},{3,67},{4,68},{5,69},{6,70},{7,71},{8,72},{9,... | collective-permute-start | bytes 1376264 | tf_op jit(solution)/shard_map/ppermute | solution.py:28
  27.4 11.0 %collective-permute-done.3 = bf16[8,28672]{1,0:T(8,128)(2,1)S(1)} collective-permute-done((bf16[8,28672]{1,0:T(8,128)(2,1)S(1)}, bf16[8,28672]{1,0:T(8,128)(2,1)S(1)}, u32[]{:S(2)}, u32[]{:S(2)}) %collective-permute-start.3) | collective-permute-done | bytes 458784 | tf_op jit(solution)/shard_map/ppermute | solution.py:28
  41.8 1.8 %collective-permute-start.11 = (bf16[8,28672]{1,0:T(8,128)(2,1)}, bf16[8,28672]{1,0:T(8,128)(2,1)S(1)}, u32[]{:S(2)}, u32[]{:S(2)}) collective-permute-start(bf16[8,28672]{1,0:T(8,128)(2,1)} %fusion.42), channel_id=1, source_target_pairs={{0,64},{1,65},{2,66},{3,67},{4,68},{5,69},{6,70},{7,71},{8,72},{9,... | collective-permute-start | bytes 1376264 | tf_op jit(solution)/shard_map/ppermute | solution.py:28
  43.6 2.0 %collective-permute-done.4 = bf16[8,14336]{1,0:T(8,128)(2,1)S(1)} collective-permute-done((bf16[8,14336]{1,0:T(8,128)(2,1)S(1)}, bf16[8,14336]{1,0:T(8,128)(2,1)S(1)}, u32[]{:S(2)}, u32[]{:S(2)}) %collective-permute-start.4) | collective-permute-done | bytes 229408 | tf_op jit(solution)/shard_map/ppermute | solution.py:28
  45.6 2.4 %collective-permute-done.5 = bf16[8,14336]{1,0:T(8,128)(2,1)S(1)} collective-permute-done((bf16[8,14336]{1,0:T(8,128)(2,1)S(1)}, bf16[8,14336]{1,0:T(8,128)(2,1)S(1)}, u32[]{:S(2)}, u32[]{:S(2)}) %collective-permute-start.5) | collective-permute-done | bytes 229408 | tf_op jit(solution)/shard_map/ppermute | solution.py:28
  50.7 6.1 %collective-permute-start.12 = (f32[1]{0:T(128)}, f32[1]{0:T(128)}, u32[]{:S(2)}, u32[]{:S(2)}) collective-permute-start(f32[1]{0:T(128)} %add.302), channel_id=1, source_target_pairs={{0,64},{8,72},{16,80},{24,88},{32,96},{40,104},{48,112},{56,120},{... | collective-permute-start | bytes 20 | tf_op jit(solution)/shard_map/ppermute | solution.py:97
  56.8 2.9 %collective-permute-start.13 = (f32[1]{0:T(128)}, f32[1]{0:T(128)}, u32[]{:S(2)}, u32[]{:S(2)}) collective-permute-start(f32[1]{0:T(128)} %add.302), channel_id=1, source_target_pairs={{0,96},{8,104},{16,112},{24,120},{32,0},{40,8},{48,16},{56,24},{64... | collective-permute-start | bytes 20 | tf_op jit(solution)/shard_map/ppermute | solution.py:97
  60.3 2.6 %collective-permute-done.13 = f32[1]{0:T(128)} collective-permute-done((f32[1]{0:T(128)}, f32[1]{0:T(128)}, u32[]{:S(2)}, u32[]{:S(2)}) %collective-permute-start.13) | collective-permute-done | bytes 36 | tf_op jit(solution)/shard_map/ppermute | solution.py:97
  63.5 1.8 %fusion.55 = bf16[8,28672]{1,0:T(8,128)(2,1)S(1)} fusion(bf16[8,28672]{1,0:T(8,128)(2,1)S(1)} %collective-permute-done.11, f32[8,28672]{1,0:T(8,128)S(1)} %get-tuple-element.6, bf16[8,28672]{1,0:T(8,128)(2,1)} %collective-permute-done.9, f32[2,8,28672]{2,1,0:T(8,128)S(1)} %get-tuple-element.9, f32[]{:T(128)} %bitcast.23, pred[]{:T(512)S(6)} %eq.77), kind=kLoop, calls=%fused_computation.94 | loop fusion | flops 4587520 | bytes 4128773 | tf_op jit(solution)/shard_map/convert_element_type | solution.py:125
  65.4 1.6 %collective-permute-start.14 = (bf16[8,14336]{1,0:T(8,128)(2,1)S(1)}, bf16[8,14336]{1,0:T(8,128)(2,1)S(1)}, u32[]{:S(2)}, u32[]{:S(2)}) collective-permute-start(bf16[8,14336]{1,0:T(8,128)(2,1)S(1)} %get-tuple-element.18), channel_id=1, source_target_pairs={{0,64},{1,65},{2,66},{3,67},{4,68},{5,69},{6,70},{7,71},{8,73},{9,... | collective-permute-start | bytes 688136 | tf_op jit(solution)/shard_map/ppermute | solution.py:28
  70.2 1.9 %collective-permute-start.21 = (bf16[8,14336]{1,0:T(8,128)(2,1)S(1)}, bf16[8,14336]{1,0:T(8,128)(2,1)S(1)}, u32[]{:S(2)}, u32[]{:S(2)}) collective-permute-start(bf16[8,14336]{1,0:T(8,128)(2,1)S(1)} %get-tuple-element.17), channel_id=1, source_target_pairs={{0,64},{1,65},{2,66},{3,67},{4,68},{5,69},{6,70},{7,71},{8,73},{9,... | collective-permute-start | bytes 688136 | tf_op jit(solution)/shard_map/ppermute | solution.py:28
  74.6 2.1 %collective-permute-done.15 = bf16[8,14336]{1,0:T(8,128)(2,1)S(1)} collective-permute-done((bf16[8,14336]{1,0:T(8,128)(2,1)S(1)}, bf16[8,14336]{1,0:T(8,128)(2,1)S(1)}, u32[]{:S(2)}, u32[]{:S(2)}) %collective-permute-start.15) | collective-permute-done | bytes 229408 | tf_op jit(solution)/shard_map/ppermute | solution.py:28
  78.7 1.9 %collective-permute-start.23 = (bf16[8,14336]{1,0:T(8,128)(2,1)S(1)}, bf16[8,14336]{1,0:T(8,128)(2,1)S(1)}, u32[]{:S(2)}, u32[]{:S(2)}) collective-permute-start(bf16[8,14336]{1,0:T(8,128)(2,1)S(1)} %collective-permute-done.21), channel_id=1, source_target_pairs={{0,64},{1,65},{2,66},{3,67},{4,68},{5,69},{6,70},{7,71},{8,73},{9,... | collective-permute-start | bytes 688136 | tf_op jit(solution)/shard_map/ppermute | solution.py:28
  80.6 5.8 %collective-permute-done.22 = bf16[8,14336]{1,0:T(8,128)(2,1)S(1)} collective-permute-done((bf16[8,14336]{1,0:T(8,128)(2,1)S(1)}, bf16[8,14336]{1,0:T(8,128)(2,1)S(1)}, u32[]{:S(2)}, u32[]{:S(2)}) %collective-permute-start.22) | collective-permute-done | bytes 229408 | tf_op jit(solution)/shard_map/ppermute | solution.py:28
  86.4 2.0 %collective-permute-start.24 = (bf16[16,14336]{1,0:T(8,128)(2,1)S(1)}, bf16[16,14336]{1,0:T(8,128)(2,1)S(1)}, u32[]{:S(2)}, u32[]{:S(2)}) collective-permute-start(bf16[16,14336]{1,0:T(8,128)(2,1)S(1)} %pad_maximum_fusion), channel_id=1, source_target_pairs={{0,64},{1,65},{2,66},{3,67},{4,68},{5,69},{6,70},{7,71},{8,73},{9,... | collective-permute-start | bytes 1376264 | tf_op jit(solution)/shard_map/ppermute | solution.py:28
  89.3 1.6 %collective-permute-start.18 = (bf16[8,14336]{1,0:T(8,128)(2,1)S(1)}, bf16[8,14336]{1,0:T(8,128)(2,1)S(1)}, u32[]{:S(2)}, u32[]{:S(2)}) collective-permute-start(bf16[8,14336]{1,0:T(8,128)(2,1)S(1)} %collective-permute-done.16), channel_id=1, source_target_pairs={{0,64},{1,65},{2,66},{3,67},{4,68},{5,69},{6,70},{7,71},{8,73},{9,... | collective-permute-start | bytes 688136 | tf_op jit(solution)/shard_map/ppermute | solution.py:28
  92.2 6.4 %collective-permute-done.18 = bf16[8,14336]{1,0:T(8,128)(2,1)S(1)} collective-permute-done((bf16[8,14336]{1,0:T(8,128)(2,1)S(1)}, bf16[8,14336]{1,0:T(8,128)(2,1)S(1)}, u32[]{:S(2)}, u32[]{:S(2)}) %collective-permute-start.18) | collective-permute-done | bytes 229408 | tf_op jit(solution)/shard_map/ppermute | solution.py:28
  99.4 3.8 %collective-permute-done.19 = bf16[8,14336]{1,0:T(8,128)(2,1)S(1)} collective-permute-done((bf16[8,14336]{1,0:T(8,128)(2,1)S(1)}, bf16[8,14336]{1,0:T(8,128)(2,1)S(1)}, u32[]{:S(2)}, u32[]{:S(2)}) %collective-permute-start.19) | collective-permute-done | bytes 229408 | tf_op jit(solution)/shard_map/ppermute | solution.py:28
  103.3 1.7 %collective-permute-start.32 = (bf16[8,14336]{1,0:T(8,128)(2,1)S(1)}, bf16[8,14336]{1,0:T(8,128)(2,1)S(1)}, u32[]{:S(2)}, u32[]{:S(2)}) collective-permute-start(bf16[8,14336]{1,0:T(8,128)(2,1)S(1)} %collective-permute-done.30), channel_id=1, source_target_pairs={{0,64},{1,65},{2,66},{3,67},{4,68},{5,69},{6,70},{7,71},{8,73},{9,... | collective-permute-start | bytes 688136 | tf_op jit(solution)/shard_map/ppermute | solution.py:28
  105.9 1.8 %collective-permute-start.27 = (bf16[16,14336]{1,0:T(8,128)(2,1)S(1)}, bf16[16,14336]{1,0:T(8,128)(2,1)S(1)}, u32[]{:S(2)}, u32[]{:S(2)}) collective-permute-start(bf16[16,14336]{1,0:T(8,128)(2,1)S(1)} %collective-permute-done.25), channel_id=1, source_target_pairs={{0,2},{1,3},{2,4},{3,5},{4,6},{5,7},{6,0},{7,1},{8,14},{9,15},{10,... | collective-permute-start | bytes 1376264 | tf_op jit(solution)/shard_map/ppermute | solution.py:28
  107.8 2.8 %collective-permute-done.32 = bf16[8,14336]{1,0:T(8,128)(2,1)S(1)} collective-permute-done((bf16[8,14336]{1,0:T(8,128)(2,1)S(1)}, bf16[8,14336]{1,0:T(8,128)(2,1)S(1)}, u32[]{:S(2)}, u32[]{:S(2)}) %collective-permute-start.32) | collective-permute-done | bytes 229408 | tf_op jit(solution)/shard_map/ppermute | solution.py:28
  111.0 2.1 %collective-permute-done.33 = bf16[8,14336]{1,0:T(8,128)(2,1)S(1)} collective-permute-done((bf16[8,14336]{1,0:T(8,128)(2,1)S(1)}, bf16[8,14336]{1,0:T(8,128)(2,1)S(1)}, u32[]{:S(2)}, u32[]{:S(2)}) %collective-permute-start.33) | collective-permute-done | bytes 229408 | tf_op jit(solution)/shard_map/ppermute | solution.py:28
  113.1 4.9 %collective-permute-done.34 = bf16[8,14336]{1,0:T(8,128)(2,1)S(1)} collective-permute-done((bf16[8,14336]{1,0:T(8,128)(2,1)S(1)}, bf16[8,14336]{1,0:T(8,128)(2,1)S(1)}, u32[]{:S(2)}, u32[]{:S(2)}) %collective-permute-start.34) | collective-permute-done | bytes 229408 | tf_op jit(solution)/shard_map/ppermute | solution.py:28
  118.4 2.1 %collective-permute-done.35 = bf16[8,14336]{1,0:T(8,128)(2,1)S(1)} collective-permute-done((bf16[8,14336]{1,0:T(8,128)(2,1)S(1)}, bf16[8,14336]{1,0:T(8,128)(2,1)S(1)}, u32[]{:S(2)}, u32[]{:S(2)}) %collective-permute-start.35) | collective-permute-done | bytes 229408 | tf_op jit(solution)/shard_map/ppermute | solution.py:28
  121.2 8.9 %collective-permute-done.28 = bf16[16,14336]{1,0:T(8,128)(2,1)S(1)} collective-permute-done((bf16[16,14336]{1,0:T(8,128)(2,1)S(1)}, bf16[16,14336]{1,0:T(8,128)(2,1)S(1)}, u32[]{:S(2)}, u32[]{:S(2)}) %collective-permute-start.28) | collective-permute-done | bytes 458784 | tf_op jit(solution)/shard_map/ppermute | solution.py:28
  130.2 2.4 %collective-permute-done.29 = bf16[16,14336]{1,0:T(8,128)(2,1)S(1)} collective-permute-done((bf16[16,14336]{1,0:T(8,128)(2,1)S(1)}, bf16[16,14336]{1,0:T(8,128)(2,1)S(1)}, u32[]{:S(2)}, u32[]{:S(2)}) %collective-permute-start.29) | collective-permute-done | bytes 458784 | tf_op jit(solution)/shard_map/ppermute | solution.py:28
  133.0 3.0 %copy-done = bf16[4,4,8,28672]{3,2,1,0:T(8,128)(2,1)} copy-done((bf16[4,4,8,28672]{3,2,1,0:T(8,128)(2,1)}, bf16[4,4,8,28672]{3,2,1,0:T(8,128)(2,1)S(1)}, u32[]{:S(2)}) %copy-start) | copy-done | bytes 7340056
  (92 shorter events, 24.1 us)
Async XLA Ops:
  7.7 6.1 %collective-permute-start.10 = (f32[1]{0:T(128)}, f32[1]{0:T(128)}, u32[]{:S(2)}, u32[]{:S(2)}) collective-permute-start(f32[1]{0:T(128)} %add.302), channel_id=1, source_target_pairs={{0,32},{8,40},{16,48},{24,56},{32,64},{40,72},{48,80},{56,88},{64,... | collective-permute-start | bytes 20 | tf_op jit(solution)/shard_map/ppermute | solution.py:97
  25.0 13.4 %collective-permute-start.3 = (bf16[8,28672]{1,0:T(8,128)(2,1)S(1)}, bf16[8,28672]{1,0:T(8,128)(2,1)S(1)}, u32[]{:S(2)}, u32[]{:S(2)}) collective-permute-start(bf16[8,28672]{1,0:T(8,128)(2,1)S(1)} %fusion.33), channel_id=1, source_target_pairs={{0,64},{1,65},{2,66},{3,67},{4,68},{5,69},{6,70},{7,71},{8,72},{9,... | collective-permute-start | bytes 1376264 | tf_op jit(solution)/shard_map/ppermute | solution.py:28
  27.2 21.2 %collective-permute-start.8 = (bf16[8,28672]{1,0:T(8,128)(2,1)S(1)}, bf16[8,28672]{1,0:T(8,128)(2,1)S(1)}, u32[]{:S(2)}, u32[]{:S(2)}) collective-permute-start(bf16[8,28672]{1,0:T(8,128)(2,1)S(1)} %fusion.36), channel_id=1, source_target_pairs={{0,64},{1,65},{2,66},{3,67},{4,68},{5,69},{6,70},{7,71},{8,72},{9,... | collective-permute-start | bytes 1376264 | tf_op jit(solution)/shard_map/ppermute | solution.py:28
  39.1 6.5 %collective-permute-start.4 = (bf16[8,14336]{1,0:T(8,128)(2,1)S(1)}, bf16[8,14336]{1,0:T(8,128)(2,1)S(1)}, u32[]{:S(2)}, u32[]{:S(2)}) collective-permute-start(bf16[8,14336]{1,0:T(8,128)(2,1)S(1)} %get-tuple-element.15), channel_id=1, source_target_pairs={{0,16},{1,17},{2,18},{3,19},{4,20},{5,21},{6,22},{7,23},{8,24},{9,... | collective-permute-start | bytes 688136 | tf_op jit(solution)/shard_map/ppermute | solution.py:28
  40.7 7.3 %collective-permute-start.5 = (bf16[8,14336]{1,0:T(8,128)(2,1)S(1)}, bf16[8,14336]{1,0:T(8,128)(2,1)S(1)}, u32[]{:S(2)}, u32[]{:S(2)}) collective-permute-start(bf16[8,14336]{1,0:T(8,128)(2,1)S(1)} %get-tuple-element.16), channel_id=1, source_target_pairs={{0,48},{1,49},{2,50},{3,51},{4,52},{5,53},{6,54},{7,55},{8,56},{9,... | collective-permute-start | bytes 688136 | tf_op jit(solution)/shard_map/ppermute | solution.py:28
  41.8 21.7 %collective-permute-start.11 = (bf16[8,28672]{1,0:T(8,128)(2,1)}, bf16[8,28672]{1,0:T(8,128)(2,1)S(1)}, u32[]{:S(2)}, u32[]{:S(2)}) collective-permute-start(bf16[8,28672]{1,0:T(8,128)(2,1)} %fusion.42), channel_id=1, source_target_pairs={{0,64},{1,65},{2,66},{3,67},{4,68},{5,69},{6,70},{7,71},{8,72},{9,... | collective-permute-start | bytes 1376264 | tf_op jit(solution)/shard_map/ppermute | solution.py:28
  49.8 13.7 %collective-permute-start.9 = (bf16[8,28672]{1,0:T(8,128)(2,1)}, bf16[8,28672]{1,0:T(8,128)(2,1)}, u32[]{:S(2)}, u32[]{:S(2)}) collective-permute-start(bf16[8,28672]{1,0:T(8,128)(2,1)} %get-tuple-element.5), channel_id=1, source_target_pairs={{0,32},{1,33},{2,34},{3,35},{4,36},{5,37},{6,38},{7,39},{8,40},{9,... | collective-permute-start | bytes 1376264 | tf_op jit(solution)/shard_map/ppermute | solution.py:28
  50.7 9.0 %collective-permute-start.12 = (f32[1]{0:T(128)}, f32[1]{0:T(128)}, u32[]{:S(2)}, u32[]{:S(2)}) collective-permute-start(f32[1]{0:T(128)} %add.302), channel_id=1, source_target_pairs={{0,64},{8,72},{16,80},{24,88},{32,96},{40,104},{48,112},{56,120},{... | collective-permute-start | bytes 20 | tf_op jit(solution)/shard_map/ppermute | solution.py:97
  65.4 7.7 %collective-permute-start.14 = (bf16[8,14336]{1,0:T(8,128)(2,1)S(1)}, bf16[8,14336]{1,0:T(8,128)(2,1)S(1)}, u32[]{:S(2)}, u32[]{:S(2)}) collective-permute-start(bf16[8,14336]{1,0:T(8,128)(2,1)S(1)} %get-tuple-element.18), channel_id=1, source_target_pairs={{0,64},{1,65},{2,66},{3,67},{4,68},{5,69},{6,70},{7,71},{8,73},{9,... | collective-permute-start | bytes 688136 | tf_op jit(solution)/shard_map/ppermute | solution.py:28
  67.0 10.1 %collective-permute-start.20 = (bf16[8,14336]{1,0:T(8,128)(2,1)S(1)}, bf16[8,14336]{1,0:T(8,128)(2,1)S(1)}, u32[]{:S(2)}, u32[]{:S(2)}) collective-permute-start(bf16[8,14336]{1,0:T(8,128)(2,1)S(1)} %get-tuple-element.18), channel_id=1, source_target_pairs={{0,2},{1,3},{2,4},{3,5},{4,6},{5,7},{6,0},{7,1},{8,14},{9,15},{10,... | collective-permute-start | bytes 688136 | tf_op jit(solution)/shard_map/ppermute | solution.py:28
  68.6 8.1 %collective-permute-start.15 = (bf16[8,14336]{1,0:T(8,128)(2,1)S(1)}, bf16[8,14336]{1,0:T(8,128)(2,1)S(1)}, u32[]{:S(2)}, u32[]{:S(2)}) collective-permute-start(bf16[8,14336]{1,0:T(8,128)(2,1)S(1)} %get-tuple-element.17), channel_id=1, source_target_pairs={{0,2},{1,3},{2,4},{3,5},{4,6},{5,7},{6,0},{7,1},{8,14},{9,15},{10,... | collective-permute-start | bytes 688136 | tf_op jit(solution)/shard_map/ppermute | solution.py:28
  70.2 8.5 %collective-permute-start.21 = (bf16[8,14336]{1,0:T(8,128)(2,1)S(1)}, bf16[8,14336]{1,0:T(8,128)(2,1)S(1)}, u32[]{:S(2)}, u32[]{:S(2)}) collective-permute-start(bf16[8,14336]{1,0:T(8,128)(2,1)S(1)} %get-tuple-element.17), channel_id=1, source_target_pairs={{0,64},{1,65},{2,66},{3,67},{4,68},{5,69},{6,70},{7,71},{8,73},{9,... | collective-permute-start | bytes 688136 | tf_op jit(solution)/shard_map/ppermute | solution.py:28
  73.1 16.1 %collective-permute-start.16 = (bf16[8,14336]{1,0:T(8,128)(2,1)S(1)}, bf16[8,14336]{1,0:T(8,128)(2,1)S(1)}, u32[]{:S(2)}, u32[]{:S(2)}) collective-permute-start(bf16[8,14336]{1,0:T(8,128)(2,1)S(1)} %collective-permute-done.14), channel_id=1, source_target_pairs={{0,64},{1,65},{2,66},{3,67},{4,68},{5,69},{6,70},{7,71},{8,73},{9,... | collective-permute-start | bytes 688136 | tf_op jit(solution)/shard_map/ppermute | solution.py:28
  76.7 14.2 %collective-permute-start.17 = (bf16[8,14336]{1,0:T(8,128)(2,1)S(1)}, bf16[8,14336]{1,0:T(8,128)(2,1)S(1)}, u32[]{:S(2)}, u32[]{:S(2)}) collective-permute-start(bf16[8,14336]{1,0:T(8,128)(2,1)S(1)} %collective-permute-done.15), channel_id=1, source_target_pairs={{0,2},{1,3},{2,4},{3,5},{4,6},{5,7},{6,0},{7,1},{8,14},{9,15},{10,... | collective-permute-start | bytes 688136 | tf_op jit(solution)/shard_map/ppermute | solution.py:28
  77.1 9.3 %collective-permute-start.22 = (bf16[8,14336]{1,0:T(8,128)(2,1)S(1)}, bf16[8,14336]{1,0:T(8,128)(2,1)S(1)}, u32[]{:S(2)}, u32[]{:S(2)}) collective-permute-start(bf16[8,14336]{1,0:T(8,128)(2,1)S(1)} %collective-permute-done.20), channel_id=1, source_target_pairs={{0,2},{1,3},{2,4},{3,5},{4,6},{5,7},{6,0},{7,1},{8,14},{9,15},{10,... | collective-permute-start | bytes 688136 | tf_op jit(solution)/shard_map/ppermute | solution.py:28
  78.7 9.8 %collective-permute-start.23 = (bf16[8,14336]{1,0:T(8,128)(2,1)S(1)}, bf16[8,14336]{1,0:T(8,128)(2,1)S(1)}, u32[]{:S(2)}, u32[]{:S(2)}) collective-permute-start(bf16[8,14336]{1,0:T(8,128)(2,1)S(1)} %collective-permute-done.21), channel_id=1, source_target_pairs={{0,64},{1,65},{2,66},{3,67},{4,68},{5,69},{6,70},{7,71},{8,73},{9,... | collective-permute-start | bytes 688136 | tf_op jit(solution)/shard_map/ppermute | solution.py:28
  86.4 19.5 %collective-permute-start.24 = (bf16[16,14336]{1,0:T(8,128)(2,1)S(1)}, bf16[16,14336]{1,0:T(8,128)(2,1)S(1)}, u32[]{:S(2)}, u32[]{:S(2)}) collective-permute-start(bf16[16,14336]{1,0:T(8,128)(2,1)S(1)} %pad_maximum_fusion), channel_id=1, source_target_pairs={{0,64},{1,65},{2,66},{3,67},{4,68},{5,69},{6,70},{7,71},{8,73},{9,... | collective-permute-start | bytes 1376264 | tf_op jit(solution)/shard_map/ppermute | solution.py:28
  88.5 17.5 %collective-permute-start.25 = (bf16[16,14336]{1,0:T(8,128)(2,1)S(1)}, bf16[16,14336]{1,0:T(8,128)(2,1)S(1)}, u32[]{:S(2)}, u32[]{:S(2)}) collective-permute-start(bf16[16,14336]{1,0:T(8,128)(2,1)S(1)} %pad_maximum_fusion.1), channel_id=1, source_target_pairs={{0,2},{1,3},{2,4},{3,5},{4,6},{5,7},{6,0},{7,1},{8,14},{9,15},{10,... | collective-permute-start | bytes 1376264 | tf_op jit(solution)/shard_map/ppermute | solution.py:28
  88.5 14.7 %collective-permute-start.30 = (bf16[8,14336]{1,0:T(8,128)(2,1)S(1)}, bf16[8,14336]{1,0:T(8,128)(2,1)S(1)}, u32[]{:S(2)}, u32[]{:S(2)}) collective-permute-start(bf16[8,14336]{1,0:T(8,128)(2,1)S(1)} %collective-permute-done.22), channel_id=1, source_target_pairs={{0,2},{1,3},{2,4},{3,5},{4,6},{5,7},{6,0},{7,1},{8,14},{9,15},{10,... | collective-permute-start | bytes 688136 | tf_op jit(solution)/shard_map/ppermute | solution.py:28
  89.3 9.4 %collective-permute-start.18 = (bf16[8,14336]{1,0:T(8,128)(2,1)S(1)}, bf16[8,14336]{1,0:T(8,128)(2,1)S(1)}, u32[]{:S(2)}, u32[]{:S(2)}) collective-permute-start(bf16[8,14336]{1,0:T(8,128)(2,1)S(1)} %collective-permute-done.16), channel_id=1, source_target_pairs={{0,64},{1,65},{2,66},{3,67},{4,68},{5,69},{6,70},{7,71},{8,73},{9,... | collective-permute-start | bytes 688136 | tf_op jit(solution)/shard_map/ppermute | solution.py:28
  90.9 12.2 %collective-permute-start.19 = (bf16[8,14336]{1,0:T(8,128)(2,1)S(1)}, bf16[8,14336]{1,0:T(8,128)(2,1)S(1)}, u32[]{:S(2)}, u32[]{:S(2)}) collective-permute-start(bf16[8,14336]{1,0:T(8,128)(2,1)S(1)} %collective-permute-done.17), channel_id=1, source_target_pairs={{0,2},{1,3},{2,4},{3,5},{4,6},{5,7},{6,0},{7,1},{8,14},{9,15},{10,... | collective-permute-start | bytes 688136 | tf_op jit(solution)/shard_map/ppermute | solution.py:28
  98.6 7.2 %collective-permute-start.31 = (bf16[8,14336]{1,0:T(8,128)(2,1)S(1)}, bf16[8,14336]{1,0:T(8,128)(2,1)S(1)}, u32[]{:S(2)}, u32[]{:S(2)}) collective-permute-start(bf16[8,14336]{1,0:T(8,128)(2,1)S(1)} %collective-permute-done.23), channel_id=1, source_target_pairs={{0,64},{1,65},{2,66},{3,67},{4,68},{5,69},{6,70},{7,71},{8,73},{9,... | collective-permute-start | bytes 688136 | tf_op jit(solution)/shard_map/ppermute | solution.py:28
  103.3 7.3 %collective-permute-start.32 = (bf16[8,14336]{1,0:T(8,128)(2,1)S(1)}, bf16[8,14336]{1,0:T(8,128)(2,1)S(1)}, u32[]{:S(2)}, u32[]{:S(2)}) collective-permute-start(bf16[8,14336]{1,0:T(8,128)(2,1)S(1)} %collective-permute-done.30), channel_id=1, source_target_pairs={{0,64},{1,65},{2,66},{3,67},{4,68},{5,69},{6,70},{7,71},{8,73},{9,... | collective-permute-start | bytes 688136 | tf_op jit(solution)/shard_map/ppermute | solution.py:28
  105.9 7.2 %collective-permute-start.33 = (bf16[8,14336]{1,0:T(8,128)(2,1)S(1)}, bf16[8,14336]{1,0:T(8,128)(2,1)S(1)}, u32[]{:S(2)}, u32[]{:S(2)}) collective-permute-start(bf16[8,14336]{1,0:T(8,128)(2,1)S(1)} %collective-permute-done.31), channel_id=1, source_target_pairs={{0,2},{1,3},{2,4},{3,5},{4,6},{5,7},{6,0},{7,1},{8,14},{9,15},{10,... | collective-permute-start | bytes 688136 | tf_op jit(solution)/shard_map/ppermute | solution.py:28
  105.9 14.6 %collective-permute-start.26 = (bf16[16,14336]{1,0:T(8,128)(2,1)S(1)}, bf16[16,14336]{1,0:T(8,128)(2,1)S(1)}, u32[]{:S(2)}, u32[]{:S(2)}) collective-permute-start(bf16[16,14336]{1,0:T(8,128)(2,1)S(1)} %collective-permute-done.24), channel_id=1, source_target_pairs={{0,64},{1,65},{2,66},{3,67},{4,68},{5,69},{6,70},{7,71},{8,73},{9,... | collective-permute-start | bytes 1376264 | tf_op jit(solution)/shard_map/ppermute | solution.py:28
  105.9 14.6 %collective-permute-start.27 = (bf16[16,14336]{1,0:T(8,128)(2,1)S(1)}, bf16[16,14336]{1,0:T(8,128)(2,1)S(1)}, u32[]{:S(2)}, u32[]{:S(2)}) collective-permute-start(bf16[16,14336]{1,0:T(8,128)(2,1)S(1)} %collective-permute-done.25), channel_id=1, source_target_pairs={{0,2},{1,3},{2,4},{3,5},{4,6},{5,7},{6,0},{7,1},{8,14},{9,15},{10,... | collective-permute-start | bytes 1376264 | tf_op jit(solution)/shard_map/ppermute | solution.py:28
  110.6 7.4 %collective-permute-start.34 = (bf16[8,14336]{1,0:T(8,128)(2,1)S(1)}, bf16[8,14336]{1,0:T(8,128)(2,1)S(1)}, u32[]{:S(2)}, u32[]{:S(2)}) collective-permute-start(bf16[8,14336]{1,0:T(8,128)(2,1)S(1)} %collective-permute-done.32), channel_id=1, source_target_pairs={{0,64},{1,65},{2,66},{3,67},{4,68},{5,69},{6,70},{7,71},{8,73},{9,... | collective-permute-start | bytes 688136 | tf_op jit(solution)/shard_map/ppermute | solution.py:28
  113.1 7.4 %collective-permute-start.35 = (bf16[8,14336]{1,0:T(8,128)(2,1)S(1)}, bf16[8,14336]{1,0:T(8,128)(2,1)S(1)}, u32[]{:S(2)}, u32[]{:S(2)}) collective-permute-start(bf16[8,14336]{1,0:T(8,128)(2,1)S(1)} %collective-permute-done.33), channel_id=1, source_target_pairs={{0,2},{1,3},{2,4},{3,5},{4,6},{5,7},{6,0},{7,1},{8,14},{9,15},{10,... | collective-permute-start | bytes 688136 | tf_op jit(solution)/shard_map/ppermute | solution.py:28
  118.0 14.9 %collective-permute-start.36 = (bf16[8,14336]{1,0:T(8,128)(2,1)S(1)}, bf16[8,14336]{1,0:T(8,128)(2,1)S(1)}, u32[]{:S(2)}, u32[]{:S(2)}) collective-permute-start(bf16[8,14336]{1,0:T(8,128)(2,1)S(1)} %collective-permute-done.34), channel_id=1, source_target_pairs={{0,64},{1,65},{2,66},{3,67},{4,68},{5,69},{6,70},{7,71},{8,73},{9,... | collective-permute-start | bytes 688136 | tf_op jit(solution)/shard_map/ppermute | solution.py:28
  120.5 12.5 %collective-permute-start.37 = (bf16[8,14336]{1,0:T(8,128)(2,1)S(1)}, bf16[8,14336]{1,0:T(8,128)(2,1)S(1)}, u32[]{:S(2)}, u32[]{:S(2)}) collective-permute-start(bf16[8,14336]{1,0:T(8,128)(2,1)S(1)} %collective-permute-done.35), channel_id=1, source_target_pairs={{0,2},{1,3},{2,4},{3,5},{4,6},{5,7},{6,0},{7,1},{8,14},{9,15},{10,... | collective-permute-start | bytes 688136 | tf_op jit(solution)/shard_map/ppermute | solution.py:28
  120.5 9.7 %collective-permute-start.28 = (bf16[16,14336]{1,0:T(8,128)(2,1)S(1)}, bf16[16,14336]{1,0:T(8,128)(2,1)S(1)}, u32[]{:S(2)}, u32[]{:S(2)}) collective-permute-start(bf16[16,14336]{1,0:T(8,128)(2,1)S(1)} %collective-permute-done.26), channel_id=1, source_target_pairs={{0,64},{1,65},{2,66},{3,67},{4,68},{5,69},{6,70},{7,71},{8,73},{9,... | collective-permute-start | bytes 1376264 | tf_op jit(solution)/shard_map/ppermute | solution.py:28
  120.5 12.1 %collective-permute-start.29 = (bf16[16,14336]{1,0:T(8,128)(2,1)S(1)}, bf16[16,14336]{1,0:T(8,128)(2,1)S(1)}, u32[]{:S(2)}, u32[]{:S(2)}) collective-permute-start(bf16[16,14336]{1,0:T(8,128)(2,1)S(1)} %collective-permute-done.27), channel_id=1, source_target_pairs={{0,2},{1,3},{2,4},{3,5},{4,6},{5,7},{6,0},{7,1},{8,14},{9,15},{10,... | collective-permute-start | bytes 1376264 | tf_op jit(solution)/shard_map/ppermute | solution.py:28
  (7 other events, 33.6 us)

commit v2 on v0

v2 whole, which is shorter than its diff:
```python
import jax
import jax.numpy as jnp
import numpy as np
from jax import lax
from jax.experimental import pallas as pl
from jax.experimental.pallas import tpu as pltpu
from jax.sharding import PartitionSpec as P

STEPS = 4
REPLICAS = 16
beta_one = 0.9
beta_two = 0.95
learn_rate = 0.1
decay_rate = 0.1
epsilon = 1e-08
adam_offset = 101

AXES = ("replica", "shard")
DIMS = (2, 4, 2, 4, 2)


def moved(value, to):
    pairs = []
    for place in np.ndindex(*DIMS):
        z_lo, x, core, y, z_hi = place
        x, y, z, core = to(x, y, 2 * z_hi + z_lo, core)
        x, y, z = x % 4, y % 4, z % 4
        target = (z % 2, x, core, y, z // 2)
        pairs.append((int(np.ravel_multi_index(place, DIMS)), int(np.ravel_multi_index(target, DIMS))))
    return lax.ppermute(value, AXES, pairs)


POWER = 15


def coded(value, bound):
    value = value * (2.0**8.5 / bound)
    second = value * value
    fourth = second * second
    return (value * second * fourth * (fourth * fourth)).astype(jnp.bfloat16)


KEEP = 1.0 - learn_rate * decay_rate
BLOCK = 14336


def moments(first_moment, second_moment, grads, steps):
    for step in range(steps):
        gradient = grads[step].astype(jnp.float32)
        first_moment = beta_one * first_moment + (1.0 - beta_one) * gradient
        second_moment = beta_two * second_moment + (1.0 - beta_two) * gradient * gradient
    return first_moment, second_moment


def update(first_moment, second_moment, step):
    count = adam_offset + step
    first_fix = 1.0 - beta_one**count
    second_fix = 1.0 - beta_two**count
    return first_moment * (1.0 / first_fix) / (jnp.sqrt(second_moment * (1.0 / second_fix)) + epsilon)


def first_kernel(weight, params, first_moment, second_moment, grads, out):
    now = moments(first_moment[0], second_moment[0], grads[0], 1)
    out[...] = (KEEP**4 * params[0] - learn_rate * KEEP**3 * update(*now, 0)) * (weight[0] / 16.0)


SMEM = pl.BlockSpec(memory_space=pltpu.SMEM)


def moment_spec(start=0):
    return pl.BlockSpec((1, 16, BLOCK), lambda i: (0, 0, i + start))


def grad_spec(steps, start=0):
    return pl.BlockSpec((steps, 1, 16, BLOCK), lambda i: (0, 0, 0, i + start))


def first_term(weight, params, first_moment, second_moment, grads):
    cols = params.shape[-1]
    spec = pl.BlockSpec((1, 16, BLOCK), lambda i: (0, 0, i))
    return pl.pallas_call(
        first_kernel,
        grid=(cols // BLOCK,),
        in_specs=[SMEM, spec, spec, spec, pl.BlockSpec((1, 1, 16, BLOCK), lambda i: (0, 0, 0, i))],
        out_specs=pl.BlockSpec((16, BLOCK), lambda i: (0, i)),
        out_shape=jax.ShapeDtypeStruct((16, cols), jnp.float32),
        cost_estimate=pl.CostEstimate(flops=20 * 16 * cols, transcendentals=2 * 16 * cols, bytes_accessed=18 * 16 * cols),
    )(weight, params, first_moment, second_moment, grads)


def decoded(code, bound):
    code = code.astype(jnp.float32)
    root = jnp.exp(jnp.log(jnp.abs(code)) * (1.0 / POWER)) * (bound / 2.0**8.5)
    return jnp.where(code < 0, -root, root)


def gathered(one, two, y, z):
    rows, half = one.shape
    along_y = lambda v, s: moved(v, lambda x, yy, zz, c: (x, yy + s, zz, c))
    along_z = lambda v, s: moved(v, lambda x, yy, zz, c: (x, yy, zz + s, c))

    def line(v, along, at):
        block = jnp.zeros((4, rows, half), v.dtype)
        block = lax.dynamic_update_slice(block, v[None], (at, 0, 0))
        for s in (1, -1, 2):
            block = lax.dynamic_update_slice(block, along(v, s)[None], ((at - s) % 4, 0, 0))
        return block

    def blocks(v, along):
        ahead, back = along(v, -1), along(v, 1)
        far = jnp.concatenate([along(back[:2], 1), along(ahead[2:], -1)])
        return ((v, 0), (back, -1), (ahead, 1), (far, 2))

    one, two = line(one, along_y, y), line(two, along_z, z)
    out = jnp.zeros((4, 4, rows, 2 * half), one.dtype)
    for (block_one, off), (block_two, _) in zip(blocks(one, along_z), blocks(two, along_y)):
        out = lax.dynamic_update_slice(out, block_one[:, None], (0, (z + off) % 4, 0, 0))
        out = lax.dynamic_update_slice(out, block_two[None], ((y + off) % 4, 0, 0, half))
    return out


def per_device(params, first_moment, second_moment, grads, push_weight):
    replica = lax.axis_index("replica")
    shard = lax.axis_index("shard")
    z_lo, y, z = replica // 8, shard // 2, 2 * (shard % 2) + replica // 8
    cols = params.shape[-1]
    half = cols // 2
    ring = lambda v, steps: lax.ppermute(v, "replica", [(r, (r + steps) % REPLICAS) for r in range(REPLICAS)])
    mixed = lambda v, steps: 0.5 * v + 0.5 * ring(v, steps)
    mine = lambda v: jnp.where(z_lo == 0, v[:8], v[8:])
    other = lambda v: jnp.where(z_lo == 0, v[8:], v[:8])
    cores = lambda x, yy, zz, cc: (x, yy, zz, cc ^ 1)
    across = lambda x, yy, zz, cc: (x, yy, zz ^ 1, cc)
    far = lambda x, yy, zz, cc: (x ^ 2, yy, zz, cc)
    near = (lambda x, yy, zz, cc: (x ^ 1, yy, zz, cc), lambda x, yy, zz, cc: (3 - x, yy, zz, cc))

    state = (first_moment[0], second_moment[0], grads[:, 0])
    sides = [slice(side * half, side * half + half) for side in range(2)]
    a = first_term(push_weight, params, first_moment, second_moment, grads)
    a_there = moved(a, cores)
    weight_one = mixed(push_weight, 1)

    factor = -learn_rate * KEEP**2 / 8.0 * weight_one[0]
    parts, codes = [], []
    for part in sides:
        local = lax.optimization_barrier((state, a, a_there, factor))
        b = local[3] * update(*moments(local[0][0][:, part], local[0][1][:, part], local[0][2][:, :, part], 2), 1)
        ab = local[1][:, part] + local[2][:, part] + b
        parts.append(ab)
        codes.append(coded(ab, 4.0))
    codes, parts, state = lax.optimization_barrier((codes, parts, state))
    c = (-learn_rate * KEEP / 4.0) * update(*moments(*state, 3), 2)
    d = (-learn_rate / 2.0) * update(*moments(*state, 4), 3)
    c, d, d_code, weight_one = lax.optimization_barrier((c, mine(d), coded(other(d), 1.0), weight_one))
    weight_two = mixed(weight_one, 2)
    near_there = [moved(codes[side], near[side]) for side in range(2)]
    parts = [parts[side] + decoded(near_there[side], 4.0) + weight_two[0] * c[:, sides[side]] for side in range(2)]
    codes = [coded(other(part), 4.0) for part in parts]
    codes, d_code, weight_two = lax.optimization_barrier((codes, d_code, weight_two))
    d_there = moved(d_code, across)
    weight_three = mixed(weight_two, 4)
    there = [moved(code, across) for code in codes]
    there, weight_three = lax.optimization_barrier((there, weight_three))
    parts = [mine(parts[side]) + decoded(there[side], 4.0) for side in range(2)]
    codes = [coded(part, 8.0) for part in parts]
    codes, weight_three = lax.optimization_barrier((codes, weight_three))
    weight_three_there = ring(weight_three, 8)
    weight_four = 0.5 * weight_three[0] + 0.5 * weight_three_there[0]

    pieces = []
    for side, part in enumerate(sides):
        own = weight_three[0] * d[:, part] + weight_three_there[0] * decoded(d_there[:, part], 1.0)
        total = parts[side] + decoded(moved(codes[side], far), 8.0) + own
        pieces.append((total / weight_four).astype(jnp.bfloat16))
    return gathered(*pieces, y, z).reshape(1, 128, cols)


def solution(mesh):
    return jax.shard_map(
        per_device,
        mesh=mesh,
        in_specs=(
            P("replica", "shard", None),
            P("replica", "shard", None),
            P("replica", "shard", None),
            P(None, "replica", "shard", None),
            P("replica"),
        ),
        out_specs=P("replica", None, None),
        check_vma=False,
    )
```

time: 284 us -> 115 us (0.40)
  waiting for transfers between devices: 133 us -> 44.3 us
  starting transfers between devices: 114 us -> 40.9 us
  between operations: 16.4 us -> 3.49 us
  Pallas kernels: 0 us -> 4.59 us
  other arithmetic: 13.8 us -> 16.9 us
    all_gather x1 -> x0, waiting for transfers between devices: 103 us -> none  [per_device(): return lax.all_gather(result, 'shard', axis=1, tiled=True)]
    ppermute x8 -> x26, starting transfers between devices: 114 us -> 40.9 us  [the longest x22 33.8 us: moved(): return lax.ppermute(value, AXES, pairs)]
    ppermute x8 -> x26, waiting for transfers between devices: 30 us -> 44.3 us  [the longest x22 29.5 us: moved(): return lax.ppermute(value, AXES, pairs)]
    mul x4 -> x1, other arithmetic: 12.6 us -> 3.48 us  [per_device(): d = -learn_rate / 2.0 * update(*moments(*state, 4), 3)]
    convert_element_type x1 -> x5, other arithmetic: 1.22 us -> 7.88 us  [coded(): return (value * second * fourth * (fourth * fourth)).astype(jnp.bfloat16)]
    dynamic_update_slice x0 -> x4, other arithmetic: none -> 4.7 us  [the longest x2 4.52 us: line(): block = lax.dynamic_update_slice(block, v[None], (at, 0, 0))]
    pallas_call x0 -> x1, Pallas kernels: none -> 4.59 us  [first_term(): pl.pallas_call(first_kernel, grid=(cols // BLOCK,), in_specs=[SMEM, spec,...]
    unnamed x7 -> x8, local copies, waits for them, and re-layouts: 6.79 us -> 3.06 us
  transfers between devices with their start and end apart: 9 -> 26, of which waited for: 5 -> 11; matrix products, arithmetic and copies ran while one was open for 0% -> 11% of each run, Pallas kernels for 0% -> 0%
where the time goes in v2:
time: 115 us
  waiting for transfers between devices  44.3 us (39%)
  starting transfers between devices  40.9 us (36%)
  other arithmetic  16.9 us (15%)
  local copies, waits for them, and re-layouts  4.62 us (4%)
  Pallas kernels  4.59 us (4%)
  between operations  3.49 us (3%)
    ppermute x22, starting transfers between devices, moved(): return lax.ppermute(value, AXES, pairs)  33.8 us
    ppermute x22, waiting for transfers between devices, moved(): return lax.ppermute(value, AXES, pairs)  29.5 us
    ppermute x4, waiting for transfers between devices, per_device(): lax.ppermute(v, 'replica', [(r, (r + steps) % REPLICAS) for r in range(RE...  14.7 us
    convert_element_type x5, other arithmetic, coded(): return (value * second * fourth * (fourth * fourth)).astype(jnp.bfloat16)  7.88 us
    ppermute x4, starting transfers between devices, per_device(): lax.ppermute(v, 'replica', [(r, (r + steps) % REPLICAS) for r in range(RE...  7.17 us
    pallas_call x1, Pallas kernels, first_term(): pl.pallas_call(first_kernel, grid=(cols // BLOCK,), in_specs=[SMEM, spec,...  4.59 us
    dynamic_update_slice x2, other arithmetic, line(): block = lax.dynamic_update_slice(block, v[None], (at, 0, 0))  4.52 us
    mul x1, other arithmetic, per_device(): d = -learn_rate / 2.0 * update(*moments(*state, 4), 3)  3.48 us
  transfers between devices with their start and end apart: 26, of which 11 were waited for; matrix products, arithmetic and copies ran while one was open for 11% of the time, Pallas kernels for 0%

profile of v2, /device:TPU:0, one launch (start us, length us, event | category | flops | bytes accessed | tf_op | source)
XLA Modules:
  0.0 114.8 jit_solution(13337015178164614624)
XLA Ops:
  0.7 4.6 %shard_map.55 = f32[16,28672]{1,0:T(8,128)} custom-call(f32[1]{0:T(128)S(6)} %copy.26.weight, f32[1,16,28672]{2,1,0:T(8,128)} %params.1, f32[1,16,28672]{2,1,0:T(8,128)} %first_moment.1, f32[1,16,28672]{2,1,0:T(8,128)} %second_moment.1, bf16[4,1,16,28672]{3,2,1,0:T(8,128)(2,1)} %grads.1), custom_call_target="tpu_custom_call" | custom-call | flops 9175040 | bytes 8257536 | tf_op jit(solution)/shard_map/pallas_call | solution.py:81
  5.8 5.3 %collective-permute-done.1 = f32[1]{0:T(128)} collective-permute-done((f32[1]{0:T(128)}, f32[1]{0:T(128)}, u32[]{:S(2)}, u32[]{:S(2)}) %collective-permute-start.1) | collective-permute-done | bytes 36 | tf_op jit(solution)/shard_map/ppermute | solution.py:128
  11.6 4.5 %fusion.31 = (bf16[16,14336]{1,0:T(8,128)(2,1)S(1)}, f32[16,14336]{1,0:T(8,128)S(1)}, bf16[16,14336]{1,0:T(8,128)(2,1)S(1)}, f32[16,14336]{1,0:T(8,128)S(1)}) fusion(f32[16,28672]{1,0:T(8,128)} %bitcast.111, bf16[4,16,28672]{2,1,0:T(8,128)(2,1)} %bitcast.107, f32[16,28672]{1,0:T(8,128)S(1)} %bitcast.109, f32[]{:T(128)} %bitcast.3, ...), kind=kLoop, calls=%fused_computation.68 | loop fusion | flops 14221312 | bytes 11927556 | tf_op jit(solution)/shard_map/convert_element_type | solution.py:40
  16.3 1.7 %collective-permute-start.4 = (bf16[16,14336]{1,0:T(8,128)(2,1)S(1)}, bf16[16,14336]{1,0:T(8,128)(2,1)S(1)}, u32[]{:S(2)}, u32[]{:S(2)}) collective-permute-start(bf16[16,14336]{1,0:T(8,128)(2,1)S(1)} %get-tuple-element.46), channel_id=1, source_target_pairs={{0,48},{1,49},{2,50},{3,51},{4,52},{5,53},{6,54},{7,55},{8,56},{9,... | collective-permute-start | bytes 1376264 | tf_op jit(solution)/shard_map/ppermute | solution.py:30
  18.0 3.5 %fusion.13 = (f32[16,28672]{1,0:T(8,128)S(1)}, f32[16,28672]{1,0:T(8,128)S(1)}) fusion(bf16[4,16,28672]{2,1,0:T(8,128)(2,1)S(1)} %bitcast.108, f32[16,28672]{1,0:T(8,128)S(1)} %bitcast.110, f32[16,28672]{1,0:T(8,128)S(1)} %bitcast.112), kind=kLoop, calls=%fused_computation.25 | loop fusion | flops 19267584 | bytes 11010048 | tf_op jit(solution)/shard_map/mul | solution.py:153
  22.5 3.7 %collective-permute-start.3 = (f32[1]{0:T(128)}, f32[1]{0:T(128)}, u32[]{:S(2)}, u32[]{:S(2)}) collective-permute-start(f32[1]{0:T(128)} %add.254), channel_id=1, source_target_pairs={{0,16},{8,24},{16,32},{24,40},{32,48},{40,56},{48,64},{56,72},{64,... | collective-permute-start | bytes 20 | tf_op jit(solution)/shard_map/ppermute | solution.py:128
  26.2 4.7 %collective-permute-done.3 = f32[1]{0:T(128)} collective-permute-done((f32[1]{0:T(128)}, f32[1]{0:T(128)}, u32[]{:S(2)}, u32[]{:S(2)}) %collective-permute-start.3) | collective-permute-done | bytes 36 | tf_op jit(solution)/shard_map/ppermute | solution.py:128
  32.9 1.9 %collective-permute-start.6 = (bf16[8,14336]{1,0:T(8,128)(2,1)S(1)}, bf16[8,14336]{1,0:T(8,128)(2,1)S(1)}, u32[]{:S(2)}, u32[]{:S(2)}) collective-permute-start(bf16[8,14336]{1,0:T(8,128)(2,1)S(1)} %get-tuple-element.49), channel_id=1, source_target_pairs={{0,64},{1,65},{2,66},{3,67},{4,68},{5,69},{6,70},{7,71},{8,72},{9,... | collective-permute-start | bytes 688136 | tf_op jit(solution)/shard_map/ppermute | solution.py:30
  36.3 1.9 %collective-permute-start.10 = (bf16[8,28672]{1,0:T(8,128)(2,1)}, bf16[8,28672]{1,0:T(8,128)(2,1)}, u32[]{:S(2)}, u32[]{:S(2)}) collective-permute-start(bf16[8,28672]{1,0:T(8,128)(2,1)} %get-tuple-element.57), channel_id=1, source_target_pairs={{0,64},{1,65},{2,66},{3,67},{4,68},{5,69},{6,70},{7,71},{8,72},{9,... | collective-permute-start | bytes 1376264 | tf_op jit(solution)/shard_map/ppermute | solution.py:30
  38.2 2.6 %collective-permute-done.7 = f32[1]{0:T(128)} collective-permute-done((f32[1]{0:T(128)}, f32[1]{0:T(128)}, u32[]{:S(2)}, u32[]{:S(2)}) %collective-permute-start.7) | collective-permute-done | bytes 36 | tf_op jit(solution)/shard_map/ppermute | solution.py:128
  41.5 4.7 %collective-permute-done.6 = bf16[8,14336]{1,0:T(8,128)(2,1)S(1)} collective-permute-done((bf16[8,14336]{1,0:T(8,128)(2,1)S(1)}, bf16[8,14336]{1,0:T(8,128)(2,1)S(1)}, u32[]{:S(2)}, u32[]{:S(2)}) %collective-permute-start.6) | collective-permute-done | bytes 229408 | tf_op jit(solution)/shard_map/ppermute | solution.py:30
  48.5 3.3 %collective-permute-start.14 = (bf16[8,14336]{1,0:T(8,128)(2,1)}, bf16[8,14336]{1,0:T(8,128)(2,1)}, u32[]{:S(2)}, u32[]{:S(2)}) collective-permute-start(bf16[8,14336]{1,0:T(8,128)(2,1)} %fusion.102), channel_id=1, source_target_pairs={{0,32},{1,33},{2,34},{3,35},{4,36},{5,37},{6,38},{7,39},{8,40},{9,... | collective-permute-start | bytes 688136 | tf_op jit(solution)/shard_map/ppermute | solution.py:30
  53.2 2.2 %collective-permute-done.9 = f32[1]{0:T(128)} collective-permute-done((f32[1]{0:T(128)}, f32[1]{0:T(128)}, u32[]{:S(2)}, u32[]{:S(2)}) %collective-permute-start.9) | collective-permute-done | bytes 36 | tf_op jit(solution)/shard_map/ppermute | solution.py:128
  56.2 2.2 %bitcast_dynamic-update-slice_fusion.13 = (bf16[4,8,14336]{2,1,0:T(8,128)(2,1)S(1)}, bf16[8,14336]{1,0:T(8,128)(2,1)S(1)}) fusion(bf16[4,8,14336]{2,1,0:T(8,128)(2,1)S(1)} %broadcast.85.clone, s32[]{:T(128)S(6)} %select_n.177, f32[]{:T(128)S(6)} %add.265, bf16[8,28672]{1,0:T(8,128)(2,1)} %collective-permute-done.10, f32[]{:T(128)} %bitcast.22, ...), kind=kLoop, calls=%fused_computation.196 | loop fusion | flops 3440640 | bytes 2523153 | tf_op jit(solution)/shard_map/dynamic_update_slice | solution.py:104
  58.4 1.6 %collective-permute-start.11 = (bf16[8,14336]{1,0:T(8,128)(2,1)S(1)}, bf16[8,14336]{1,0:T(8,128)(2,1)S(1)}, u32[]{:S(2)}, u32[]{:S(2)}) collective-permute-start(bf16[8,14336]{1,0:T(8,128)(2,1)S(1)} %get-tuple-element.62), channel_id=1, source_target_pairs={{0,2},{1,3},{2,4},{3,5},{4,6},{5,7},{6,0},{7,1},{8,10},{9,11},{10,... | collective-permute-start | bytes 688136 | tf_op jit(solution)/shard_map/ppermute | solution.py:30
  60.1 2.3 %bitcast_dynamic-update-slice_fusion.9 = (bf16[4,8,14336]{2,1,0:T(8,128)(2,1)S(1)}, bf16[8,14336]{1,0:T(8,128)(2,1)S(1)}) fusion(bf16[4,8,14336]{2,1,0:T(8,128)(2,1)S(1)} %broadcast.85.clone.1, s32[]{:T(128)S(6)} %select_n.189, f32[]{:T(128)S(6)} %add.265, bf16[8,28672]{1,0:T(8,128)(2,1)} %collective-permute-done.10, f32[]{:T(128)} %bitcast.22, ...), kind=kLoop, calls=%fused_computation.192 | loop fusion | flops 3440640 | bytes 2523153 | tf_op jit(solution)/shard_map/dynamic_update_slice | solution.py:104
  62.8 3.0 %collective-permute-start.16 = (bf16[8,14336]{1,0:T(8,128)(2,1)S(1)}, bf16[8,14336]{1,0:T(8,128)(2,1)S(1)}, u32[]{:S(2)}, u32[]{:S(2)}) collective-permute-start(bf16[8,14336]{1,0:T(8,128)(2,1)S(1)} %get-tuple-element.60), channel_id=1, source_target_pairs={{0,65},{1,64},{2,67},{3,66},{4,69},{5,68},{6,71},{7,70},{8,73},{9,... | collective-permute-start | bytes 688136 | tf_op jit(solution)/shard_map/ppermute | solution.py:30
  65.9 2.4 %collective-permute-start.17 = (bf16[8,14336]{1,0:T(8,128)(2,1)S(1)}, bf16[8,14336]{1,0:T(8,128)(2,1)S(1)}, u32[]{:S(2)}, u32[]{:S(2)}) collective-permute-start(bf16[8,14336]{1,0:T(8,128)(2,1)S(1)} %get-tuple-element.60), channel_id=1, source_target_pairs={{0,1},{1,0},{2,3},{3,2},{4,5},{5,4},{6,7},{7,6},{8,9},{9,8},{10,11... | collective-permute-start | bytes 688136 | tf_op jit(solution)/shard_map/ppermute | solution.py:30
  68.3 1.7 %collective-permute-start.12 = (bf16[8,14336]{1,0:T(8,128)(2,1)S(1)}, bf16[8,14336]{1,0:T(8,128)(2,1)S(1)}, u32[]{:S(2)}, u32[]{:S(2)}) collective-permute-start(bf16[8,14336]{1,0:T(8,128)(2,1)S(1)} %get-tuple-element.62), channel_id=1, source_target_pairs={{0,6},{1,7},{2,0},{3,1},{4,2},{5,3},{6,4},{7,5},{8,14},{9,15},{10,... | collective-permute-start | bytes 688136 | tf_op jit(solution)/shard_map/ppermute | solution.py:30
  69.9 2.0 %collective-permute-start.13 = (bf16[8,14336]{1,0:T(8,128)(2,1)S(1)}, bf16[8,14336]{1,0:T(8,128)(2,1)S(1)}, u32[]{:S(2)}, u32[]{:S(2)}) collective-permute-start(bf16[8,14336]{1,0:T(8,128)(2,1)S(1)} %get-tuple-element.62), channel_id=1, source_target_pairs={{0,4},{1,5},{2,6},{3,7},{4,0},{5,1},{6,2},{7,3},{8,12},{9,13},{10,... | collective-permute-start | bytes 688136 | tf_op jit(solution)/shard_map/ppermute | solution.py:30
  71.9 2.4 %collective-permute-done.12 = bf16[8,14336]{1,0:T(8,128)(2,1)S(1)} collective-permute-done((bf16[8,14336]{1,0:T(8,128)(2,1)S(1)}, bf16[8,14336]{1,0:T(8,128)(2,1)S(1)}, u32[]{:S(2)}, u32[]{:S(2)}) %collective-permute-start.12) | collective-permute-done | bytes 229408 | tf_op jit(solution)/shard_map/ppermute | solution.py:30
  74.3 3.1 %collective-permute-done.13 = bf16[8,14336]{1,0:T(8,128)(2,1)S(1)} collective-permute-done((bf16[8,14336]{1,0:T(8,128)(2,1)S(1)}, bf16[8,14336]{1,0:T(8,128)(2,1)S(1)}, u32[]{:S(2)}, u32[]{:S(2)}) %collective-permute-start.13) | collective-permute-done | bytes 229408 | tf_op jit(solution)/shard_map/ppermute | solution.py:30
  77.5 3.2 %collective-permute-start.20 = (bf16[4,8,14336]{2,1,0:T(8,128)(2,1)S(1)}, bf16[4,8,14336]{2,1,0:T(8,128)(2,1)S(1)}, u32[]{:S(2)}, u32[]{:S(2)}) collective-permute-start(bf16[4,8,14336]{2,1,0:T(8,128)(2,1)S(1)} %bitcast_dynamic-update-slice_fusion.10), channel_id=1, source_target_pairs={{0,65},{1,64},{2,67},{3,66},{4,69},{5,68},{6,71},{7,70},{8,73},{9,... | collective-permute-start | bytes 2752520 | tf_op jit(solution)/shard_map/ppermute | solution.py:30
  80.9 1.7 %collective-permute-start.19 = (bf16[4,8,14336]{2,1,0:T(8,128)(2,1)S(1)}, bf16[4,8,14336]{2,1,0:T(8,128)(2,1)S(1)}, u32[]{:S(2)}, u32[]{:S(2)}) collective-permute-start(bf16[4,8,14336]{2,1,0:T(8,128)(2,1)S(1)} %bitcast_dynamic-update-slice_fusion.6), channel_id=1, source_target_pairs={{0,2},{1,3},{2,4},{3,5},{4,6},{5,7},{6,0},{7,1},{8,10},{9,11},{10,... | collective-permute-start | bytes 2752520 | tf_op jit(solution)/shard_map/ppermute | solution.py:30
  82.5 1.7 %collective-permute-start.21 = (bf16[4,8,14336]{2,1,0:T(8,128)(2,1)S(1)}, bf16[4,8,14336]{2,1,0:T(8,128)(2,1)S(1)}, u32[]{:S(2)}, u32[]{:S(2)}) collective-permute-start(bf16[4,8,14336]{2,1,0:T(8,128)(2,1)S(1)} %bitcast_dynamic-update-slice_fusion.6), channel_id=1, source_target_pairs={{0,6},{1,7},{2,0},{3,1},{4,2},{5,3},{6,4},{7,5},{8,14},{9,15},{10,... | collective-permute-start | bytes 2752520 | tf_op jit(solution)/shard_map/ppermute | solution.py:30
  85.1 12.9 %collective-permute-done.18 = bf16[4,8,14336]{2,1,0:T(8,128)(2,1)S(1)} collective-permute-done((bf16[4,8,14336]{2,1,0:T(8,128)(2,1)S(1)}, bf16[4,8,14336]{2,1,0:T(8,128)(2,1)S(1)}, u32[]{:S(2)}, u32[]{:S(2)}) %collective-permute-start.18) | collective-permute-done | bytes 917536 | tf_op jit(solution)/shard_map/ppermute | solution.py:30
  98.1 3.3 %collective-permute-start.23 = (bf16[2,8,14336]{2,1,0:T(8,128)(2,1)S(1)}, bf16[2,8,14336]{2,1,0:T(8,128)(2,1)S(1)}, u32[]{:S(2)}, u32[]{:S(2)}) collective-permute-start(bf16[2,8,14336]{2,1,0:T(8,128)(2,1)S(1)} %slice.152), channel_id=1, source_target_pairs={{0,65},{1,64},{2,67},{3,66},{4,69},{5,68},{6,71},{7,70},{8,73},{9,... | collective-permute-start | bytes 1376264 | tf_op jit(solution)/shard_map/ppermute | solution.py:30
  101.4 1.7 %collective-permute-start.24 = (bf16[2,8,14336]{2,1,0:T(8,128)(2,1)S(1)}, bf16[2,8,14336]{2,1,0:T(8,128)(2,1)S(1)}, u32[]{:S(2)}, u32[]{:S(2)}) collective-permute-start(bf16[2,8,14336]{2,1,0:T(8,128)(2,1)S(1)} %slice.153), channel_id=1, source_target_pairs={{0,2},{1,3},{2,4},{3,5},{4,6},{5,7},{6,0},{7,1},{8,10},{9,11},{10,... | collective-permute-start | bytes 1376264 | tf_op jit(solution)/shard_map/ppermute | solution.py:30
  103.1 1.7 %collective-permute-start.25 = (bf16[2,8,14336]{2,1,0:T(8,128)(2,1)S(1)}, bf16[2,8,14336]{2,1,0:T(8,128)(2,1)S(1)}, u32[]{:S(2)}, u32[]{:S(2)}) collective-permute-start(bf16[2,8,14336]{2,1,0:T(8,128)(2,1)S(1)} %slice.154), channel_id=1, source_target_pairs={{0,6},{1,7},{2,0},{3,1},{4,2},{5,3},{6,4},{7,5},{8,14},{9,15},{10,... | collective-permute-start | bytes 1376264 | tf_op jit(solution)/shard_map/ppermute | solution.py:30
  105.2 2.5 %collective-permute-done.22 = bf16[2,8,14336]{2,1,0:T(8,128)(2,1)S(1)} collective-permute-done((bf16[2,8,14336]{2,1,0:T(8,128)(2,1)S(1)}, bf16[2,8,14336]{2,1,0:T(8,128)(2,1)S(1)}, u32[]{:S(2)}, u32[]{:S(2)}) %collective-permute-start.22) | collective-permute-done | bytes 458784 | tf_op jit(solution)/shard_map/ppermute | solution.py:30
  107.8 3.4 %collective-permute-done.24 = bf16[2,8,14336]{2,1,0:T(8,128)(2,1)S(1)} collective-permute-done((bf16[2,8,14336]{2,1,0:T(8,128)(2,1)S(1)}, bf16[2,8,14336]{2,1,0:T(8,128)(2,1)S(1)}, u32[]{:S(2)}, u32[]{:S(2)}) %collective-permute-start.24) | collective-permute-done | bytes 458784 | tf_op jit(solution)/shard_map/ppermute | solution.py:30
  111.8 3.0 %copy-done.3 = bf16[4,4,8,28672]{3,2,1,0:T(8,128)(2,1)} copy-done((bf16[4,4,8,28672]{3,2,1,0:T(8,128)(2,1)}, bf16[4,4,8,28672]{3,2,1,0:T(8,128)(2,1)S(1)}, u32[]{:S(2)}) %copy-start.3) | copy-done | bytes 7340056
  (59 shorter events, 11.0 us)
Async XLA Ops:
  0.7 11.0 %copy-start.1 = (f32[1,16,28672]{2,1,0:T(8,128)S(1)}, f32[1,16,28672]{2,1,0:T(8,128)}, u32[]{:S(2)}) copy-start(f32[1,16,28672]{2,1,0:T(8,128)} %first_moment.1) | copy-start | bytes 5505028
  5.3 6.3 %collective-permute-start = (f32[16,28672]{1,0:T(8,128)}, f32[16,28672]{1,0:T(8,128)}, u32[]{:S(2)}, u32[]{:S(2)}) collective-permute-start(f32[16,28672]{1,0:T(8,128)} %shard_map.55), channel_id=1, source_target_pairs={{0,8},{1,9},{2,10},{3,11},{4,12},{5,13},{6,14},{7,15},{8,0},{9,1},... | collective-permute-start | bytes 5505032 | tf_op jit(solution)/shard_map/ppermute | solution.py:30
  5.3 5.8 %collective-permute-start.1 = (f32[1]{0:T(128)}, f32[1]{0:T(128)}, u32[]{:S(2)}, u32[]{:S(2)}) collective-permute-start(f32[1]{0:T(128)} %param.9), channel_id=1, source_target_pairs={{0,8},{8,16},{16,24},{24,32},{32,40},{40,48},{48,56},{56,64},{64,7... | collective-permute-start | bytes 20 | tf_op jit(solution)/shard_map/ppermute | solution.py:128
  11.6 6.3 %copy-start = (bf16[4,1,16,28672]{3,2,1,0:T(8,128)(2,1)S(1)}, bf16[4,1,16,28672]{3,2,1,0:T(8,128)(2,1)}, u32[]{:S(2)}) copy-start(bf16[4,1,16,28672]{3,2,1,0:T(8,128)(2,1)} %grads.1) | copy-start | bytes 11010052
  11.6 6.3 %copy-start.2 = (f32[1,16,28672]{2,1,0:T(8,128)S(1)}, f32[1,16,28672]{2,1,0:T(8,128)}, u32[]{:S(2)}) copy-start(f32[1,16,28672]{2,1,0:T(8,128)} %second_moment.1) | copy-start | bytes 5505028
  16.2 15.3 %collective-permute-start.2 = (bf16[16,14336]{1,0:T(8,128)(2,1)S(1)}, bf16[16,14336]{1,0:T(8,128)(2,1)S(1)}, u32[]{:S(2)}, u32[]{:S(2)}) collective-permute-start(bf16[16,14336]{1,0:T(8,128)(2,1)S(1)} %get-tuple-element.39), channel_id=1, source_target_pairs={{0,16},{1,17},{2,18},{3,19},{4,20},{5,21},{6,22},{7,23},{8,24},{9,... | collective-permute-start | bytes 1376264 | tf_op jit(solution)/shard_map/ppermute | solution.py:30
  16.3 15.3 %collective-permute-start.4 = (bf16[16,14336]{1,0:T(8,128)(2,1)S(1)}, bf16[16,14336]{1,0:T(8,128)(2,1)S(1)}, u32[]{:S(2)}, u32[]{:S(2)}) collective-permute-start(bf16[16,14336]{1,0:T(8,128)(2,1)S(1)} %get-tuple-element.46), channel_id=1, source_target_pairs={{0,48},{1,49},{2,50},{3,51},{4,52},{5,53},{6,54},{7,55},{8,56},{9,... | collective-permute-start | bytes 1376264 | tf_op jit(solution)/shard_map/ppermute | solution.py:30
  22.5 8.4 %collective-permute-start.3 = (f32[1]{0:T(128)}, f32[1]{0:T(128)}, u32[]{:S(2)}, u32[]{:S(2)}) collective-permute-start(f32[1]{0:T(128)} %add.254), channel_id=1, source_target_pairs={{0,16},{8,24},{16,32},{24,40},{32,48},{40,56},{48,64},{56,72},{64,... | collective-permute-start | bytes 20 | tf_op jit(solution)/shard_map/ppermute | solution.py:128
  32.7 8.8 %collective-permute-start.5 = (bf16[8,14336]{1,0:T(8,128)(2,1)S(1)}, bf16[8,14336]{1,0:T(8,128)(2,1)S(1)}, u32[]{:S(2)}, u32[]{:S(2)}) collective-permute-start(bf16[8,14336]{1,0:T(8,128)(2,1)S(1)} %get-tuple-element.48), channel_id=1, source_target_pairs={{0,64},{1,65},{2,66},{3,67},{4,68},{5,69},{6,70},{7,71},{8,72},{9,... | collective-permute-start | bytes 688136 | tf_op jit(solution)/shard_map/ppermute | solution.py:30
  32.9 13.4 %collective-permute-start.6 = (bf16[8,14336]{1,0:T(8,128)(2,1)S(1)}, bf16[8,14336]{1,0:T(8,128)(2,1)S(1)}, u32[]{:S(2)}, u32[]{:S(2)}) collective-permute-start(bf16[8,14336]{1,0:T(8,128)(2,1)S(1)} %get-tuple-element.49), channel_id=1, source_target_pairs={{0,64},{1,65},{2,66},{3,67},{4,68},{5,69},{6,70},{7,71},{8,72},{9,... | collective-permute-start | bytes 688136 | tf_op jit(solution)/shard_map/ppermute | solution.py:30
  34.8 6.1 %collective-permute-start.7 = (f32[1]{0:T(128)}, f32[1]{0:T(128)}, u32[]{:S(2)}, u32[]{:S(2)}) collective-permute-start(f32[1]{0:T(128)} %add.255), channel_id=1, source_target_pairs={{0,32},{8,40},{16,48},{24,56},{32,64},{40,72},{48,80},{56,88},{64,... | collective-permute-start | bytes 20 | tf_op jit(solution)/shard_map/ppermute | solution.py:128
  36.3 19.7 %collective-permute-start.10 = (bf16[8,28672]{1,0:T(8,128)(2,1)}, bf16[8,28672]{1,0:T(8,128)(2,1)}, u32[]{:S(2)}, u32[]{:S(2)}) collective-permute-start(bf16[8,28672]{1,0:T(8,128)(2,1)} %get-tuple-element.57), channel_id=1, source_target_pairs={{0,64},{1,65},{2,66},{3,67},{4,68},{5,69},{6,70},{7,71},{8,72},{9,... | collective-permute-start | bytes 1376264 | tf_op jit(solution)/shard_map/ppermute | solution.py:30
  48.2 7.8 %collective-permute-start.8 = (bf16[8,14336]{1,0:T(8,128)(2,1)}, bf16[8,14336]{1,0:T(8,128)(2,1)S(1)}, u32[]{:S(2)}, u32[]{:S(2)}) collective-permute-start(bf16[8,14336]{1,0:T(8,128)(2,1)} %fusion.99), channel_id=1, source_target_pairs={{0,32},{1,33},{2,34},{3,35},{4,36},{5,37},{6,38},{7,39},{8,40},{9,... | collective-permute-start | bytes 688136 | tf_op jit(solution)/shard_map/ppermute | solution.py:30
  48.5 11.5 %collective-permute-start.14 = (bf16[8,14336]{1,0:T(8,128)(2,1)}, bf16[8,14336]{1,0:T(8,128)(2,1)}, u32[]{:S(2)}, u32[]{:S(2)}) collective-permute-start(bf16[8,14336]{1,0:T(8,128)(2,1)} %fusion.102), channel_id=1, source_target_pairs={{0,32},{1,33},{2,34},{3,35},{4,36},{5,37},{6,38},{7,39},{8,40},{9,... | collective-permute-start | bytes 688136 | tf_op jit(solution)/shard_map/ppermute | solution.py:30
  51.8 3.6 %collective-permute-start.9 = (f32[1]{0:T(128)}, f32[1]{0:T(128)}, u32[]{:S(2)}, u32[]{:S(2)}) collective-permute-start(f32[1]{0:T(128)} %add.259), channel_id=1, source_target_pairs={{0,64},{8,72},{16,80},{24,88},{32,96},{40,104},{48,112},{56,120},{... | collective-permute-start | bytes 20 | tf_op jit(solution)/shard_map/ppermute | solution.py:128
  58.4 11.6 %collective-permute-start.11 = (bf16[8,14336]{1,0:T(8,128)(2,1)S(1)}, bf16[8,14336]{1,0:T(8,128)(2,1)S(1)}, u32[]{:S(2)}, u32[]{:S(2)}) collective-permute-start(bf16[8,14336]{1,0:T(8,128)(2,1)S(1)} %get-tuple-element.62), channel_id=1, source_target_pairs={{0,2},{1,3},{2,4},{3,5},{4,6},{5,7},{6,0},{7,1},{8,10},{9,11},{10,... | collective-permute-start | bytes 688136 | tf_op jit(solution)/shard_map/ppermute | solution.py:30
  62.4 18.4 %collective-permute-start.15 = (bf16[8,14336]{1,0:T(8,128)(2,1)S(1)}, bf16[8,14336]{1,0:T(8,128)(2,1)S(1)}, u32[]{:S(2)}, u32[]{:S(2)}) collective-permute-start(bf16[8,14336]{1,0:T(8,128)(2,1)S(1)} %get-tuple-element.60), channel_id=1, source_target_pairs={{0,64},{1,65},{2,66},{3,67},{4,68},{5,69},{6,70},{7,71},{8,72},{9,... | collective-permute-start | bytes 688136 | tf_op jit(solution)/shard_map/ppermute | solution.py:30
  62.8 18.0 %collective-permute-start.16 = (bf16[8,14336]{1,0:T(8,128)(2,1)S(1)}, bf16[8,14336]{1,0:T(8,128)(2,1)S(1)}, u32[]{:S(2)}, u32[]{:S(2)}) collective-permute-start(bf16[8,14336]{1,0:T(8,128)(2,1)S(1)} %get-tuple-element.60), channel_id=1, source_target_pairs={{0,65},{1,64},{2,67},{3,66},{4,69},{5,68},{6,71},{7,70},{8,73},{9,... | collective-permute-start | bytes 688136 | tf_op jit(solution)/shard_map/ppermute | solution.py:30
  65.9 15.0 %collective-permute-start.17 = (bf16[8,14336]{1,0:T(8,128)(2,1)S(1)}, bf16[8,14336]{1,0:T(8,128)(2,1)S(1)}, u32[]{:S(2)}, u32[]{:S(2)}) collective-permute-start(bf16[8,14336]{1,0:T(8,128)(2,1)S(1)} %get-tuple-element.60), channel_id=1, source_target_pairs={{0,1},{1,0},{2,3},{3,2},{4,5},{5,4},{6,7},{7,6},{8,9},{9,8},{10,11... | collective-permute-start | bytes 688136 | tf_op jit(solution)/shard_map/ppermute | solution.py:30
  68.3 6.0 %collective-permute-start.12 = (bf16[8,14336]{1,0:T(8,128)(2,1)S(1)}, bf16[8,14336]{1,0:T(8,128)(2,1)S(1)}, u32[]{:S(2)}, u32[]{:S(2)}) collective-permute-start(bf16[8,14336]{1,0:T(8,128)(2,1)S(1)} %get-tuple-element.62), channel_id=1, source_target_pairs={{0,6},{1,7},{2,0},{3,1},{4,2},{5,3},{6,4},{7,5},{8,14},{9,15},{10,... | collective-permute-start | bytes 688136 | tf_op jit(solution)/shard_map/ppermute | solution.py:30
  69.9 7.5 %collective-permute-start.13 = (bf16[8,14336]{1,0:T(8,128)(2,1)S(1)}, bf16[8,14336]{1,0:T(8,128)(2,1)S(1)}, u32[]{:S(2)}, u32[]{:S(2)}) collective-permute-start(bf16[8,14336]{1,0:T(8,128)(2,1)S(1)} %get-tuple-element.62), channel_id=1, source_target_pairs={{0,4},{1,5},{2,6},{3,7},{4,0},{5,1},{6,2},{7,3},{8,12},{9,13},{10,... | collective-permute-start | bytes 688136 | tf_op jit(solution)/shard_map/ppermute | solution.py:30
  77.5 20.5 %collective-permute-start.18 = (bf16[4,8,14336]{2,1,0:T(8,128)(2,1)S(1)}, bf16[4,8,14336]{2,1,0:T(8,128)(2,1)S(1)}, u32[]{:S(2)}, u32[]{:S(2)}) collective-permute-start(bf16[4,8,14336]{2,1,0:T(8,128)(2,1)S(1)} %bitcast_dynamic-update-slice_fusion.10), channel_id=1, source_target_pairs={{0,64},{1,65},{2,66},{3,67},{4,68},{5,69},{6,70},{7,71},{8,72},{9,... | collective-permute-start | bytes 2752520 | tf_op jit(solution)/shard_map/ppermute | solution.py:30
  77.5 20.5 %collective-permute-start.20 = (bf16[4,8,14336]{2,1,0:T(8,128)(2,1)S(1)}, bf16[4,8,14336]{2,1,0:T(8,128)(2,1)S(1)}, u32[]{:S(2)}, u32[]{:S(2)}) collective-permute-start(bf16[4,8,14336]{2,1,0:T(8,128)(2,1)S(1)} %bitcast_dynamic-update-slice_fusion.10), channel_id=1, source_target_pairs={{0,65},{1,64},{2,67},{3,66},{4,69},{5,68},{6,71},{7,70},{8,73},{9,... | collective-permute-start | bytes 2752520 | tf_op jit(solution)/shard_map/ppermute | solution.py:30
  80.9 20.5 %collective-permute-start.19 = (bf16[4,8,14336]{2,1,0:T(8,128)(2,1)S(1)}, bf16[4,8,14336]{2,1,0:T(8,128)(2,1)S(1)}, u32[]{:S(2)}, u32[]{:S(2)}) collective-permute-start(bf16[4,8,14336]{2,1,0:T(8,128)(2,1)S(1)} %bitcast_dynamic-update-slice_fusion.6), channel_id=1, source_target_pairs={{0,2},{1,3},{2,4},{3,5},{4,6},{5,7},{6,0},{7,1},{8,10},{9,11},{10,... | collective-permute-start | bytes 2752520 | tf_op jit(solution)/shard_map/ppermute | solution.py:30
  82.5 20.6 %collective-permute-start.21 = (bf16[4,8,14336]{2,1,0:T(8,128)(2,1)S(1)}, bf16[4,8,14336]{2,1,0:T(8,128)(2,1)S(1)}, u32[]{:S(2)}, u32[]{:S(2)}) collective-permute-start(bf16[4,8,14336]{2,1,0:T(8,128)(2,1)S(1)} %bitcast_dynamic-update-slice_fusion.6), channel_id=1, source_target_pairs={{0,6},{1,7},{2,0},{3,1},{4,2},{5,3},{6,4},{7,5},{8,14},{9,15},{10,... | collective-permute-start | bytes 2752520 | tf_op jit(solution)/shard_map/ppermute | solution.py:30
  98.0 9.8 %collective-permute-start.22 = (bf16[2,8,14336]{2,1,0:T(8,128)(2,1)S(1)}, bf16[2,8,14336]{2,1,0:T(8,128)(2,1)S(1)}, u32[]{:S(2)}, u32[]{:S(2)}) collective-permute-start(bf16[2,8,14336]{2,1,0:T(8,128)(2,1)S(1)} %slice.151), channel_id=1, source_target_pairs={{0,64},{1,65},{2,66},{3,67},{4,68},{5,69},{6,70},{7,71},{8,72},{9,... | collective-permute-start | bytes 1376264 | tf_op jit(solution)/shard_map/ppermute | solution.py:30
  98.1 9.6 %collective-permute-start.23 = (bf16[2,8,14336]{2,1,0:T(8,128)(2,1)S(1)}, bf16[2,8,14336]{2,1,0:T(8,128)(2,1)S(1)}, u32[]{:S(2)}, u32[]{:S(2)}) collective-permute-start(bf16[2,8,14336]{2,1,0:T(8,128)(2,1)S(1)} %slice.152), channel_id=1, source_target_pairs={{0,65},{1,64},{2,67},{3,66},{4,69},{5,68},{6,71},{7,70},{8,73},{9,... | collective-permute-start | bytes 1376264 | tf_op jit(solution)/shard_map/ppermute | solution.py:30
  101.4 9.8 %collective-permute-start.24 = (bf16[2,8,14336]{2,1,0:T(8,128)(2,1)S(1)}, bf16[2,8,14336]{2,1,0:T(8,128)(2,1)S(1)}, u32[]{:S(2)}, u32[]{:S(2)}) collective-permute-start(bf16[2,8,14336]{2,1,0:T(8,128)(2,1)S(1)} %slice.153), channel_id=1, source_target_pairs={{0,2},{1,3},{2,4},{3,5},{4,6},{5,7},{6,0},{7,1},{8,10},{9,11},{10,... | collective-permute-start | bytes 1376264 | tf_op jit(solution)/shard_map/ppermute | solution.py:30
  103.1 8.5 %collective-permute-start.25 = (bf16[2,8,14336]{2,1,0:T(8,128)(2,1)S(1)}, bf16[2,8,14336]{2,1,0:T(8,128)(2,1)S(1)}, u32[]{:S(2)}, u32[]{:S(2)}) collective-permute-start(bf16[2,8,14336]{2,1,0:T(8,128)(2,1)S(1)} %slice.154), channel_id=1, source_target_pairs={{0,6},{1,7},{2,0},{3,1},{4,2},{5,3},{6,4},{7,5},{8,14},{9,15},{10,... | collective-permute-start | bytes 1376264 | tf_op jit(solution)/shard_map/ppermute | solution.py:30
  111.8 3.1 %copy-start.3 = (bf16[4,4,8,28672]{3,2,1,0:T(8,128)(2,1)}, bf16[4,4,8,28672]{3,2,1,0:T(8,128)(2,1)S(1)}, u32[]{:S(2)}) copy-start(bf16[4,4,8,28672]{3,2,1,0:T(8,128)(2,1)S(1)} %fusion.66) | copy-start | bytes 22020100

commit v3 on v2

--- a/solution.py
+++ b/solution.py
@@ -140,37 +140,35 @@
     a_there = moved(a, cores)
     weight_one = mixed(push_weight, 1)
 
+    a, later = lax.optimization_barrier((a, state))
+    c = (-learn_rate * KEEP / 4.0) * update(*moments(*later, 3), 2)
+    d = (-learn_rate / 2.0) * update(*moments(*later, 4), 3)
+    d, d_code = mine(d), coded(other(d), 1.0)
+    d_there = moved(d_code, across)
     factor = -learn_rate * KEEP**2 / 8.0 * weight_one[0]
-    parts, codes = [], []
-    for part in sides:
-        local = lax.optimization_barrier((state, a, a_there, factor))
-        b = local[3] * update(*moments(local[0][0][:, part], local[0][1][:, part], local[0][2][:, :, part], 2), 1)
-        ab = local[1][:, part] + local[2][:, part] + b
-        parts.append(ab)
-        codes.append(coded(ab, 4.0))
-    codes, parts, state = lax.optimization_barrier((codes, parts, state))
-    c = (-learn_rate * KEEP / 4.0) * update(*moments(*state, 3), 2)
-    d = (-learn_rate / 2.0) * update(*moments(*state, 4), 3)
-    c, d, d_code, weight_one = lax.optimization_barrier((c, mine(d), coded(other(d), 1.0), weight_one))
+    c, d_code, factor, state = lax.optimization_barrier((c, d_code, factor, state))
+    b = factor * update(*moments(*state, 2), 1)
+    ab = a + a_there + b
+    codes = [coded(ab[:, part], 4.0) for part in sides]
+    d_there, weight_one = lax.optimization_barrier((d_there, weight_one))
     weight_two = mixed(weight_one, 2)
     near_there = [moved(codes[side], near[side]) for side in range(2)]
-    parts = [parts[side] + decoded(near_there[side], 4.0) + weight_two[0] * c[:, sides[side]] for side in range(2)]
+    parts = [ab[:, part] + decoded(near_there[side], 4.0) + weight_two[0] * c[:, part] for side, part in enumerate(sides)]
     codes = [coded(other(part), 4.0) for part in parts]
-    codes, d_code, weight_two = lax.optimization_barrier((codes, d_code, weight_two))
-    d_there = moved(d_code, across)
+    codes, weight_two = lax.optimization_barrier((codes, weight_two))
     weight_three = mixed(weight_two, 4)
     there = [moved(code, across) for code in codes]
-    there, weight_three = lax.optimization_barrier((there, weight_three))
     parts = [mine(parts[side]) + decoded(there[side], 4.0) for side in range(2)]
     codes = [coded(part, 8.0) for part in parts]
-    codes, weight_three = lax.optimization_barrier((codes, weight_three))
+    codes[1], weight_three = lax.optimization_barrier((codes[1], weight_three))
     weight_three_there = ring(weight_three, 8)
     weight_four = 0.5 * weight_three[0] + 0.5 * weight_three_there[0]
+    own = weight_three[0] * d + weight_three_there[0] * decoded(d_there, 1.0)
 
     pieces = []
     for side, part in enumerate(sides):
-        own = weight_three[0] * d[:, part] + weight_three_there[0] * decoded(d_there[:, part], 1.0)
-        total = parts[side] + decoded(moved(codes[side], far), 8.0) + own
+        before = lax.optimization_barrier(parts[side] + own[:, part])
+        total = before + decoded(moved(codes[side], far), 8.0)
         pieces.append((total / weight_four).astype(jnp.bfloat16))
     return gathered(*pieces, y, z).reshape(1, 128, cols)
 

time: 115 us -> 112 us (0.974); the launches traced: 115 us -> 110 us
  waiting for transfers between devices: 44.3 us -> 35.8 us
  starting transfers between devices: 40.9 us -> 45.2 us
    ppermute x4, waiting for transfers between devices: 14.7 us -> 8.27 us  [per_device(): lax.ppermute(v, 'replica', [(r, (r + steps) % REPLICAS) for r in range(RE...]
    convert_element_type x5, other arithmetic: 7.88 us -> 3.3 us  [coded(): return (value * second * fourth * (fourth * fourth)).astype(jnp.bfloat16)]
    add x1 -> x3, other arithmetic: 0.85 us -> 5.34 us  [the longest x1 3.46 us: per_device(): ab = a + a_there + b]
    dynamic_update_slice x2, other arithmetic: 4.52 us -> 1.38 us  [line(): block = lax.dynamic_update_slice(block, v[None], (at, 0, 0))]
    ppermute x4, starting transfers between devices: 7.17 us -> 9.36 us  [per_device(): lax.ppermute(v, 'replica', [(r, (r + steps) % REPLICAS) for r in range(RE...]
    mul x1, other arithmetic: 3.48 us -> 5.65 us  [per_device(): d = -learn_rate / 2.0 * update(*moments(*later, 4), 3)]
    ppermute x22, starting transfers between devices: 33.8 us -> 35.9 us  [moved(): return lax.ppermute(value, AXES, pairs)]
    ppermute x22, waiting for transfers between devices: 29.5 us -> 27.6 us  [moved(): return lax.ppermute(value, AXES, pairs)]
  transfers between devices with their start and end apart: 26 -> 26, of which waited for: 11 -> 12; matrix products, arithmetic and copies ran while one was open for 11% -> 14% of each run, Pallas kernels for 0% -> 4%
where the time goes in v3:
time: 112 us; the launch traced here: 110 us
  starting transfers between devices  45.2 us (40%)
  waiting for transfers between devices  35.8 us (32%)
  other arithmetic  15.8 us (14%)
  local copies, waits for them, and re-layouts  5.54 us (5%)
  Pallas kernels  4.47 us (4%)
  between operations  3.49 us (3%)
    ppermute x22, starting transfers between devices, moved(): return lax.ppermute(value, AXES, pairs)  35.9 us
    ppermute x22, waiting for transfers between devices, moved(): return lax.ppermute(value, AXES, pairs)  27.6 us
    ppermute x4, starting transfers between devices, per_device(): lax.ppermute(v, 'replica', [(r, (r + steps) % REPLICAS) for r in range(RE...  9.36 us
    ppermute x4, waiting for transfers between devices, per_device(): lax.ppermute(v, 'replica', [(r, (r + steps) % REPLICAS) for r in range(RE...  8.27 us
    mul x1, other arithmetic, per_device(): d = -learn_rate / 2.0 * update(*moments(*later, 4), 3)  5.65 us
    pallas_call x1, Pallas kernels, first_term(): pl.pallas_call(first_kernel, grid=(cols // BLOCK,), in_specs=[SMEM, spec,...  4.47 us
    unnamed x14, local copies, waits for them, and re-layouts  3.98 us
    add x1, other arithmetic, per_device(): ab = a + a_there + b  3.46 us
  transfers between devices with their start and end apart: 26, of which 12 were waited for; matrix products, arithmetic and copies ran while one was open for 14% of the time, Pallas kernels for 4%

profile of v3, /device:TPU:0, one launch (start us, length us, event | category | flops | bytes accessed | tf_op | source)
XLA Modules:
  0.0 110.4 jit_solution(16668628018658128274)
XLA Ops:
  0.7 4.5 %shard_map.55 = f32[16,28672]{1,0:T(8,128)} custom-call(f32[1]{0:T(128)S(6)} %copy.26.weight, f32[1,16,28672]{2,1,0:T(8,128)} %params.1, f32[1,16,28672]{2,1,0:T(8,128)} %first_moment.1, f32[1,16,28672]{2,1,0:T(8,128)} %second_moment.1, bf16[4,1,16,28672]{3,2,1,0:T(8,128)(2,1)} %grads.1), custom_call_target="tpu_custom_call" | custom-call | flops 9175040 | bytes 8257536 | tf_op jit(solution)/shard_map/pallas_call | solution.py:81
  5.1 1.7 %collective-permute-start = (f32[16,28672]{1,0:T(8,128)}, f32[16,28672]{1,0:T(8,128)}, u32[]{:S(2)}, u32[]{:S(2)}) collective-permute-start(f32[16,28672]{1,0:T(8,128)} %shard_map.55), channel_id=1, source_target_pairs={{0,8},{1,9},{2,10},{3,11},{4,12},{5,13},{6,14},{7,15},{8,0},{9,1},... | collective-permute-start | bytes 5505032 | tf_op jit(solution)/shard_map/ppermute | solution.py:30
  6.9 5.6 %fusion.13 = (f32[16,28672]{1,0:T(8,128)S(1)}, f32[16,28672]{1,0:T(8,128)S(1)}) fusion(bf16[4,16,28672]{2,1,0:T(8,128)(2,1)} %bitcast.97, f32[16,28672]{1,0:T(8,128)} %bitcast.101, f32[16,28672]{1,0:T(8,128)} %bitcast.99), kind=kLoop, calls=%fused_computation.31 | loop fusion | flops 19267584 | bytes 11010048 | tf_op jit(solution)/shard_map/mul | solution.py:145
  12.8 2.0 %collective-permute-start.3 = (bf16[8,28672]{1,0:T(8,128)(2,1)S(1)}, bf16[8,28672]{1,0:T(8,128)(2,1)S(1)}, u32[]{:S(2)}, u32[]{:S(2)}) collective-permute-start(bf16[8,28672]{1,0:T(8,128)(2,1)S(1)} %fusion.45), channel_id=1, source_target_pairs={{0,64},{1,65},{2,66},{3,67},{4,68},{5,69},{6,70},{7,71},{8,72},{9,... | collective-permute-start | bytes 1376264 | tf_op jit(solution)/shard_map/ppermute | solution.py:30
  15.5 3.5 %fusion.24 = f32[16,28672]{1,0:T(8,128)S(1)} fusion(f32[16,28672]{1,0:T(8,128)S(1)} %bitcast.100, f32[16,28672]{1,0:T(8,128)S(1)} %bitcast.102, f32[16,28672]{1,0:T(8,128)S(1)} %copy-done.6, f32[16,28672]{1,0:T(8,128)} %collective-permute-done, bf16[4,16,28672]{2,1,0:T(8,128)(2,1)S(1)} %bitcast.98, f32[]{:T(128)} %bitcast.11), kind=kLoop, calls=%fused_computation.42 | loop fusion | flops 10551296 | bytes 11010052 | tf_op jit(solution)/shard_map/add | solution.py:151
  19.4 1.6 %collective-permute-start.2 = (bf16[16,14336]{1,0:T(8,128)(2,1)S(1)}, bf16[16,14336]{1,0:T(8,128)(2,1)S(1)}, u32[]{:S(2)}, u32[]{:S(2)}) collective-permute-start(bf16[16,14336]{1,0:T(8,128)(2,1)S(1)} %get-tuple-element.46), channel_id=1, source_target_pairs={{0,16},{1,17},{2,18},{3,19},{4,20},{5,21},{6,22},{7,23},{8,24},{9,... | collective-permute-start | bytes 1376264 | tf_op jit(solution)/shard_map/ppermute | solution.py:30
  21.0 1.8 %collective-permute-start.5 = (bf16[16,14336]{1,0:T(8,128)(2,1)S(1)}, bf16[16,14336]{1,0:T(8,128)(2,1)S(1)}, u32[]{:S(2)}, u32[]{:S(2)}) collective-permute-start(bf16[16,14336]{1,0:T(8,128)(2,1)S(1)} %get-tuple-element.45), channel_id=1, source_target_pairs={{0,48},{1,49},{2,50},{3,51},{4,52},{5,53},{6,54},{7,55},{8,56},{9,... | collective-permute-start | bytes 1376264 | tf_op jit(solution)/shard_map/ppermute | solution.py:30
  22.8 2.7 %collective-permute-done.3 = bf16[8,28672]{1,0:T(8,128)(2,1)S(1)} collective-permute-done((bf16[8,28672]{1,0:T(8,128)(2,1)S(1)}, bf16[8,28672]{1,0:T(8,128)(2,1)S(1)}, u32[]{:S(2)}, u32[]{:S(2)}) %collective-permute-start.3) | collective-permute-done | bytes 458784 | tf_op jit(solution)/shard_map/ppermute | solution.py:30
  25.5 5.2 %collective-permute-start.4 = (f32[1]{0:T(128)}, f32[1]{0:T(128)}, u32[]{:S(2)}, u32[]{:S(2)}) collective-permute-start(f32[1]{0:T(128)} %add.223), channel_id=1, source_target_pairs={{0,16},{8,24},{16,32},{24,40},{32,48},{40,56},{48,64},{56,72},{64,... | collective-permute-start | bytes 20 | tf_op jit(solution)/shard_map/ppermute | solution.py:128
  30.7 3.6 %collective-permute-done.4 = f32[1]{0:T(128)} collective-permute-done((f32[1]{0:T(128)}, f32[1]{0:T(128)}, u32[]{:S(2)}, u32[]{:S(2)}) %collective-permute-start.4) | collective-permute-done | bytes 36 | tf_op jit(solution)/shard_map/ppermute | solution.py:128
  37.8 1.3 %collective-permute-start.7 = (bf16[8,14336]{1,0:T(8,128)(2,1)}, bf16[8,14336]{1,0:T(8,128)(2,1)S(1)}, u32[]{:S(2)}, u32[]{:S(2)}) collective-permute-start(bf16[8,14336]{1,0:T(8,128)(2,1)} %get-tuple-element.32), channel_id=1, source_target_pairs={{0,64},{1,65},{2,66},{3,67},{4,68},{5,69},{6,70},{7,71},{8,72},{9,... | collective-permute-start | bytes 688136 | tf_op jit(solution)/shard_map/ppermute | solution.py:30
  39.1 1.9 %collective-permute-start.8 = (f32[1]{0:T(128)}, f32[1]{0:T(128)}, u32[]{:S(2)}, u32[]{:S(2)}) collective-permute-start(f32[1]{0:T(128)} %add.224), channel_id=1, source_target_pairs={{0,32},{8,40},{16,48},{24,56},{32,64},{40,72},{48,80},{56,88},{64,... | collective-permute-start | bytes 20 | tf_op jit(solution)/shard_map/ppermute | solution.py:128
  41.7 3.3 %collective-permute-done.8 = f32[1]{0:T(128)} collective-permute-done((f32[1]{0:T(128)}, f32[1]{0:T(128)}, u32[]{:S(2)}, u32[]{:S(2)}) %collective-permute-start.8) | collective-permute-done | bytes 36 | tf_op jit(solution)/shard_map/ppermute | solution.py:128
  47.4 2.3 %collective-permute-start.9 = (f32[1]{0:T(128)}, f32[1]{0:T(128)}, u32[]{:S(2)}, u32[]{:S(2)}) collective-permute-start(f32[1]{0:T(128)} %add.230), channel_id=1, source_target_pairs={{0,64},{8,72},{16,80},{24,88},{32,96},{40,104},{48,112},{56,120},{... | collective-permute-start | bytes 20 | tf_op jit(solution)/shard_map/ppermute | solution.py:128
  49.7 1.4 %collective-permute-done.9 = f32[1]{0:T(128)} collective-permute-done((f32[1]{0:T(128)}, f32[1]{0:T(128)}, u32[]{:S(2)}, u32[]{:S(2)}) %collective-permute-start.9) | collective-permute-done | bytes 36 | tf_op jit(solution)/shard_map/ppermute | solution.py:128
  53.2 2.4 %collective-permute-start.10 = (bf16[8,14336]{1,0:T(8,128)(2,1)S(1)}, bf16[8,14336]{1,0:T(8,128)(2,1)S(1)}, u32[]{:S(2)}, u32[]{:S(2)}) collective-permute-start(bf16[8,14336]{1,0:T(8,128)(2,1)S(1)} %get-tuple-element.47), channel_id=1, source_target_pairs={{0,32},{1,33},{2,34},{3,35},{4,36},{5,37},{6,38},{7,39},{8,40},{9,... | collective-permute-start | bytes 688136 | tf_op jit(solution)/shard_map/ppermute | solution.py:30
  55.7 2.3 %collective-permute-done.14 = bf16[8,14336]{1,0:T(8,128)(2,1)} collective-permute-done((bf16[8,14336]{1,0:T(8,128)(2,1)}, bf16[8,14336]{1,0:T(8,128)(2,1)}, u32[]{:S(2)}, u32[]{:S(2)}) %collective-permute-start.14) | collective-permute-done | bytes 229408 | tf_op jit(solution)/shard_map/ppermute | solution.py:30
  60.2 2.3 %collective-permute-start.16 = (bf16[8,14336]{1,0:T(8,128)(2,1)S(1)}, bf16[8,14336]{1,0:T(8,128)(2,1)S(1)}, u32[]{:S(2)}, u32[]{:S(2)}) collective-permute-start(bf16[8,14336]{1,0:T(8,128)(2,1)S(1)} %get-tuple-element.38), channel_id=1, source_target_pairs={{0,65},{1,64},{2,67},{3,66},{4,69},{5,68},{6,71},{7,70},{8,73},{9,... | collective-permute-start | bytes 688136 | tf_op jit(solution)/shard_map/ppermute | solution.py:30
  62.4 2.4 %collective-permute-start.17 = (bf16[8,14336]{1,0:T(8,128)(2,1)S(1)}, bf16[8,14336]{1,0:T(8,128)(2,1)S(1)}, u32[]{:S(2)}, u32[]{:S(2)}) collective-permute-start(bf16[8,14336]{1,0:T(8,128)(2,1)S(1)} %get-tuple-element.38), channel_id=1, source_target_pairs={{0,1},{1,0},{2,3},{3,2},{4,5},{5,4},{6,7},{7,6},{8,9},{9,8},{10,11... | collective-permute-start | bytes 688136 | tf_op jit(solution)/shard_map/ppermute | solution.py:30
  65.1 1.6 %collective-permute-start.11 = (bf16[8,14336]{1,0:T(8,128)(2,1)S(1)}, bf16[8,14336]{1,0:T(8,128)(2,1)S(1)}, u32[]{:S(2)}, u32[]{:S(2)}) collective-permute-start(bf16[8,14336]{1,0:T(8,128)(2,1)S(1)} %get-tuple-element.40), channel_id=1, source_target_pairs={{0,2},{1,3},{2,4},{3,5},{4,6},{5,7},{6,0},{7,1},{8,10},{9,11},{10,... | collective-permute-start | bytes 688136 | tf_op jit(solution)/shard_map/ppermute | solution.py:30
  66.8 1.7 %collective-permute-start.12 = (bf16[8,14336]{1,0:T(8,128)(2,1)S(1)}, bf16[8,14336]{1,0:T(8,128)(2,1)S(1)}, u32[]{:S(2)}, u32[]{:S(2)}) collective-permute-start(bf16[8,14336]{1,0:T(8,128)(2,1)S(1)} %get-tuple-element.40), channel_id=1, source_target_pairs={{0,6},{1,7},{2,0},{3,1},{4,2},{5,3},{6,4},{7,5},{8,14},{9,15},{10,... | collective-permute-start | bytes 688136 | tf_op jit(solution)/shard_map/ppermute | solution.py:30
  68.4 2.0 %collective-permute-start.13 = (bf16[8,14336]{1,0:T(8,128)(2,1)S(1)}, bf16[8,14336]{1,0:T(8,128)(2,1)S(1)}, u32[]{:S(2)}, u32[]{:S(2)}) collective-permute-start(bf16[8,14336]{1,0:T(8,128)(2,1)S(1)} %get-tuple-element.40), channel_id=1, source_target_pairs={{0,4},{1,5},{2,6},{3,7},{4,0},{5,1},{6,2},{7,3},{8,12},{9,13},{10,... | collective-permute-start | bytes 688136 | tf_op jit(solution)/shard_map/ppermute | solution.py:30
  70.5 1.4 %collective-permute-start.19 = (bf16[4,8,14336]{2,1,0:T(8,128)(2,1)S(1)}, bf16[4,8,14336]{2,1,0:T(8,128)(2,1)S(1)}, u32[]{:S(2)}, u32[]{:S(2)}) collective-permute-start(bf16[4,8,14336]{2,1,0:T(8,128)(2,1)S(1)} %bitcast_dynamic-update-slice_fusion.6), channel_id=1, source_target_pairs={{0,2},{1,3},{2,4},{3,5},{4,6},{5,7},{6,0},{7,1},{8,10},{9,11},{10,... | collective-permute-start | bytes 2752520 | tf_op jit(solution)/shard_map/ppermute | solution.py:30
  71.9 1.9 %collective-permute-start.21 = (bf16[4,8,14336]{2,1,0:T(8,128)(2,1)S(1)}, bf16[4,8,14336]{2,1,0:T(8,128)(2,1)S(1)}, u32[]{:S(2)}, u32[]{:S(2)}) collective-permute-start(bf16[4,8,14336]{2,1,0:T(8,128)(2,1)S(1)} %bitcast_dynamic-update-slice_fusion.6), channel_id=1, source_target_pairs={{0,6},{1,7},{2,0},{3,1},{4,2},{5,3},{6,4},{7,5},{8,14},{9,15},{10,... | collective-permute-start | bytes 2752520 | tf_op jit(solution)/shard_map/ppermute | solution.py:30
  75.3 5.8 %collective-permute-done.13 = bf16[8,14336]{1,0:T(8,128)(2,1)S(1)} collective-permute-done((bf16[8,14336]{1,0:T(8,128)(2,1)S(1)}, bf16[8,14336]{1,0:T(8,128)(2,1)S(1)}, u32[]{:S(2)}, u32[]{:S(2)}) %collective-permute-start.13) | collective-permute-done | bytes 229408 | tf_op jit(solution)/shard_map/ppermute | solution.py:30
  81.5 2.9 %collective-permute-start.20 = (bf16[4,8,14336]{2,1,0:T(8,128)(2,1)S(1)}, bf16[4,8,14336]{2,1,0:T(8,128)(2,1)S(1)}, u32[]{:S(2)}, u32[]{:S(2)}) collective-permute-start(bf16[4,8,14336]{2,1,0:T(8,128)(2,1)S(1)} %bitcast_dynamic-update-slice_fusion.10), channel_id=1, source_target_pairs={{0,65},{1,64},{2,67},{3,66},{4,69},{5,68},{6,71},{7,70},{8,73},{9,... | collective-permute-start | bytes 2752520 | tf_op jit(solution)/shard_map/ppermute | solution.py:30
  85.3 8.1 %collective-permute-done.19 = bf16[4,8,14336]{2,1,0:T(8,128)(2,1)S(1)} collective-permute-done((bf16[4,8,14336]{2,1,0:T(8,128)(2,1)S(1)}, bf16[4,8,14336]{2,1,0:T(8,128)(2,1)S(1)}, u32[]{:S(2)}, u32[]{:S(2)}) %collective-permute-start.19) | collective-permute-done | bytes 917536 | tf_op jit(solution)/shard_map/ppermute | solution.py:30
  94.0 2.9 %collective-permute-start.25 = (bf16[2,8,14336]{2,1,0:T(8,128)(2,1)S(1)}, bf16[2,8,14336]{2,1,0:T(8,128)(2,1)S(1)}, u32[]{:S(2)}, u32[]{:S(2)}) collective-permute-start(bf16[2,8,14336]{2,1,0:T(8,128)(2,1)S(1)} %slice.112), channel_id=1, source_target_pairs={{0,6},{1,7},{2,0},{3,1},{4,2},{5,3},{6,4},{7,5},{8,14},{9,15},{10,... | collective-permute-start | bytes 1376264 | tf_op jit(solution)/shard_map/ppermute | solution.py:30
  96.9 1.6 %collective-permute-start.22 = (bf16[2,8,14336]{2,1,0:T(8,128)(2,1)S(1)}, bf16[2,8,14336]{2,1,0:T(8,128)(2,1)S(1)}, u32[]{:S(2)}, u32[]{:S(2)}) collective-permute-start(bf16[2,8,14336]{2,1,0:T(8,128)(2,1)S(1)} %slice.109), channel_id=1, source_target_pairs={{0,64},{1,65},{2,66},{3,67},{4,68},{5,69},{6,70},{7,71},{8,72},{9,... | collective-permute-start | bytes 1376264 | tf_op jit(solution)/shard_map/ppermute | solution.py:30
  98.6 1.8 %collective-permute-start.23 = (bf16[2,8,14336]{2,1,0:T(8,128)(2,1)S(1)}, bf16[2,8,14336]{2,1,0:T(8,128)(2,1)S(1)}, u32[]{:S(2)}, u32[]{:S(2)}) collective-permute-start(bf16[2,8,14336]{2,1,0:T(8,128)(2,1)S(1)} %slice.110), channel_id=1, source_target_pairs={{0,65},{1,64},{2,67},{3,66},{4,69},{5,68},{6,71},{7,70},{8,73},{9,... | collective-permute-start | bytes 1376264 | tf_op jit(solution)/shard_map/ppermute | solution.py:30
  100.7 6.0 %collective-permute-done.22 = bf16[2,8,14336]{2,1,0:T(8,128)(2,1)S(1)} collective-permute-done((bf16[2,8,14336]{2,1,0:T(8,128)(2,1)S(1)}, bf16[2,8,14336]{2,1,0:T(8,128)(2,1)S(1)}, u32[]{:S(2)}, u32[]{:S(2)}) %collective-permute-start.22) | collective-permute-done | bytes 458784 | tf_op jit(solution)/shard_map/ppermute | solution.py:30
  107.4 3.0 %copy-done.5 = bf16[4,4,8,28672]{3,2,1,0:T(8,128)(2,1)} copy-done((bf16[4,4,8,28672]{3,2,1,0:T(8,128)(2,1)}, bf16[4,4,8,28672]{3,2,1,0:T(8,128)(2,1)S(1)}, u32[]{:S(2)}) %copy-start.5) | copy-done | bytes 7340056
  (67 shorter events, 14.6 us)
Async XLA Ops:
  0.0 14.8 %collective-permute-start.1 = (f32[1]{0:T(128)}, f32[1]{0:T(128)}, u32[]{:S(2)}, u32[]{:S(2)}) collective-permute-start(f32[1]{0:T(128)} %param.9), channel_id=1, source_target_pairs={{0,8},{8,16},{16,24},{24,32},{32,40},{40,48},{48,56},{56,64},{64,7... | collective-permute-start | bytes 20 | tf_op jit(solution)/shard_map/ppermute | solution.py:128
  5.1 10.3 %collective-permute-start = (f32[16,28672]{1,0:T(8,128)}, f32[16,28672]{1,0:T(8,128)}, u32[]{:S(2)}, u32[]{:S(2)}) collective-permute-start(f32[16,28672]{1,0:T(8,128)} %shard_map.55), channel_id=1, source_target_pairs={{0,8},{1,9},{2,10},{3,11},{4,12},{5,13},{6,14},{7,15},{8,0},{9,1},... | collective-permute-start | bytes 5505032 | tf_op jit(solution)/shard_map/ppermute | solution.py:30
  6.8 8.6 %copy-start = (bf16[4,1,16,28672]{3,2,1,0:T(8,128)(2,1)S(1)}, bf16[4,1,16,28672]{3,2,1,0:T(8,128)(2,1)}, u32[]{:S(2)}) copy-start(bf16[4,1,16,28672]{3,2,1,0:T(8,128)(2,1)} %grads.1) | copy-start | bytes 11010052
  6.9 8.6 %copy-start.2 = (f32[1,16,28672]{2,1,0:T(8,128)S(1)}, f32[1,16,28672]{2,1,0:T(8,128)}, u32[]{:S(2)}) copy-start(f32[1,16,28672]{2,1,0:T(8,128)} %first_moment.1) | copy-start | bytes 5505028
  6.9 8.6 %copy-start.6 = (f32[16,28672]{1,0:T(8,128)S(1)}, f32[16,28672]{1,0:T(8,128)}, u32[]{:S(2)}) copy-start(f32[16,28672]{1,0:T(8,128)} %shard_map.55) | copy-start | bytes 5505028
  12.5 3.0 %copy-start.1 = (f32[1,16,28672]{2,1,0:T(8,128)S(1)}, f32[1,16,28672]{2,1,0:T(8,128)}, u32[]{:S(2)}) copy-start(f32[1,16,28672]{2,1,0:T(8,128)} %second_moment.1) | copy-start | bytes 5505028
  12.8 12.7 %collective-permute-start.3 = (bf16[8,28672]{1,0:T(8,128)(2,1)S(1)}, bf16[8,28672]{1,0:T(8,128)(2,1)S(1)}, u32[]{:S(2)}, u32[]{:S(2)}) collective-permute-start(bf16[8,28672]{1,0:T(8,128)(2,1)S(1)} %fusion.45), channel_id=1, source_target_pairs={{0,64},{1,65},{2,66},{3,67},{4,68},{5,69},{6,70},{7,71},{8,72},{9,... | collective-permute-start | bytes 1376264 | tf_op jit(solution)/shard_map/ppermute | solution.py:30
  19.4 15.6 %collective-permute-start.2 = (bf16[16,14336]{1,0:T(8,128)(2,1)S(1)}, bf16[16,14336]{1,0:T(8,128)(2,1)S(1)}, u32[]{:S(2)}, u32[]{:S(2)}) collective-permute-start(bf16[16,14336]{1,0:T(8,128)(2,1)S(1)} %get-tuple-element.46), channel_id=1, source_target_pairs={{0,16},{1,17},{2,18},{3,19},{4,20},{5,21},{6,22},{7,23},{8,24},{9,... | collective-permute-start | bytes 1376264 | tf_op jit(solution)/shard_map/ppermute | solution.py:30
  21.0 14.0 %collective-permute-start.5 = (bf16[16,14336]{1,0:T(8,128)(2,1)S(1)}, bf16[16,14336]{1,0:T(8,128)(2,1)S(1)}, u32[]{:S(2)}, u32[]{:S(2)}) collective-permute-start(bf16[16,14336]{1,0:T(8,128)(2,1)S(1)} %get-tuple-element.45), channel_id=1, source_target_pairs={{0,48},{1,49},{2,50},{3,51},{4,52},{5,53},{6,54},{7,55},{8,56},{9,... | collective-permute-start | bytes 1376264 | tf_op jit(solution)/shard_map/ppermute | solution.py:30
  25.5 8.8 %collective-permute-start.4 = (f32[1]{0:T(128)}, f32[1]{0:T(128)}, u32[]{:S(2)}, u32[]{:S(2)}) collective-permute-start(f32[1]{0:T(128)} %add.223), channel_id=1, source_target_pairs={{0,16},{8,24},{16,32},{24,40},{32,48},{40,56},{48,64},{56,72},{64,... | collective-permute-start | bytes 20 | tf_op jit(solution)/shard_map/ppermute | solution.py:128
  37.8 8.6 %collective-permute-start.7 = (bf16[8,14336]{1,0:T(8,128)(2,1)}, bf16[8,14336]{1,0:T(8,128)(2,1)S(1)}, u32[]{:S(2)}, u32[]{:S(2)}) collective-permute-start(bf16[8,14336]{1,0:T(8,128)(2,1)} %get-tuple-element.32), channel_id=1, source_target_pairs={{0,64},{1,65},{2,66},{3,67},{4,68},{5,69},{6,70},{7,71},{8,72},{9,... | collective-permute-start | bytes 688136 | tf_op jit(solution)/shard_map/ppermute | solution.py:30
  39.1 5.9 %collective-permute-start.8 = (f32[1]{0:T(128)}, f32[1]{0:T(128)}, u32[]{:S(2)}, u32[]{:S(2)}) collective-permute-start(f32[1]{0:T(128)} %add.224), channel_id=1, source_target_pairs={{0,32},{8,40},{16,48},{24,56},{32,64},{40,72},{48,80},{56,88},{64,... | collective-permute-start | bytes 20 | tf_op jit(solution)/shard_map/ppermute | solution.py:128
  41.0 11.1 %collective-permute-start.6 = (bf16[8,14336]{1,0:T(8,128)(2,1)}, bf16[8,14336]{1,0:T(8,128)(2,1)S(1)}, u32[]{:S(2)}, u32[]{:S(2)}) collective-permute-start(bf16[8,14336]{1,0:T(8,128)(2,1)} %get-tuple-element.31), channel_id=1, source_target_pairs={{0,64},{1,65},{2,66},{3,67},{4,68},{5,69},{6,70},{7,71},{8,72},{9,... | collective-permute-start | bytes 688136 | tf_op jit(solution)/shard_map/ppermute | solution.py:30
  47.4 4.7 %copy-start.4 = (f32[16,14336]{1,0:T(8,128)S(1)}, f32[16,14336]{1,0:T(8,128)}, u32[]{:S(2)}) copy-start(f32[16,14336]{1,0:T(8,128)} %copy-done.3) | copy-start | bytes 2752516
  47.4 3.6 %collective-permute-start.9 = (f32[1]{0:T(128)}, f32[1]{0:T(128)}, u32[]{:S(2)}, u32[]{:S(2)}) collective-permute-start(f32[1]{0:T(128)} %add.230), channel_id=1, source_target_pairs={{0,64},{8,72},{16,80},{24,88},{32,96},{40,104},{48,112},{56,120},{... | collective-permute-start | bytes 20 | tf_op jit(solution)/shard_map/ppermute | solution.py:128
  49.7 8.3 %collective-permute-start.14 = (bf16[8,14336]{1,0:T(8,128)(2,1)}, bf16[8,14336]{1,0:T(8,128)(2,1)}, u32[]{:S(2)}, u32[]{:S(2)}) collective-permute-start(bf16[8,14336]{1,0:T(8,128)(2,1)} %fusion.84), channel_id=1, source_target_pairs={{0,32},{1,33},{2,34},{3,35},{4,36},{5,37},{6,38},{7,39},{8,40},{9,... | collective-permute-start | bytes 688136 | tf_op jit(solution)/shard_map/ppermute | solution.py:30
  53.2 11.6 %collective-permute-start.10 = (bf16[8,14336]{1,0:T(8,128)(2,1)S(1)}, bf16[8,14336]{1,0:T(8,128)(2,1)S(1)}, u32[]{:S(2)}, u32[]{:S(2)}) collective-permute-start(bf16[8,14336]{1,0:T(8,128)(2,1)S(1)} %get-tuple-element.47), channel_id=1, source_target_pairs={{0,32},{1,33},{2,34},{3,35},{4,36},{5,37},{6,38},{7,39},{8,40},{9,... | collective-permute-start | bytes 688136 | tf_op jit(solution)/shard_map/ppermute | solution.py:30
  59.1 9.3 %collective-permute-start.15 = (bf16[8,14336]{1,0:T(8,128)(2,1)S(1)}, bf16[8,14336]{1,0:T(8,128)(2,1)S(1)}, u32[]{:S(2)}, u32[]{:S(2)}) collective-permute-start(bf16[8,14336]{1,0:T(8,128)(2,1)S(1)} %get-tuple-element.38), channel_id=1, source_target_pairs={{0,64},{1,65},{2,66},{3,67},{4,68},{5,69},{6,70},{7,71},{8,72},{9,... | collective-permute-start | bytes 688136 | tf_op jit(solution)/shard_map/ppermute | solution.py:30
  60.2 10.3 %collective-permute-start.16 = (bf16[8,14336]{1,0:T(8,128)(2,1)S(1)}, bf16[8,14336]{1,0:T(8,128)(2,1)S(1)}, u32[]{:S(2)}, u32[]{:S(2)}) collective-permute-start(bf16[8,14336]{1,0:T(8,128)(2,1)S(1)} %get-tuple-element.38), channel_id=1, source_target_pairs={{0,65},{1,64},{2,67},{3,66},{4,69},{5,68},{6,71},{7,70},{8,73},{9,... | collective-permute-start | bytes 688136 | tf_op jit(solution)/shard_map/ppermute | solution.py:30
  62.4 8.0 %collective-permute-start.17 = (bf16[8,14336]{1,0:T(8,128)(2,1)S(1)}, bf16[8,14336]{1,0:T(8,128)(2,1)S(1)}, u32[]{:S(2)}, u32[]{:S(2)}) collective-permute-start(bf16[8,14336]{1,0:T(8,128)(2,1)S(1)} %get-tuple-element.38), channel_id=1, source_target_pairs={{0,1},{1,0},{2,3},{3,2},{4,5},{5,4},{6,7},{7,6},{8,9},{9,8},{10,11... | collective-permute-start | bytes 688136 | tf_op jit(solution)/shard_map/ppermute | solution.py:30
  65.1 9.8 %collective-permute-start.11 = (bf16[8,14336]{1,0:T(8,128)(2,1)S(1)}, bf16[8,14336]{1,0:T(8,128)(2,1)S(1)}, u32[]{:S(2)}, u32[]{:S(2)}) collective-permute-start(bf16[8,14336]{1,0:T(8,128)(2,1)S(1)} %get-tuple-element.40), channel_id=1, source_target_pairs={{0,2},{1,3},{2,4},{3,5},{4,6},{5,7},{6,0},{7,1},{8,10},{9,11},{10,... | collective-permute-start | bytes 688136 | tf_op jit(solution)/shard_map/ppermute | solution.py:30
  66.8 8.5 %collective-permute-start.12 = (bf16[8,14336]{1,0:T(8,128)(2,1)S(1)}, bf16[8,14336]{1,0:T(8,128)(2,1)S(1)}, u32[]{:S(2)}, u32[]{:S(2)}) collective-permute-start(bf16[8,14336]{1,0:T(8,128)(2,1)S(1)} %get-tuple-element.40), channel_id=1, source_target_pairs={{0,6},{1,7},{2,0},{3,1},{4,2},{5,3},{6,4},{7,5},{8,14},{9,15},{10,... | collective-permute-start | bytes 688136 | tf_op jit(solution)/shard_map/ppermute | solution.py:30
  68.4 12.7 %collective-permute-start.13 = (bf16[8,14336]{1,0:T(8,128)(2,1)S(1)}, bf16[8,14336]{1,0:T(8,128)(2,1)S(1)}, u32[]{:S(2)}, u32[]{:S(2)}) collective-permute-start(bf16[8,14336]{1,0:T(8,128)(2,1)S(1)} %get-tuple-element.40), channel_id=1, source_target_pairs={{0,4},{1,5},{2,6},{3,7},{4,0},{5,1},{6,2},{7,3},{8,12},{9,13},{10,... | collective-permute-start | bytes 688136 | tf_op jit(solution)/shard_map/ppermute | solution.py:30
  70.5 22.9 %collective-permute-start.19 = (bf16[4,8,14336]{2,1,0:T(8,128)(2,1)S(1)}, bf16[4,8,14336]{2,1,0:T(8,128)(2,1)S(1)}, u32[]{:S(2)}, u32[]{:S(2)}) collective-permute-start(bf16[4,8,14336]{2,1,0:T(8,128)(2,1)S(1)} %bitcast_dynamic-update-slice_fusion.6), channel_id=1, source_target_pairs={{0,2},{1,3},{2,4},{3,5},{4,6},{5,7},{6,0},{7,1},{8,10},{9,11},{10,... | collective-permute-start | bytes 2752520 | tf_op jit(solution)/shard_map/ppermute | solution.py:30
  71.9 22.1 %collective-permute-start.21 = (bf16[4,8,14336]{2,1,0:T(8,128)(2,1)S(1)}, bf16[4,8,14336]{2,1,0:T(8,128)(2,1)S(1)}, u32[]{:S(2)}, u32[]{:S(2)}) collective-permute-start(bf16[4,8,14336]{2,1,0:T(8,128)(2,1)S(1)} %bitcast_dynamic-update-slice_fusion.6), channel_id=1, source_target_pairs={{0,6},{1,7},{2,0},{3,1},{4,2},{5,3},{6,4},{7,5},{8,14},{9,15},{10,... | collective-permute-start | bytes 2752520 | tf_op jit(solution)/shard_map/ppermute | solution.py:30
  81.1 15.8 %collective-permute-start.18 = (bf16[4,8,14336]{2,1,0:T(8,128)(2,1)S(1)}, bf16[4,8,14336]{2,1,0:T(8,128)(2,1)S(1)}, u32[]{:S(2)}, u32[]{:S(2)}) collective-permute-start(bf16[4,8,14336]{2,1,0:T(8,128)(2,1)S(1)} %bitcast_dynamic-update-slice_fusion.10), channel_id=1, source_target_pairs={{0,64},{1,65},{2,66},{3,67},{4,68},{5,69},{6,70},{7,71},{8,72},{9,... | collective-permute-start | bytes 2752520 | tf_op jit(solution)/shard_map/ppermute | solution.py:30
  81.5 17.0 %collective-permute-start.20 = (bf16[4,8,14336]{2,1,0:T(8,128)(2,1)S(1)}, bf16[4,8,14336]{2,1,0:T(8,128)(2,1)S(1)}, u32[]{:S(2)}, u32[]{:S(2)}) collective-permute-start(bf16[4,8,14336]{2,1,0:T(8,128)(2,1)S(1)} %bitcast_dynamic-update-slice_fusion.10), channel_id=1, source_target_pairs={{0,65},{1,64},{2,67},{3,66},{4,69},{5,68},{6,71},{7,70},{8,73},{9,... | collective-permute-start | bytes 2752520 | tf_op jit(solution)/shard_map/ppermute | solution.py:30
  93.5 13.8 %collective-permute-start.24 = (bf16[2,8,14336]{2,1,0:T(8,128)(2,1)S(1)}, bf16[2,8,14336]{2,1,0:T(8,128)(2,1)S(1)}, u32[]{:S(2)}, u32[]{:S(2)}) collective-permute-start(bf16[2,8,14336]{2,1,0:T(8,128)(2,1)S(1)} %slice.111), channel_id=1, source_target_pairs={{0,2},{1,3},{2,4},{3,5},{4,6},{5,7},{6,0},{7,1},{8,10},{9,11},{10,... | collective-permute-start | bytes 1376264 | tf_op jit(solution)/shard_map/ppermute | solution.py:30
  94.0 13.2 %collective-permute-start.25 = (bf16[2,8,14336]{2,1,0:T(8,128)(2,1)S(1)}, bf16[2,8,14336]{2,1,0:T(8,128)(2,1)S(1)}, u32[]{:S(2)}, u32[]{:S(2)}) collective-permute-start(bf16[2,8,14336]{2,1,0:T(8,128)(2,1)S(1)} %slice.112), channel_id=1, source_target_pairs={{0,6},{1,7},{2,0},{3,1},{4,2},{5,3},{6,4},{7,5},{8,14},{9,15},{10,... | collective-permute-start | bytes 1376264 | tf_op jit(solution)/shard_map/ppermute | solution.py:30
  96.9 9.8 %collective-permute-start.22 = (bf16[2,8,14336]{2,1,0:T(8,128)(2,1)S(1)}, bf16[2,8,14336]{2,1,0:T(8,128)(2,1)S(1)}, u32[]{:S(2)}, u32[]{:S(2)}) collective-permute-start(bf16[2,8,14336]{2,1,0:T(8,128)(2,1)S(1)} %slice.109), channel_id=1, source_target_pairs={{0,64},{1,65},{2,66},{3,67},{4,68},{5,69},{6,70},{7,71},{8,72},{9,... | collective-permute-start | bytes 1376264 | tf_op jit(solution)/shard_map/ppermute | solution.py:30
  98.6 8.5 %collective-permute-start.23 = (bf16[2,8,14336]{2,1,0:T(8,128)(2,1)S(1)}, bf16[2,8,14336]{2,1,0:T(8,128)(2,1)S(1)}, u32[]{:S(2)}, u32[]{:S(2)}) collective-permute-start(bf16[2,8,14336]{2,1,0:T(8,128)(2,1)S(1)} %slice.110), channel_id=1, source_target_pairs={{0,65},{1,64},{2,67},{3,66},{4,69},{5,68},{6,71},{7,70},{8,73},{9,... | collective-permute-start | bytes 1376264 | tf_op jit(solution)/shard_map/ppermute | solution.py:30
  107.4 3.1 %copy-start.5 = (bf16[4,4,8,28672]{3,2,1,0:T(8,128)(2,1)}, bf16[4,4,8,28672]{3,2,1,0:T(8,128)(2,1)S(1)}, u32[]{:S(2)}) copy-start(bf16[4,4,8,28672]{3,2,1,0:T(8,128)(2,1)S(1)} %fusion.59) | copy-start | bytes 22020100
  (1 other events, 0.9 us)

commit v4 on v3

--- a/solution.py
+++ b/solution.py
@@ -94,6 +94,23 @@
     return jnp.where(code < 0, -root, root)
 
 
+def unwritten(shape, dtype):
+    return pl.pallas_call(
+        lambda out: None, out_specs=pl.BlockSpec(memory_space=pltpu.HBM), out_shape=jax.ShapeDtypeStruct(shape, dtype)
+    )()
+
+
+def held(value):
+    spec = pl.BlockSpec(memory_space=pltpu.HBM)
+    return pl.pallas_call(
+        lambda value, out: None,
+        in_specs=[spec],
+        out_specs=spec,
+        out_shape=jax.ShapeDtypeStruct(value.shape, value.dtype),
+        input_output_aliases={0: 0},
+    )(value)
+
+
 def gathered(one, two, y, z):
     rows, half = one.shape
     along_y = lambda v, s: moved(v, lambda x, yy, zz, c: (x, yy + s, zz, c))
@@ -106,17 +123,25 @@
             block = lax.dynamic_update_slice(block, along(v, s)[None], ((at - s) % 4, 0, 0))
         return block
 
-    def blocks(v, along):
-        ahead, back = along(v, -1), along(v, 1)
-        far = jnp.concatenate([along(back[:2], 1), along(ahead[2:], -1)])
-        return ((v, 0), (back, -1), (ahead, 1), (far, 2))
+    def put_one(out, block, first, off):
+        return lax.dynamic_update_slice(out, block[:, None], (first, (z + off) % 4, 0, 0))
+
+    def put_two(out, block, first, off):
+        return lax.dynamic_update_slice(out, block[None], ((y + off) % 4, first, 0, half))
 
     one, two = line(one, along_y, y), line(two, along_z, z)
-    out = jnp.zeros((4, 4, rows, 2 * half), one.dtype)
-    for (block_one, off), (block_two, _) in zip(blocks(one, along_z), blocks(two, along_y)):
-        out = lax.dynamic_update_slice(out, block_one[:, None], (0, (z + off) % 4, 0, 0))
-        out = lax.dynamic_update_slice(out, block_two[None], ((y + off) % 4, 0, 0, half))
-    return out
+    out = unwritten((4, 4, rows, 2 * half), one.dtype)
+    out = put_two(put_one(out, one, 0, 0), two, 0, 0)
+    near, ends = [], []
+    for put, block, along in ((put_one, one, along_z), (put_two, two, along_y)):
+        ahead, back = along(block, -1), along(block, 1)
+        near.append((put, back, ahead))
+        ends.append((put, along(back[:2], 1), along(ahead[2:], -1)))
+    for put, back, ahead in reversed(near):
+        out = put(put(out, back, 0, -1), ahead, 0, 1)
+    for put, low, high in reversed(ends):
+        out = put(put(out, low, 0, 2), high, 2, 2)
+    return held(out)
 
 
 def per_device(params, first_moment, second_moment, grads, push_weight):

time: 112 us -> 111 us (level)
  local copies, waits for them, and re-layouts: 5.54 us -> 10.4 us
  waiting for transfers between devices: 35.8 us -> 31 us
    dynamic_update_slice x6 -> x10, local copies, waits for them, and re-layouts: 0.49 us -> 9.08 us  [the longest x5 4.54 us: put_two(): lax.dynamic_update_slice(out, block[None], ((y + off) % 4, first, 0, half))]
    ppermute x22, waiting for transfers between devices: 27.6 us -> 22.8 us  [moved(): return lax.ppermute(value, AXES, pairs)]
    unnamed x14 -> x12, local copies, waits for them, and re-layouts: 3.98 us -> 0.94 us
  transfers between devices with their start and end apart: 26 -> 26, of which waited for: 12 -> 11; matrix products, arithmetic and copies ran while one was open for 14% -> 20% of each run, Pallas kernels for 4% -> 4%
where the time goes in v4:
time: 111 us; the launch traced here: 110 us
  starting transfers between devices  45.4 us (41%)
  waiting for transfers between devices  31 us (28%)
  other arithmetic  15.7 us (14%)
  local copies, waits for them, and re-layouts  10.4 us (9%)
  Pallas kernels  4.47 us (4%)
  between operations  3.39 us (3%)
    ppermute x22, starting transfers between devices, moved(): return lax.ppermute(value, AXES, pairs)  36 us
    ppermute x22, waiting for transfers between devices, moved(): return lax.ppermute(value, AXES, pairs)  22.8 us
    ppermute x4, starting transfers between devices, per_device(): lax.ppermute(v, 'replica', [(r, (r + steps) % REPLICAS) for r in range(RE...  9.35 us
    ppermute x4, waiting for transfers between devices, per_device(): lax.ppermute(v, 'replica', [(r, (r + steps) % REPLICAS) for r in range(RE...  8.13 us
    mul x1, other arithmetic, per_device(): d = -learn_rate / 2.0 * update(*moments(*later, 4), 3)  5.65 us
    dynamic_update_slice x5, local copies, waits for them, and re-layouts, put_two(): lax.dynamic_update_slice(out, block[None], ((y + off) % 4, first, 0, half))  4.54 us
    dynamic_update_slice x5, local copies, waits for them, and re-layouts, put_one(): lax.dynamic_update_slice(out, block[:, None], (first, (z + off) % 4, 0, 0))  4.54 us
    pallas_call x1, Pallas kernels, first_term(): pl.pallas_call(first_kernel, grid=(cols // BLOCK,), in_specs=[SMEM, spec,...  4.47 us
  transfers between devices with their start and end apart: 26, of which 11 were waited for; matrix products, arithmetic and copies ran while one was open for 20% of the time, Pallas kernels for 4%

profile of v4, /device:TPU:0, one launch (start us, length us, event | category | flops | bytes accessed | tf_op | source)
XLA Modules:
  0.0 110.3 jit_solution(9217272411495639507)
XLA Ops:
  0.7 4.5 %shard_map.56 = f32[16,28672]{1,0:T(8,128)} custom-call(f32[1]{0:T(128)S(6)} %copy.30.weight, f32[1,16,28672]{2,1,0:T(8,128)} %params.1, f32[1,16,28672]{2,1,0:T(8,128)} %first_moment.1, f32[1,16,28672]{2,1,0:T(8,128)} %second_moment.1, bf16[4,1,16,28672]{3,2,1,0:T(8,128)(2,1)} %grads.1), custom_call_target="tpu_custom_call" | custom-call | flops 9175040 | bytes 8257536 | tf_op jit(solution)/shard_map/pallas_call | solution.py:81
  5.1 1.7 %collective-permute-start = (f32[16,28672]{1,0:T(8,128)}, f32[16,28672]{1,0:T(8,128)}, u32[]{:S(2)}, u32[]{:S(2)}) collective-permute-start(f32[16,28672]{1,0:T(8,128)} %shard_map.56), channel_id=1, source_target_pairs={{0,8},{1,9},{2,10},{3,11},{4,12},{5,13},{6,14},{7,15},{8,0},{9,1},... | collective-permute-start | bytes 5505032 | tf_op jit(solution)/shard_map/ppermute | solution.py:30
  6.9 5.6 %fusion.13 = (f32[16,28672]{1,0:T(8,128)S(1)}, f32[16,28672]{1,0:T(8,128)S(1)}) fusion(bf16[4,16,28672]{2,1,0:T(8,128)(2,1)} %bitcast.97, f32[16,28672]{1,0:T(8,128)} %bitcast.101, f32[16,28672]{1,0:T(8,128)} %bitcast.99), kind=kLoop, calls=%fused_computation.31 | loop fusion | flops 19267584 | bytes 11010048 | tf_op jit(solution)/shard_map/mul | solution.py:170
  12.8 2.0 %collective-permute-start.3 = (bf16[8,28672]{1,0:T(8,128)(2,1)S(1)}, bf16[8,28672]{1,0:T(8,128)(2,1)S(1)}, u32[]{:S(2)}, u32[]{:S(2)}) collective-permute-start(bf16[8,28672]{1,0:T(8,128)(2,1)S(1)} %fusion.45), channel_id=1, source_target_pairs={{0,64},{1,65},{2,66},{3,67},{4,68},{5,69},{6,70},{7,71},{8,72},{9,... | collective-permute-start | bytes 1376264 | tf_op jit(solution)/shard_map/ppermute | solution.py:30
  15.5 3.5 %fusion.24 = f32[16,28672]{1,0:T(8,128)S(1)} fusion(f32[16,28672]{1,0:T(8,128)S(1)} %bitcast.100, f32[16,28672]{1,0:T(8,128)S(1)} %bitcast.102, f32[16,28672]{1,0:T(8,128)S(1)} %copy-done.5, f32[16,28672]{1,0:T(8,128)} %collective-permute-done, bf16[4,16,28672]{2,1,0:T(8,128)(2,1)S(1)} %bitcast.98, f32[]{:T(128)} %bitcast.11), kind=kLoop, calls=%fused_computation.42 | loop fusion | flops 10551296 | bytes 11010052 | tf_op jit(solution)/shard_map/add | solution.py:176
  19.4 1.6 %collective-permute-start.2 = (bf16[16,14336]{1,0:T(8,128)(2,1)S(1)}, bf16[16,14336]{1,0:T(8,128)(2,1)S(1)}, u32[]{:S(2)}, u32[]{:S(2)}) collective-permute-start(bf16[16,14336]{1,0:T(8,128)(2,1)S(1)} %get-tuple-element.46), channel_id=1, source_target_pairs={{0,16},{1,17},{2,18},{3,19},{4,20},{5,21},{6,22},{7,23},{8,24},{9,... | collective-permute-start | bytes 1376264 | tf_op jit(solution)/shard_map/ppermute | solution.py:30
  21.0 1.8 %collective-permute-start.5 = (bf16[16,14336]{1,0:T(8,128)(2,1)S(1)}, bf16[16,14336]{1,0:T(8,128)(2,1)S(1)}, u32[]{:S(2)}, u32[]{:S(2)}) collective-permute-start(bf16[16,14336]{1,0:T(8,128)(2,1)S(1)} %get-tuple-element.45), channel_id=1, source_target_pairs={{0,48},{1,49},{2,50},{3,51},{4,52},{5,53},{6,54},{7,55},{8,56},{9,... | collective-permute-start | bytes 1376264 | tf_op jit(solution)/shard_map/ppermute | solution.py:30
  22.8 2.7 %collective-permute-done.3 = bf16[8,28672]{1,0:T(8,128)(2,1)S(1)} collective-permute-done((bf16[8,28672]{1,0:T(8,128)(2,1)S(1)}, bf16[8,28672]{1,0:T(8,128)(2,1)S(1)}, u32[]{:S(2)}, u32[]{:S(2)}) %collective-permute-start.3) | collective-permute-done | bytes 458784 | tf_op jit(solution)/shard_map/ppermute | solution.py:30
  25.5 5.2 %collective-permute-start.4 = (f32[1]{0:T(128)}, f32[1]{0:T(128)}, u32[]{:S(2)}, u32[]{:S(2)}) collective-permute-start(f32[1]{0:T(128)} %add.229), channel_id=1, source_target_pairs={{0,16},{8,24},{16,32},{24,40},{32,48},{40,56},{48,64},{56,72},{64,... | collective-permute-start | bytes 20 | tf_op jit(solution)/shard_map/ppermute | solution.py:153
  30.7 3.6 %collective-permute-done.4 = f32[1]{0:T(128)} collective-permute-done((f32[1]{0:T(128)}, f32[1]{0:T(128)}, u32[]{:S(2)}, u32[]{:S(2)}) %collective-permute-start.4) | collective-permute-done | bytes 36 | tf_op jit(solution)/shard_map/ppermute | solution.py:153
  37.7 1.3 %collective-permute-start.7 = (bf16[8,14336]{1,0:T(8,128)(2,1)}, bf16[8,14336]{1,0:T(8,128)(2,1)S(1)}, u32[]{:S(2)}, u32[]{:S(2)}) collective-permute-start(bf16[8,14336]{1,0:T(8,128)(2,1)} %get-tuple-element.32), channel_id=1, source_target_pairs={{0,64},{1,65},{2,66},{3,67},{4,68},{5,69},{6,70},{7,71},{8,72},{9,... | collective-permute-start | bytes 688136 | tf_op jit(solution)/shard_map/ppermute | solution.py:30
  39.0 1.9 %collective-permute-start.8 = (f32[1]{0:T(128)}, f32[1]{0:T(128)}, u32[]{:S(2)}, u32[]{:S(2)}) collective-permute-start(f32[1]{0:T(128)} %add.230), channel_id=1, source_target_pairs={{0,32},{8,40},{16,48},{24,56},{32,64},{40,72},{48,80},{56,88},{64,... | collective-permute-start | bytes 20 | tf_op jit(solution)/shard_map/ppermute | solution.py:153
  41.7 3.3 %collective-permute-done.8 = f32[1]{0:T(128)} collective-permute-done((f32[1]{0:T(128)}, f32[1]{0:T(128)}, u32[]{:S(2)}, u32[]{:S(2)}) %collective-permute-start.8) | collective-permute-done | bytes 36 | tf_op jit(solution)/shard_map/ppermute | solution.py:153
  47.4 2.3 %collective-permute-start.9 = (f32[1]{0:T(128)}, f32[1]{0:T(128)}, u32[]{:S(2)}, u32[]{:S(2)}) collective-permute-start(f32[1]{0:T(128)} %add.236), channel_id=1, source_target_pairs={{0,64},{8,72},{16,80},{24,88},{32,96},{40,104},{48,112},{56,120},{... | collective-permute-start | bytes 20 | tf_op jit(solution)/shard_map/ppermute | solution.py:153
  49.6 1.2 %collective-permute-done.9 = f32[1]{0:T(128)} collective-permute-done((f32[1]{0:T(128)}, f32[1]{0:T(128)}, u32[]{:S(2)}, u32[]{:S(2)}) %collective-permute-start.9) | collective-permute-done | bytes 36 | tf_op jit(solution)/shard_map/ppermute | solution.py:153
  53.2 2.6 %collective-permute-start.10 = (bf16[8,14336]{1,0:T(8,128)(2,1)S(1)}, bf16[8,14336]{1,0:T(8,128)(2,1)S(1)}, u32[]{:S(2)}, u32[]{:S(2)}) collective-permute-start(bf16[8,14336]{1,0:T(8,128)(2,1)S(1)} %get-tuple-element.47), channel_id=1, source_target_pairs={{0,32},{1,33},{2,34},{3,35},{4,36},{5,37},{6,38},{7,39},{8,40},{9,... | collective-permute-start | bytes 688136 | tf_op jit(solution)/shard_map/ppermute | solution.py:30
  55.7 2.2 %collective-permute-done.14 = bf16[8,14336]{1,0:T(8,128)(2,1)} collective-permute-done((bf16[8,14336]{1,0:T(8,128)(2,1)}, bf16[8,14336]{1,0:T(8,128)(2,1)}, u32[]{:S(2)}, u32[]{:S(2)}) %collective-permute-start.14) | collective-permute-done | bytes 229408 | tf_op jit(solution)/shard_map/ppermute | solution.py:30
  58.0 1.2 %bitcast_dynamic-update-slice_fusion.13 = (bf16[4,8,14336]{2,1,0:T(8,128)(2,1)S(1)}, bf16[8,14336]{1,0:T(8,128)(2,1)S(1)}) fusion(bf16[4,8,14336]{2,1,0:T(8,128)(2,1)S(1)} %broadcast.61.clone.1, s32[]{:T(128)S(6)} %select_n.192, f32[]{:T(128)S(6)} %add.240, f32[8,14336]{1,0:T(8,128)S(1)} %get-tuple-element.49, bf16[8,14336]{1,0:T(8,128)(2,1)} %collective-permute-done.14), kind=kLoop, calls=%fused_computation.163 | loop fusion | flops 1146880 | bytes 1146888 | tf_op jit(solution)/shard_map/dynamic_update_slice | solution.py:121
  60.2 2.3 %collective-permute-start.16 = (bf16[8,14336]{1,0:T(8,128)(2,1)S(1)}, bf16[8,14336]{1,0:T(8,128)(2,1)S(1)}, u32[]{:S(2)}, u32[]{:S(2)}) collective-permute-start(bf16[8,14336]{1,0:T(8,128)(2,1)S(1)} %get-tuple-element.38), channel_id=1, source_target_pairs={{0,65},{1,64},{2,67},{3,66},{4,69},{5,68},{6,71},{7,70},{8,73},{9,... | collective-permute-start | bytes 688136 | tf_op jit(solution)/shard_map/ppermute | solution.py:30
  62.5 2.4 %collective-permute-start.17 = (bf16[8,14336]{1,0:T(8,128)(2,1)S(1)}, bf16[8,14336]{1,0:T(8,128)(2,1)S(1)}, u32[]{:S(2)}, u32[]{:S(2)}) collective-permute-start(bf16[8,14336]{1,0:T(8,128)(2,1)S(1)} %get-tuple-element.38), channel_id=1, source_target_pairs={{0,1},{1,0},{2,3},{3,2},{4,5},{5,4},{6,7},{7,6},{8,9},{9,8},{10,11... | collective-permute-start | bytes 688136 | tf_op jit(solution)/shard_map/ppermute | solution.py:30
  65.2 1.6 %collective-permute-start.11 = (bf16[8,14336]{1,0:T(8,128)(2,1)S(1)}, bf16[8,14336]{1,0:T(8,128)(2,1)S(1)}, u32[]{:S(2)}, u32[]{:S(2)}) collective-permute-start(bf16[8,14336]{1,0:T(8,128)(2,1)S(1)} %get-tuple-element.40), channel_id=1, source_target_pairs={{0,2},{1,3},{2,4},{3,5},{4,6},{5,7},{6,0},{7,1},{8,10},{9,11},{10,... | collective-permute-start | bytes 688136 | tf_op jit(solution)/shard_map/ppermute | solution.py:30
  66.8 1.7 %collective-permute-start.12 = (bf16[8,14336]{1,0:T(8,128)(2,1)S(1)}, bf16[8,14336]{1,0:T(8,128)(2,1)S(1)}, u32[]{:S(2)}, u32[]{:S(2)}) collective-permute-start(bf16[8,14336]{1,0:T(8,128)(2,1)S(1)} %get-tuple-element.40), channel_id=1, source_target_pairs={{0,6},{1,7},{2,0},{3,1},{4,2},{5,3},{6,4},{7,5},{8,14},{9,15},{10,... | collective-permute-start | bytes 688136 | tf_op jit(solution)/shard_map/ppermute | solution.py:30
  68.5 2.0 %collective-permute-start.13 = (bf16[8,14336]{1,0:T(8,128)(2,1)S(1)}, bf16[8,14336]{1,0:T(8,128)(2,1)S(1)}, u32[]{:S(2)}, u32[]{:S(2)}) collective-permute-start(bf16[8,14336]{1,0:T(8,128)(2,1)S(1)} %get-tuple-element.40), channel_id=1, source_target_pairs={{0,4},{1,5},{2,6},{3,7},{4,0},{5,1},{6,2},{7,3},{8,12},{9,13},{10,... | collective-permute-start | bytes 688136 | tf_op jit(solution)/shard_map/ppermute | solution.py:30
  70.6 1.4 %collective-permute-start.18 = (bf16[4,8,14336]{2,1,0:T(8,128)(2,1)S(1)}, bf16[4,8,14336]{2,1,0:T(8,128)(2,1)S(1)}, u32[]{:S(2)}, u32[]{:S(2)}) collective-permute-start(bf16[4,8,14336]{2,1,0:T(8,128)(2,1)S(1)} %bitcast_dynamic-update-slice_fusion.10), channel_id=1, source_target_pairs={{0,2},{1,3},{2,4},{3,5},{4,6},{5,7},{6,0},{7,1},{8,10},{9,11},{10,... | collective-permute-start | bytes 2752520 | tf_op jit(solution)/shard_map/ppermute | solution.py:30
  72.0 1.9 %collective-permute-start.19 = (bf16[4,8,14336]{2,1,0:T(8,128)(2,1)S(1)}, bf16[4,8,14336]{2,1,0:T(8,128)(2,1)S(1)}, u32[]{:S(2)}, u32[]{:S(2)}) collective-permute-start(bf16[4,8,14336]{2,1,0:T(8,128)(2,1)S(1)} %bitcast_dynamic-update-slice_fusion.10), channel_id=1, source_target_pairs={{0,6},{1,7},{2,0},{3,1},{4,2},{5,3},{6,4},{7,5},{8,14},{9,15},{10,... | collective-permute-start | bytes 2752520 | tf_op jit(solution)/shard_map/ppermute | solution.py:30
  75.4 5.8 %collective-permute-done.13 = bf16[8,14336]{1,0:T(8,128)(2,1)S(1)} collective-permute-done((bf16[8,14336]{1,0:T(8,128)(2,1)S(1)}, bf16[8,14336]{1,0:T(8,128)(2,1)S(1)}, u32[]{:S(2)}, u32[]{:S(2)}) %collective-permute-start.13) | collective-permute-done | bytes 229408 | tf_op jit(solution)/shard_map/ppermute | solution.py:30
  81.6 2.9 %collective-permute-start.21 = (bf16[4,8,14336]{2,1,0:T(8,128)(2,1)S(1)}, bf16[4,8,14336]{2,1,0:T(8,128)(2,1)S(1)}, u32[]{:S(2)}, u32[]{:S(2)}) collective-permute-start(bf16[4,8,14336]{2,1,0:T(8,128)(2,1)S(1)} %bitcast_dynamic-update-slice_fusion.14), channel_id=1, source_target_pairs={{0,65},{1,64},{2,67},{3,66},{4,69},{5,68},{6,71},{7,70},{8,73},{9,... | collective-permute-start | bytes 2752520 | tf_op jit(solution)/shard_map/ppermute | solution.py:30
  86.4 7.1 %collective-permute-done.18 = bf16[4,8,14336]{2,1,0:T(8,128)(2,1)S(1)} collective-permute-done((bf16[4,8,14336]{2,1,0:T(8,128)(2,1)S(1)}, bf16[4,8,14336]{2,1,0:T(8,128)(2,1)S(1)}, u32[]{:S(2)}, u32[]{:S(2)}) %collective-permute-start.18) | collective-permute-done | bytes 917536 | tf_op jit(solution)/shard_map/ppermute | solution.py:30
  94.1 2.9 %collective-permute-start.23 = (bf16[2,8,14336]{2,1,0:T(8,128)(2,1)S(1)}, bf16[2,8,14336]{2,1,0:T(8,128)(2,1)S(1)}, u32[]{:S(2)}, u32[]{:S(2)}) collective-permute-start(bf16[2,8,14336]{2,1,0:T(8,128)(2,1)S(1)} %slice.110), channel_id=1, source_target_pairs={{0,6},{1,7},{2,0},{3,1},{4,2},{5,3},{6,4},{7,5},{8,14},{9,15},{10,... | collective-permute-start | bytes 1376264 | tf_op jit(solution)/shard_map/ppermute | solution.py:30
  99.0 1.6 %collective-permute-start.24 = (bf16[2,8,14336]{2,1,0:T(8,128)(2,1)S(1)}, bf16[2,8,14336]{2,1,0:T(8,128)(2,1)S(1)}, u32[]{:S(2)}, u32[]{:S(2)}) collective-permute-start(bf16[2,8,14336]{2,1,0:T(8,128)(2,1)S(1)} %slice.111), channel_id=1, source_target_pairs={{0,64},{1,65},{2,66},{3,67},{4,68},{5,69},{6,70},{7,71},{8,72},{9,... | collective-permute-start | bytes 1376264 | tf_op jit(solution)/shard_map/ppermute | solution.py:30
  100.6 1.8 %collective-permute-start.25 = (bf16[2,8,14336]{2,1,0:T(8,128)(2,1)S(1)}, bf16[2,8,14336]{2,1,0:T(8,128)(2,1)S(1)}, u32[]{:S(2)}, u32[]{:S(2)}) collective-permute-start(bf16[2,8,14336]{2,1,0:T(8,128)(2,1)S(1)} %slice.112), channel_id=1, source_target_pairs={{0,65},{1,64},{2,67},{3,66},{4,69},{5,68},{6,71},{7,70},{8,73},{9,... | collective-permute-start | bytes 1376264 | tf_op jit(solution)/shard_map/ppermute | solution.py:30
  105.9 2.8 %collective-permute-done.24 = bf16[2,8,14336]{2,1,0:T(8,128)(2,1)S(1)} collective-permute-done((bf16[2,8,14336]{2,1,0:T(8,128)(2,1)S(1)}, bf16[2,8,14336]{2,1,0:T(8,128)(2,1)S(1)}, u32[]{:S(2)}, u32[]{:S(2)}) %collective-permute-start.24) | collective-permute-done | bytes 458784 | tf_op jit(solution)/shard_map/ppermute | solution.py:30
  (68 shorter events, 20.8 us)
Async XLA Ops:
  0.0 14.8 %collective-permute-start.1 = (f32[1]{0:T(128)}, f32[1]{0:T(128)}, u32[]{:S(2)}, u32[]{:S(2)}) collective-permute-start(f32[1]{0:T(128)} %param.9), channel_id=1, source_target_pairs={{0,8},{8,16},{16,24},{24,32},{32,40},{40,48},{48,56},{56,64},{64,7... | collective-permute-start | bytes 20 | tf_op jit(solution)/shard_map/ppermute | solution.py:153
  5.1 10.3 %collective-permute-start = (f32[16,28672]{1,0:T(8,128)}, f32[16,28672]{1,0:T(8,128)}, u32[]{:S(2)}, u32[]{:S(2)}) collective-permute-start(f32[16,28672]{1,0:T(8,128)} %shard_map.56), channel_id=1, source_target_pairs={{0,8},{1,9},{2,10},{3,11},{4,12},{5,13},{6,14},{7,15},{8,0},{9,1},... | collective-permute-start | bytes 5505032 | tf_op jit(solution)/shard_map/ppermute | solution.py:30
  6.8 8.6 %copy-start = (bf16[4,1,16,28672]{3,2,1,0:T(8,128)(2,1)S(1)}, bf16[4,1,16,28672]{3,2,1,0:T(8,128)(2,1)}, u32[]{:S(2)}) copy-start(bf16[4,1,16,28672]{3,2,1,0:T(8,128)(2,1)} %grads.1) | copy-start | bytes 11010052
  6.9 8.6 %copy-start.2 = (f32[1,16,28672]{2,1,0:T(8,128)S(1)}, f32[1,16,28672]{2,1,0:T(8,128)}, u32[]{:S(2)}) copy-start(f32[1,16,28672]{2,1,0:T(8,128)} %first_moment.1) | copy-start | bytes 5505028
  6.9 8.6 %copy-start.5 = (f32[16,28672]{1,0:T(8,128)S(1)}, f32[16,28672]{1,0:T(8,128)}, u32[]{:S(2)}) copy-start(f32[16,28672]{1,0:T(8,128)} %shard_map.56) | copy-start | bytes 5505028
  12.5 3.0 %copy-start.1 = (f32[1,16,28672]{2,1,0:T(8,128)S(1)}, f32[1,16,28672]{2,1,0:T(8,128)}, u32[]{:S(2)}) copy-start(f32[1,16,28672]{2,1,0:T(8,128)} %second_moment.1) | copy-start | bytes 5505028
  12.8 12.7 %collective-permute-start.3 = (bf16[8,28672]{1,0:T(8,128)(2,1)S(1)}, bf16[8,28672]{1,0:T(8,128)(2,1)S(1)}, u32[]{:S(2)}, u32[]{:S(2)}) collective-permute-start(bf16[8,28672]{1,0:T(8,128)(2,1)S(1)} %fusion.45), channel_id=1, source_target_pairs={{0,64},{1,65},{2,66},{3,67},{4,68},{5,69},{6,70},{7,71},{8,72},{9,... | collective-permute-start | bytes 1376264 | tf_op jit(solution)/shard_map/ppermute | solution.py:30
  19.4 15.5 %collective-permute-start.2 = (bf16[16,14336]{1,0:T(8,128)(2,1)S(1)}, bf16[16,14336]{1,0:T(8,128)(2,1)S(1)}, u32[]{:S(2)}, u32[]{:S(2)}) collective-permute-start(bf16[16,14336]{1,0:T(8,128)(2,1)S(1)} %get-tuple-element.46), channel_id=1, source_target_pairs={{0,16},{1,17},{2,18},{3,19},{4,20},{5,21},{6,22},{7,23},{8,24},{9,... | collective-permute-start | bytes 1376264 | tf_op jit(solution)/shard_map/ppermute | solution.py:30
  21.0 14.0 %collective-permute-start.5 = (bf16[16,14336]{1,0:T(8,128)(2,1)S(1)}, bf16[16,14336]{1,0:T(8,128)(2,1)S(1)}, u32[]{:S(2)}, u32[]{:S(2)}) collective-permute-start(bf16[16,14336]{1,0:T(8,128)(2,1)S(1)} %get-tuple-element.45), channel_id=1, source_target_pairs={{0,48},{1,49},{2,50},{3,51},{4,52},{5,53},{6,54},{7,55},{8,56},{9,... | collective-permute-start | bytes 1376264 | tf_op jit(solution)/shard_map/ppermute | solution.py:30
  25.5 8.8 %collective-permute-start.4 = (f32[1]{0:T(128)}, f32[1]{0:T(128)}, u32[]{:S(2)}, u32[]{:S(2)}) collective-permute-start(f32[1]{0:T(128)} %add.229), channel_id=1, source_target_pairs={{0,16},{8,24},{16,32},{24,40},{32,48},{40,56},{48,64},{56,72},{64,... | collective-permute-start | bytes 20 | tf_op jit(solution)/shard_map/ppermute | solution.py:153
  35.8 0.9 copy-start.3
  37.7 8.6 %collective-permute-start.7 = (bf16[8,14336]{1,0:T(8,128)(2,1)}, bf16[8,14336]{1,0:T(8,128)(2,1)S(1)}, u32[]{:S(2)}, u32[]{:S(2)}) collective-permute-start(bf16[8,14336]{1,0:T(8,128)(2,1)} %get-tuple-element.32), channel_id=1, source_target_pairs={{0,64},{1,65},{2,66},{3,67},{4,68},{5,69},{6,70},{7,71},{8,72},{9,... | collective-permute-start | bytes 688136 | tf_op jit(solution)/shard_map/ppermute | solution.py:30
  39.0 5.9 %collective-permute-start.8 = (f32[1]{0:T(128)}, f32[1]{0:T(128)}, u32[]{:S(2)}, u32[]{:S(2)}) collective-permute-start(f32[1]{0:T(128)} %add.230), channel_id=1, source_target_pairs={{0,32},{8,40},{16,48},{24,56},{32,64},{40,72},{48,80},{56,88},{64,... | collective-permute-start | bytes 20 | tf_op jit(solution)/shard_map/ppermute | solution.py:153
  40.9 11.0 %collective-permute-start.6 = (bf16[8,14336]{1,0:T(8,128)(2,1)}, bf16[8,14336]{1,0:T(8,128)(2,1)S(1)}, u32[]{:S(2)}, u32[]{:S(2)}) collective-permute-start(bf16[8,14336]{1,0:T(8,128)(2,1)} %get-tuple-element.31), channel_id=1, source_target_pairs={{0,64},{1,65},{2,66},{3,67},{4,68},{5,69},{6,70},{7,71},{8,72},{9,... | collective-permute-start | bytes 688136 | tf_op jit(solution)/shard_map/ppermute | solution.py:30
  47.4 4.6 %copy-start.4 = (f32[16,14336]{1,0:T(8,128)S(1)}, f32[16,14336]{1,0:T(8,128)}, u32[]{:S(2)}) copy-start(f32[16,14336]{1,0:T(8,128)} %copy-done.3) | copy-start | bytes 2752516
  47.4 3.5 %collective-permute-start.9 = (f32[1]{0:T(128)}, f32[1]{0:T(128)}, u32[]{:S(2)}, u32[]{:S(2)}) collective-permute-start(f32[1]{0:T(128)} %add.236), channel_id=1, source_target_pairs={{0,64},{8,72},{16,80},{24,88},{32,96},{40,104},{48,112},{56,120},{... | collective-permute-start | bytes 20 | tf_op jit(solution)/shard_map/ppermute | solution.py:153
  49.6 8.3 %collective-permute-start.14 = (bf16[8,14336]{1,0:T(8,128)(2,1)}, bf16[8,14336]{1,0:T(8,128)(2,1)}, u32[]{:S(2)}, u32[]{:S(2)}) collective-permute-start(bf16[8,14336]{1,0:T(8,128)(2,1)} %fusion.82), channel_id=1, source_target_pairs={{0,32},{1,33},{2,34},{3,35},{4,36},{5,37},{6,38},{7,39},{8,40},{9,... | collective-permute-start | bytes 688136 | tf_op jit(solution)/shard_map/ppermute | solution.py:30
  53.2 11.7 %collective-permute-start.10 = (bf16[8,14336]{1,0:T(8,128)(2,1)S(1)}, bf16[8,14336]{1,0:T(8,128)(2,1)S(1)}, u32[]{:S(2)}, u32[]{:S(2)}) collective-permute-start(bf16[8,14336]{1,0:T(8,128)(2,1)S(1)} %get-tuple-element.47), channel_id=1, source_target_pairs={{0,32},{1,33},{2,34},{3,35},{4,36},{5,37},{6,38},{7,39},{8,40},{9,... | collective-permute-start | bytes 688136 | tf_op jit(solution)/shard_map/ppermute | solution.py:30
  59.2 9.3 %collective-permute-start.15 = (bf16[8,14336]{1,0:T(8,128)(2,1)S(1)}, bf16[8,14336]{1,0:T(8,128)(2,1)S(1)}, u32[]{:S(2)}, u32[]{:S(2)}) collective-permute-start(bf16[8,14336]{1,0:T(8,128)(2,1)S(1)} %get-tuple-element.38), channel_id=1, source_target_pairs={{0,64},{1,65},{2,66},{3,67},{4,68},{5,69},{6,70},{7,71},{8,72},{9,... | collective-permute-start | bytes 688136 | tf_op jit(solution)/shard_map/ppermute | solution.py:30
  60.2 10.2 %collective-permute-start.16 = (bf16[8,14336]{1,0:T(8,128)(2,1)S(1)}, bf16[8,14336]{1,0:T(8,128)(2,1)S(1)}, u32[]{:S(2)}, u32[]{:S(2)}) collective-permute-start(bf16[8,14336]{1,0:T(8,128)(2,1)S(1)} %get-tuple-element.38), channel_id=1, source_target_pairs={{0,65},{1,64},{2,67},{3,66},{4,69},{5,68},{6,71},{7,70},{8,73},{9,... | collective-permute-start | bytes 688136 | tf_op jit(solution)/shard_map/ppermute | solution.py:30
  62.5 8.0 %collective-permute-start.17 = (bf16[8,14336]{1,0:T(8,128)(2,1)S(1)}, bf16[8,14336]{1,0:T(8,128)(2,1)S(1)}, u32[]{:S(2)}, u32[]{:S(2)}) collective-permute-start(bf16[8,14336]{1,0:T(8,128)(2,1)S(1)} %get-tuple-element.38), channel_id=1, source_target_pairs={{0,1},{1,0},{2,3},{3,2},{4,5},{5,4},{6,7},{7,6},{8,9},{9,8},{10,11... | collective-permute-start | bytes 688136 | tf_op jit(solution)/shard_map/ppermute | solution.py:30
  65.2 9.8 %collective-permute-start.11 = (bf16[8,14336]{1,0:T(8,128)(2,1)S(1)}, bf16[8,14336]{1,0:T(8,128)(2,1)S(1)}, u32[]{:S(2)}, u32[]{:S(2)}) collective-permute-start(bf16[8,14336]{1,0:T(8,128)(2,1)S(1)} %get-tuple-element.40), channel_id=1, source_target_pairs={{0,2},{1,3},{2,4},{3,5},{4,6},{5,7},{6,0},{7,1},{8,10},{9,11},{10,... | collective-permute-start | bytes 688136 | tf_op jit(solution)/shard_map/ppermute | solution.py:30
  66.8 8.5 %collective-permute-start.12 = (bf16[8,14336]{1,0:T(8,128)(2,1)S(1)}, bf16[8,14336]{1,0:T(8,128)(2,1)S(1)}, u32[]{:S(2)}, u32[]{:S(2)}) collective-permute-start(bf16[8,14336]{1,0:T(8,128)(2,1)S(1)} %get-tuple-element.40), channel_id=1, source_target_pairs={{0,6},{1,7},{2,0},{3,1},{4,2},{5,3},{6,4},{7,5},{8,14},{9,15},{10,... | collective-permute-start | bytes 688136 | tf_op jit(solution)/shard_map/ppermute | solution.py:30
  68.5 12.7 %collective-permute-start.13 = (bf16[8,14336]{1,0:T(8,128)(2,1)S(1)}, bf16[8,14336]{1,0:T(8,128)(2,1)S(1)}, u32[]{:S(2)}, u32[]{:S(2)}) collective-permute-start(bf16[8,14336]{1,0:T(8,128)(2,1)S(1)} %get-tuple-element.40), channel_id=1, source_target_pairs={{0,4},{1,5},{2,6},{3,7},{4,0},{5,1},{6,2},{7,3},{8,12},{9,13},{10,... | collective-permute-start | bytes 688136 | tf_op jit(solution)/shard_map/ppermute | solution.py:30
  70.6 22.9 %collective-permute-start.18 = (bf16[4,8,14336]{2,1,0:T(8,128)(2,1)S(1)}, bf16[4,8,14336]{2,1,0:T(8,128)(2,1)S(1)}, u32[]{:S(2)}, u32[]{:S(2)}) collective-permute-start(bf16[4,8,14336]{2,1,0:T(8,128)(2,1)S(1)} %bitcast_dynamic-update-slice_fusion.10), channel_id=1, source_target_pairs={{0,2},{1,3},{2,4},{3,5},{4,6},{5,7},{6,0},{7,1},{8,10},{9,11},{10,... | collective-permute-start | bytes 2752520 | tf_op jit(solution)/shard_map/ppermute | solution.py:30
  72.0 22.1 %collective-permute-start.19 = (bf16[4,8,14336]{2,1,0:T(8,128)(2,1)S(1)}, bf16[4,8,14336]{2,1,0:T(8,128)(2,1)S(1)}, u32[]{:S(2)}, u32[]{:S(2)}) collective-permute-start(bf16[4,8,14336]{2,1,0:T(8,128)(2,1)S(1)} %bitcast_dynamic-update-slice_fusion.10), channel_id=1, source_target_pairs={{0,6},{1,7},{2,0},{3,1},{4,2},{5,3},{6,4},{7,5},{8,14},{9,15},{10,... | collective-permute-start | bytes 2752520 | tf_op jit(solution)/shard_map/ppermute | solution.py:30
  81.2 17.8 %collective-permute-start.20 = (bf16[4,8,14336]{2,1,0:T(8,128)(2,1)S(1)}, bf16[4,8,14336]{2,1,0:T(8,128)(2,1)S(1)}, u32[]{:S(2)}, u32[]{:S(2)}) collective-permute-start(bf16[4,8,14336]{2,1,0:T(8,128)(2,1)S(1)} %bitcast_dynamic-update-slice_fusion.14), channel_id=1, source_target_pairs={{0,64},{1,65},{2,66},{3,67},{4,68},{5,69},{6,70},{7,71},{8,72},{9,... | collective-permute-start | bytes 2752520 | tf_op jit(solution)/shard_map/ppermute | solution.py:30
  81.6 19.0 %collective-permute-start.21 = (bf16[4,8,14336]{2,1,0:T(8,128)(2,1)S(1)}, bf16[4,8,14336]{2,1,0:T(8,128)(2,1)S(1)}, u32[]{:S(2)}, u32[]{:S(2)}) collective-permute-start(bf16[4,8,14336]{2,1,0:T(8,128)(2,1)S(1)} %bitcast_dynamic-update-slice_fusion.14), channel_id=1, source_target_pairs={{0,65},{1,64},{2,67},{3,66},{4,69},{5,68},{6,71},{7,70},{8,73},{9,... | collective-permute-start | bytes 2752520 | tf_op jit(solution)/shard_map/ppermute | solution.py:30
  93.5 10.8 %collective-permute-start.22 = (bf16[2,8,14336]{2,1,0:T(8,128)(2,1)S(1)}, bf16[2,8,14336]{2,1,0:T(8,128)(2,1)S(1)}, u32[]{:S(2)}, u32[]{:S(2)}) collective-permute-start(bf16[2,8,14336]{2,1,0:T(8,128)(2,1)S(1)} %slice.109), channel_id=1, source_target_pairs={{0,2},{1,3},{2,4},{3,5},{4,6},{5,7},{6,0},{7,1},{8,10},{9,11},{10,... | collective-permute-start | bytes 1376264 | tf_op jit(solution)/shard_map/ppermute | solution.py:30
  94.1 11.1 %collective-permute-start.23 = (bf16[2,8,14336]{2,1,0:T(8,128)(2,1)S(1)}, bf16[2,8,14336]{2,1,0:T(8,128)(2,1)S(1)}, u32[]{:S(2)}, u32[]{:S(2)}) collective-permute-start(bf16[2,8,14336]{2,1,0:T(8,128)(2,1)S(1)} %slice.110), channel_id=1, source_target_pairs={{0,6},{1,7},{2,0},{3,1},{4,2},{5,3},{6,4},{7,5},{8,14},{9,15},{10,... | collective-permute-start | bytes 1376264 | tf_op jit(solution)/shard_map/ppermute | solution.py:30
  99.0 9.8 %collective-permute-start.24 = (bf16[2,8,14336]{2,1,0:T(8,128)(2,1)S(1)}, bf16[2,8,14336]{2,1,0:T(8,128)(2,1)S(1)}, u32[]{:S(2)}, u32[]{:S(2)}) collective-permute-start(bf16[2,8,14336]{2,1,0:T(8,128)(2,1)S(1)} %slice.111), channel_id=1, source_target_pairs={{0,64},{1,65},{2,66},{3,67},{4,68},{5,69},{6,70},{7,71},{8,72},{9,... | collective-permute-start | bytes 1376264 | tf_op jit(solution)/shard_map/ppermute | solution.py:30
  100.6 8.9 %collective-permute-start.25 = (bf16[2,8,14336]{2,1,0:T(8,128)(2,1)S(1)}, bf16[2,8,14336]{2,1,0:T(8,128)(2,1)S(1)}, u32[]{:S(2)}, u32[]{:S(2)}) collective-permute-start(bf16[2,8,14336]{2,1,0:T(8,128)(2,1)S(1)} %slice.112), channel_id=1, source_target_pairs={{0,65},{1,64},{2,67},{3,66},{4,69},{5,68},{6,71},{7,70},{8,73},{9,... | collective-permute-start | bytes 1376264 | tf_op jit(solution)/shard_map/ppermute | solution.py:30

commit v5 on v4

--- a/solution.py
+++ b/solution.py
@@ -180,7 +180,7 @@
     near_there = [moved(codes[side], near[side]) for side in range(2)]
     parts = [ab[:, part] + decoded(near_there[side], 4.0) + weight_two[0] * c[:, part] for side, part in enumerate(sides)]
     codes = [coded(other(part), 4.0) for part in parts]
-    codes, weight_two = lax.optimization_barrier((codes, weight_two))
+    codes[1], weight_two = lax.optimization_barrier((codes[1], weight_two))
     weight_three = mixed(weight_two, 4)
     there = [moved(code, across) for code in codes]
     parts = [mine(parts[side]) + decoded(there[side], 4.0) for side in range(2)]

time: 111 us -> 117 us (1.054)
  starting transfers between devices: 45.4 us -> 50.3 us
  other arithmetic: 15.7 us -> 18 us
    ppermute x4, waiting for transfers between devices: 8.13 us -> 4.58 us  [per_device(): lax.ppermute(v, 'replica', [(r, (r + steps) % REPLICAS) for r in range(RE...]
    ppermute x4, starting transfers between devices: 9.35 us -> 12.1 us  [per_device(): lax.ppermute(v, 'replica', [(r, (r + steps) % REPLICAS) for r in range(RE...]
    ppermute x22, waiting for transfers between devices: 22.8 us -> 25.3 us  [moved(): return lax.ppermute(value, AXES, pairs)]
    ppermute x22, starting transfers between devices: 36 us -> 38.2 us  [moved(): return lax.ppermute(value, AXES, pairs)]
    add x1, other arithmetic: 0.86 us -> 2.85 us  [per_device(): ab[:, part] + decoded(near_there[side], 4.0) + weight_two[0] * c[:, part]]
    convert_element_type x5 -> x6, other arithmetic: 3.34 us -> 3.58 us  [coded(): return (value * second * fourth * (fourth * fourth)).astype(jnp.bfloat16)]
where the time goes in v5:
time: 117 us
  starting transfers between devices  50.3 us (43%)
  waiting for transfers between devices  29.9 us (26%)
  other arithmetic  18 us (15%)
  local copies, waits for them, and re-layouts  10.7 us (9%)
  Pallas kernels  4.47 us (4%)
  between operations  3.55 us (3%)
    ppermute x22, starting transfers between devices, moved(): return lax.ppermute(value, AXES, pairs)  38.2 us
    ppermute x22, waiting for transfers between devices, moved(): return lax.ppermute(value, AXES, pairs)  25.3 us
    ppermute x4, starting transfers between devices, per_device(): lax.ppermute(v, 'replica', [(r, (r + steps) % REPLICAS) for r in range(RE...  12.1 us
    mul x1, other arithmetic, per_device(): d = -learn_rate / 2.0 * update(*moments(*later, 4), 3)  6.57 us
    ppermute x4, waiting for transfers between devices, per_device(): lax.ppermute(v, 'replica', [(r, (r + steps) % REPLICAS) for r in range(RE...  4.58 us
    dynamic_update_slice x5, local copies, waits for them, and re-layouts, put_two(): lax.dynamic_update_slice(out, block[None], ((y + off) % 4, first, 0, half))  4.54 us
    dynamic_update_slice x5, local copies, waits for them, and re-layouts, put_one(): lax.dynamic_update_slice(out, block[:, None], (first, (z + off) % 4, 0, 0))  4.54 us
    pallas_call x1, Pallas kernels, first_term(): pl.pallas_call(first_kernel, grid=(cols // BLOCK,), in_specs=[SMEM, spec,...  4.47 us
  transfers between devices with their start and end apart: 26, of which 11 were waited for; matrix products, arithmetic and copies ran while one was open for 20% of the time, Pallas kernels for 4%

profile of v5, /device:TPU:0, one launch (start us, length us, event | category | flops | bytes accessed | tf_op | source)
XLA Modules:
  0.0 116.9 jit_solution(18195715145211794550)
XLA Ops:
  0.7 4.5 %shard_map.56 = f32[16,28672]{1,0:T(8,128)} custom-call(f32[1]{0:T(128)S(6)} %copy.30.weight, f32[1,16,28672]{2,1,0:T(8,128)} %params.1, f32[1,16,28672]{2,1,0:T(8,128)} %first_moment.1, f32[1,16,28672]{2,1,0:T(8,128)} %second_moment.1, bf16[4,1,16,28672]{3,2,1,0:T(8,128)(2,1)} %grads.1), custom_call_target="tpu_custom_call" | custom-call | flops 9175040 | bytes 8257536 | tf_op jit(solution)/shard_map/pallas_call | solution.py:81
  5.1 1.7 %collective-permute-start = (f32[16,28672]{1,0:T(8,128)}, f32[16,28672]{1,0:T(8,128)}, u32[]{:S(2)}, u32[]{:S(2)}) collective-permute-start(f32[16,28672]{1,0:T(8,128)} %shard_map.56), channel_id=1, source_target_pairs={{0,8},{1,9},{2,10},{3,11},{4,12},{5,13},{6,14},{7,15},{8,0},{9,1},... | collective-permute-start | bytes 5505032 | tf_op jit(solution)/shard_map/ppermute | solution.py:30
  6.9 6.6 %fusion.13 = (f32[16,28672]{1,0:T(8,128)S(1)}, f32[16,28672]{1,0:T(8,128)}) fusion(bf16[4,16,28672]{2,1,0:T(8,128)(2,1)} %bitcast.97, f32[16,28672]{1,0:T(8,128)} %bitcast.101, f32[16,28672]{1,0:T(8,128)} %bitcast.99), kind=kLoop, calls=%fused_computation.31 | loop fusion | flops 19267584 | bytes 11010048 | tf_op jit(solution)/shard_map/mul | solution.py:170
  14.5 1.9 %collective-permute-start.3 = (bf16[8,28672]{1,0:T(8,128)(2,1)}, bf16[8,28672]{1,0:T(8,128)(2,1)S(1)}, u32[]{:S(2)}, u32[]{:S(2)}) collective-permute-start(bf16[8,28672]{1,0:T(8,128)(2,1)} %fusion.45), channel_id=1, source_target_pairs={{0,64},{1,65},{2,66},{3,67},{4,68},{5,69},{6,70},{7,71},{8,72},{9,... | collective-permute-start | bytes 1376264 | tf_op jit(solution)/shard_map/ppermute | solution.py:30
  17.1 3.5 %fusion.24 = f32[16,28672]{1,0:T(8,128)S(1)} fusion(f32[16,28672]{1,0:T(8,128)S(1)} %bitcast.100, f32[16,28672]{1,0:T(8,128)S(1)} %bitcast.102, f32[16,28672]{1,0:T(8,128)S(1)} %copy-done.4, f32[16,28672]{1,0:T(8,128)} %collective-permute-done, bf16[4,16,28672]{2,1,0:T(8,128)(2,1)S(1)} %bitcast.98, f32[]{:T(128)} %bitcast.11), kind=kLoop, calls=%fused_computation.42 | loop fusion | flops 10551296 | bytes 11010052 | tf_op jit(solution)/shard_map/add | solution.py:176
  23.2 1.5 %collective-permute-start.2 = (bf16[16,14336]{1,0:T(8,128)(2,1)}, bf16[16,14336]{1,0:T(8,128)(2,1)S(1)}, u32[]{:S(2)}, u32[]{:S(2)}) collective-permute-start(bf16[16,14336]{1,0:T(8,128)(2,1)} %get-tuple-element.43), channel_id=1, source_target_pairs={{0,16},{1,17},{2,18},{3,19},{4,20},{5,21},{6,22},{7,23},{8,24},{9,... | collective-permute-start | bytes 1376264 | tf_op jit(solution)/shard_map/ppermute | solution.py:30
  24.6 1.8 %collective-permute-start.6 = (bf16[16,14336]{1,0:T(8,128)(2,1)}, bf16[16,14336]{1,0:T(8,128)(2,1)S(1)}, u32[]{:S(2)}, u32[]{:S(2)}) collective-permute-start(bf16[16,14336]{1,0:T(8,128)(2,1)} %get-tuple-element.44), channel_id=1, source_target_pairs={{0,48},{1,49},{2,50},{3,51},{4,52},{5,53},{6,54},{7,55},{8,56},{9,... | collective-permute-start | bytes 1376264 | tf_op jit(solution)/shard_map/ppermute | solution.py:30
  27.3 7.4 %collective-permute-start.4 = (f32[1]{0:T(128)}, f32[1]{0:T(128)}, u32[]{:S(2)}, u32[]{:S(2)}) collective-permute-start(f32[1]{0:T(128)} %add.229), channel_id=1, source_target_pairs={{0,16},{8,24},{16,32},{24,40},{32,48},{40,56},{48,64},{56,72},{64,... | collective-permute-start | bytes 20 | tf_op jit(solution)/shard_map/ppermute | solution.py:153
  34.7 3.0 %collective-permute-done.4 = f32[1]{0:T(128)} collective-permute-done((f32[1]{0:T(128)}, f32[1]{0:T(128)}, u32[]{:S(2)}, u32[]{:S(2)}) %collective-permute-start.4) | collective-permute-done | bytes 36 | tf_op jit(solution)/shard_map/ppermute | solution.py:153
  38.3 2.8 %fusion.53 = (f32[16,14336]{1,0:T(8,128)S(1)}, f32[16,14336]{1,0:T(8,128)S(1)}) fusion(bf16[16,14336]{1,0:T(8,128)(2,1)S(1)} %collective-permute-done.2, f32[16,28672]{1,0:T(8,128)} %get-tuple-element.29, f32[16,28672]{1,0:T(8,128)} %copy-done.1, f32[]{:T(128)} %bitcast.16, bf16[16,14336]{1,0:T(8,128)(2,1)S(1)} %collective-permute-done.6), kind=kLoop, calls=%fused_computation.87 | loop fusion | flops 4587520 | bytes 6422532 | tf_op jit(solution)/shard_map/add | solution.py:181
  41.3 2.1 %collective-permute-start.8 = (f32[1]{0:T(128)}, f32[1]{0:T(128)}, u32[]{:S(2)}, u32[]{:S(2)}) collective-permute-start(f32[1]{0:T(128)} %add.230), channel_id=1, source_target_pairs={{0,32},{8,40},{16,48},{24,56},{32,64},{40,72},{48,80},{56,88},{64,... | collective-permute-start | bytes 20 | tf_op jit(solution)/shard_map/ppermute | solution.py:153
  43.4 1.6 %collective-permute-start.7 = (bf16[8,14336]{1,0:T(8,128)(2,1)S(1)}, bf16[8,14336]{1,0:T(8,128)(2,1)S(1)}, u32[]{:S(2)}, u32[]{:S(2)}) collective-permute-start(bf16[8,14336]{1,0:T(8,128)(2,1)S(1)} %fusion.79), channel_id=1, source_target_pairs={{0,64},{1,65},{2,66},{3,67},{4,68},{5,69},{6,70},{7,71},{8,72},{9,... | collective-permute-start | bytes 688136 | tf_op jit(solution)/shard_map/ppermute | solution.py:30
  45.7 1.6 %collective-permute-done.8 = f32[1]{0:T(128)} collective-permute-done((f32[1]{0:T(128)}, f32[1]{0:T(128)}, u32[]{:S(2)}, u32[]{:S(2)}) %collective-permute-start.8) | collective-permute-done | bytes 36 | tf_op jit(solution)/shard_map/ppermute | solution.py:153
  48.0 3.5 %collective-permute-done.7 = bf16[8,14336]{1,0:T(8,128)(2,1)S(1)} collective-permute-done((bf16[8,14336]{1,0:T(8,128)(2,1)S(1)}, bf16[8,14336]{1,0:T(8,128)(2,1)S(1)}, u32[]{:S(2)}, u32[]{:S(2)}) %collective-permute-start.7) | collective-permute-done | bytes 229408 | tf_op jit(solution)/shard_map/ppermute | solution.py:30
  51.8 2.6 %collective-permute-start.9 = (f32[1]{0:T(128)}, f32[1]{0:T(128)}, u32[]{:S(2)}, u32[]{:S(2)}) collective-permute-start(f32[1]{0:T(128)} %add.236), channel_id=1, source_target_pairs={{0,64},{8,72},{16,80},{24,88},{32,96},{40,104},{48,112},{56,120},{... | collective-permute-start | bytes 20 | tf_op jit(solution)/shard_map/ppermute | solution.py:153
  54.4 2.7 %collective-permute-start.14 = (bf16[8,14336]{1,0:T(8,128)(2,1)S(1)}, bf16[8,14336]{1,0:T(8,128)(2,1)S(1)}, u32[]{:S(2)}, u32[]{:S(2)}) collective-permute-start(bf16[8,14336]{1,0:T(8,128)(2,1)S(1)} %fusion.82), channel_id=1, source_target_pairs={{0,32},{1,33},{2,34},{3,35},{4,36},{5,37},{6,38},{7,39},{8,40},{9,... | collective-permute-start | bytes 688136 | tf_op jit(solution)/shard_map/ppermute | solution.py:30
  59.5 2.0 %collective-permute-start.10 = (bf16[8,14336]{1,0:T(8,128)(2,1)S(1)}, bf16[8,14336]{1,0:T(8,128)(2,1)S(1)}, u32[]{:S(2)}, u32[]{:S(2)}) collective-permute-start(bf16[8,14336]{1,0:T(8,128)(2,1)S(1)} %get-tuple-element.45), channel_id=1, source_target_pairs={{0,32},{1,33},{2,34},{3,35},{4,36},{5,37},{6,38},{7,39},{8,40},{9,... | collective-permute-start | bytes 688136 | tf_op jit(solution)/shard_map/ppermute | solution.py:30
  61.5 2.2 %collective-permute-done.14 = bf16[8,14336]{1,0:T(8,128)(2,1)S(1)} collective-permute-done((bf16[8,14336]{1,0:T(8,128)(2,1)S(1)}, bf16[8,14336]{1,0:T(8,128)(2,1)S(1)}, u32[]{:S(2)}, u32[]{:S(2)}) %collective-permute-start.14) | collective-permute-done | bytes 229408 | tf_op jit(solution)/shard_map/ppermute | solution.py:30
  65.3 2.2 %collective-permute-start.16 = (bf16[8,14336]{1,0:T(8,128)(2,1)S(1)}, bf16[8,14336]{1,0:T(8,128)(2,1)S(1)}, u32[]{:S(2)}, u32[]{:S(2)}) collective-permute-start(bf16[8,14336]{1,0:T(8,128)(2,1)S(1)} %get-tuple-element.36), channel_id=1, source_target_pairs={{0,65},{1,64},{2,67},{3,66},{4,69},{5,68},{6,71},{7,70},{8,73},{9,... | collective-permute-start | bytes 688136 | tf_op jit(solution)/shard_map/ppermute | solution.py:30
  67.5 1.8 %collective-permute-start.17 = (bf16[8,14336]{1,0:T(8,128)(2,1)S(1)}, bf16[8,14336]{1,0:T(8,128)(2,1)S(1)}, u32[]{:S(2)}, u32[]{:S(2)}) collective-permute-start(bf16[8,14336]{1,0:T(8,128)(2,1)S(1)} %get-tuple-element.36), channel_id=1, source_target_pairs={{0,1},{1,0},{2,3},{3,2},{4,5},{5,4},{6,7},{7,6},{8,9},{9,8},{10,11... | collective-permute-start | bytes 688136 | tf_op jit(solution)/shard_map/ppermute | solution.py:30
  69.6 1.6 %collective-permute-start.11 = (bf16[8,14336]{1,0:T(8,128)(2,1)S(1)}, bf16[8,14336]{1,0:T(8,128)(2,1)S(1)}, u32[]{:S(2)}, u32[]{:S(2)}) collective-permute-start(bf16[8,14336]{1,0:T(8,128)(2,1)S(1)} %get-tuple-element.38), channel_id=1, source_target_pairs={{0,2},{1,3},{2,4},{3,5},{4,6},{5,7},{6,0},{7,1},{8,10},{9,11},{10,... | collective-permute-start | bytes 688136 | tf_op jit(solution)/shard_map/ppermute | solution.py:30
  71.3 1.7 %collective-permute-start.12 = (bf16[8,14336]{1,0:T(8,128)(2,1)S(1)}, bf16[8,14336]{1,0:T(8,128)(2,1)S(1)}, u32[]{:S(2)}, u32[]{:S(2)}) collective-permute-start(bf16[8,14336]{1,0:T(8,128)(2,1)S(1)} %get-tuple-element.38), channel_id=1, source_target_pairs={{0,6},{1,7},{2,0},{3,1},{4,2},{5,3},{6,4},{7,5},{8,14},{9,15},{10,... | collective-permute-start | bytes 688136 | tf_op jit(solution)/shard_map/ppermute | solution.py:30
  72.9 2.0 %collective-permute-start.13 = (bf16[8,14336]{1,0:T(8,128)(2,1)S(1)}, bf16[8,14336]{1,0:T(8,128)(2,1)S(1)}, u32[]{:S(2)}, u32[]{:S(2)}) collective-permute-start(bf16[8,14336]{1,0:T(8,128)(2,1)S(1)} %get-tuple-element.38), channel_id=1, source_target_pairs={{0,4},{1,5},{2,6},{3,7},{4,0},{5,1},{6,2},{7,3},{8,12},{9,13},{10,... | collective-permute-start | bytes 688136 | tf_op jit(solution)/shard_map/ppermute | solution.py:30
  75.4 1.6 %collective-permute-start.18 = (bf16[4,8,14336]{2,1,0:T(8,128)(2,1)S(1)}, bf16[4,8,14336]{2,1,0:T(8,128)(2,1)S(1)}, u32[]{:S(2)}, u32[]{:S(2)}) collective-permute-start(bf16[4,8,14336]{2,1,0:T(8,128)(2,1)S(1)} %bitcast_dynamic-update-slice_fusion.10), channel_id=1, source_target_pairs={{0,2},{1,3},{2,4},{3,5},{4,6},{5,7},{6,0},{7,1},{8,10},{9,11},{10,... | collective-permute-start | bytes 2752520 | tf_op jit(solution)/shard_map/ppermute | solution.py:30
  77.0 1.7 %collective-permute-start.19 = (bf16[4,8,14336]{2,1,0:T(8,128)(2,1)S(1)}, bf16[4,8,14336]{2,1,0:T(8,128)(2,1)S(1)}, u32[]{:S(2)}, u32[]{:S(2)}) collective-permute-start(bf16[4,8,14336]{2,1,0:T(8,128)(2,1)S(1)} %bitcast_dynamic-update-slice_fusion.10), channel_id=1, source_target_pairs={{0,6},{1,7},{2,0},{3,1},{4,2},{5,3},{6,4},{7,5},{8,14},{9,15},{10,... | collective-permute-start | bytes 2752520 | tf_op jit(solution)/shard_map/ppermute | solution.py:30
  79.8 5.8 %collective-permute-done.13 = bf16[8,14336]{1,0:T(8,128)(2,1)S(1)} collective-permute-done((bf16[8,14336]{1,0:T(8,128)(2,1)S(1)}, bf16[8,14336]{1,0:T(8,128)(2,1)S(1)}, u32[]{:S(2)}, u32[]{:S(2)}) %collective-permute-start.13) | collective-permute-done | bytes 229408 | tf_op jit(solution)/shard_map/ppermute | solution.py:30
  86.7 2.2 %collective-permute-start.21 = (bf16[4,8,14336]{2,1,0:T(8,128)(2,1)S(1)}, bf16[4,8,14336]{2,1,0:T(8,128)(2,1)S(1)}, u32[]{:S(2)}, u32[]{:S(2)}) collective-permute-start(bf16[4,8,14336]{2,1,0:T(8,128)(2,1)S(1)} %bitcast_dynamic-update-slice_fusion.14), channel_id=1, source_target_pairs={{0,65},{1,64},{2,67},{3,66},{4,69},{5,68},{6,71},{7,70},{8,73},{9,... | collective-permute-start | bytes 2752520 | tf_op jit(solution)/shard_map/ppermute | solution.py:30
  90.9 7.4 %collective-permute-done.18 = bf16[4,8,14336]{2,1,0:T(8,128)(2,1)S(1)} collective-permute-done((bf16[4,8,14336]{2,1,0:T(8,128)(2,1)S(1)}, bf16[4,8,14336]{2,1,0:T(8,128)(2,1)S(1)}, u32[]{:S(2)}, u32[]{:S(2)}) %collective-permute-start.18) | collective-permute-done | bytes 917536 | tf_op jit(solution)/shard_map/ppermute | solution.py:30
  99.0 2.8 %collective-permute-start.23 = (bf16[2,8,14336]{2,1,0:T(8,128)(2,1)S(1)}, bf16[2,8,14336]{2,1,0:T(8,128)(2,1)S(1)}, u32[]{:S(2)}, u32[]{:S(2)}) collective-permute-start(bf16[2,8,14336]{2,1,0:T(8,128)(2,1)S(1)} %slice.110), channel_id=1, source_target_pairs={{0,6},{1,7},{2,0},{3,1},{4,2},{5,3},{6,4},{7,5},{8,14},{9,15},{10,... | collective-permute-start | bytes 1376264 | tf_op jit(solution)/shard_map/ppermute | solution.py:30
  103.8 1.6 %collective-permute-start.24 = (bf16[2,8,14336]{2,1,0:T(8,128)(2,1)S(1)}, bf16[2,8,14336]{2,1,0:T(8,128)(2,1)S(1)}, u32[]{:S(2)}, u32[]{:S(2)}) collective-permute-start(bf16[2,8,14336]{2,1,0:T(8,128)(2,1)S(1)} %slice.111), channel_id=1, source_target_pairs={{0,64},{1,65},{2,66},{3,67},{4,68},{5,69},{6,70},{7,71},{8,72},{9,... | collective-permute-start | bytes 1376264 | tf_op jit(solution)/shard_map/ppermute | solution.py:30
  105.4 2.3 %collective-permute-start.25 = (bf16[2,8,14336]{2,1,0:T(8,128)(2,1)S(1)}, bf16[2,8,14336]{2,1,0:T(8,128)(2,1)S(1)}, u32[]{:S(2)}, u32[]{:S(2)}) collective-permute-start(bf16[2,8,14336]{2,1,0:T(8,128)(2,1)S(1)} %slice.112), channel_id=1, source_target_pairs={{0,65},{1,64},{2,67},{3,66},{4,69},{5,68},{6,71},{7,70},{8,73},{9,... | collective-permute-start | bytes 1376264 | tf_op jit(solution)/shard_map/ppermute | solution.py:30
  111.2 4.1 %collective-permute-done.24 = bf16[2,8,14336]{2,1,0:T(8,128)(2,1)S(1)} collective-permute-done((bf16[2,8,14336]{2,1,0:T(8,128)(2,1)S(1)}, bf16[2,8,14336]{2,1,0:T(8,128)(2,1)S(1)}, u32[]{:S(2)}, u32[]{:S(2)}) %collective-permute-start.24) | collective-permute-done | bytes 458784 | tf_op jit(solution)/shard_map/ppermute | solution.py:30
  (67 shorter events, 21.8 us)
Async XLA Ops:
  0.0 16.4 %collective-permute-start.1 = (f32[1]{0:T(128)}, f32[1]{0:T(128)}, u32[]{:S(2)}, u32[]{:S(2)}) collective-permute-start(f32[1]{0:T(128)} %param.9), channel_id=1, source_target_pairs={{0,8},{8,16},{16,24},{24,32},{32,40},{40,48},{48,56},{56,64},{64,7... | collective-permute-start | bytes 20 | tf_op jit(solution)/shard_map/ppermute | solution.py:153
  5.1 11.9 %collective-permute-start = (f32[16,28672]{1,0:T(8,128)}, f32[16,28672]{1,0:T(8,128)}, u32[]{:S(2)}, u32[]{:S(2)}) collective-permute-start(f32[16,28672]{1,0:T(8,128)} %shard_map.56), channel_id=1, source_target_pairs={{0,8},{1,9},{2,10},{3,11},{4,12},{5,13},{6,14},{7,15},{8,0},{9,1},... | collective-permute-start | bytes 5505032 | tf_op jit(solution)/shard_map/ppermute | solution.py:30
  6.8 10.2 %copy-start = (bf16[4,1,16,28672]{3,2,1,0:T(8,128)(2,1)S(1)}, bf16[4,1,16,28672]{3,2,1,0:T(8,128)(2,1)}, u32[]{:S(2)}) copy-start(bf16[4,1,16,28672]{3,2,1,0:T(8,128)(2,1)} %grads.1) | copy-start | bytes 11010052
  6.9 10.2 %copy-start.3 = (f32[1,16,28672]{2,1,0:T(8,128)S(1)}, f32[1,16,28672]{2,1,0:T(8,128)}, u32[]{:S(2)}) copy-start(f32[1,16,28672]{2,1,0:T(8,128)} %first_moment.1) | copy-start | bytes 5505028
  6.9 10.2 %copy-start.4 = (f32[16,28672]{1,0:T(8,128)S(1)}, f32[16,28672]{1,0:T(8,128)}, u32[]{:S(2)}) copy-start(f32[16,28672]{1,0:T(8,128)} %shard_map.56) | copy-start | bytes 5505028
  13.4 3.6 %copy-start.2 = (f32[1,16,28672]{2,1,0:T(8,128)S(1)}, f32[1,16,28672]{2,1,0:T(8,128)}, u32[]{:S(2)}) copy-start(f32[1,16,28672]{2,1,0:T(8,128)} %second_moment.1) | copy-start | bytes 5505028
  14.5 12.8 %collective-permute-start.3 = (bf16[8,28672]{1,0:T(8,128)(2,1)}, bf16[8,28672]{1,0:T(8,128)(2,1)S(1)}, u32[]{:S(2)}, u32[]{:S(2)}) collective-permute-start(bf16[8,28672]{1,0:T(8,128)(2,1)} %fusion.45), channel_id=1, source_target_pairs={{0,64},{1,65},{2,66},{3,67},{4,68},{5,69},{6,70},{7,71},{8,72},{9,... | collective-permute-start | bytes 1376264 | tf_op jit(solution)/shard_map/ppermute | solution.py:30
  20.5 1.2 %copy-start.1 = (f32[16,28672]{1,0:T(8,128)}, f32[16,28672]{1,0:T(8,128)S(1)}, u32[]{:S(2)}) copy-start(f32[16,28672]{1,0:T(8,128)S(1)} %fusion.24) | copy-start | bytes 5505028
  23.2 15.1 %collective-permute-start.2 = (bf16[16,14336]{1,0:T(8,128)(2,1)}, bf16[16,14336]{1,0:T(8,128)(2,1)S(1)}, u32[]{:S(2)}, u32[]{:S(2)}) collective-permute-start(bf16[16,14336]{1,0:T(8,128)(2,1)} %get-tuple-element.43), channel_id=1, source_target_pairs={{0,16},{1,17},{2,18},{3,19},{4,20},{5,21},{6,22},{7,23},{8,24},{9,... | collective-permute-start | bytes 1376264 | tf_op jit(solution)/shard_map/ppermute | solution.py:30
  24.6 13.7 %collective-permute-start.6 = (bf16[16,14336]{1,0:T(8,128)(2,1)}, bf16[16,14336]{1,0:T(8,128)(2,1)S(1)}, u32[]{:S(2)}, u32[]{:S(2)}) collective-permute-start(bf16[16,14336]{1,0:T(8,128)(2,1)} %get-tuple-element.44), channel_id=1, source_target_pairs={{0,48},{1,49},{2,50},{3,51},{4,52},{5,53},{6,54},{7,55},{8,56},{9,... | collective-permute-start | bytes 1376264 | tf_op jit(solution)/shard_map/ppermute | solution.py:30
  27.3 10.3 %collective-permute-start.4 = (f32[1]{0:T(128)}, f32[1]{0:T(128)}, u32[]{:S(2)}, u32[]{:S(2)}) collective-permute-start(f32[1]{0:T(128)} %add.229), channel_id=1, source_target_pairs={{0,16},{8,24},{16,32},{24,40},{32,48},{40,56},{48,64},{56,72},{64,... | collective-permute-start | bytes 20 | tf_op jit(solution)/shard_map/ppermute | solution.py:153
  41.3 6.0 %collective-permute-start.8 = (f32[1]{0:T(128)}, f32[1]{0:T(128)}, u32[]{:S(2)}, u32[]{:S(2)}) collective-permute-start(f32[1]{0:T(128)} %add.230), channel_id=1, source_target_pairs={{0,32},{8,40},{16,48},{24,56},{32,64},{40,72},{48,80},{56,88},{64,... | collective-permute-start | bytes 20 | tf_op jit(solution)/shard_map/ppermute | solution.py:153
  43.4 8.0 %collective-permute-start.7 = (bf16[8,14336]{1,0:T(8,128)(2,1)S(1)}, bf16[8,14336]{1,0:T(8,128)(2,1)S(1)}, u32[]{:S(2)}, u32[]{:S(2)}) collective-permute-start(bf16[8,14336]{1,0:T(8,128)(2,1)S(1)} %fusion.79), channel_id=1, source_target_pairs={{0,64},{1,65},{2,66},{3,67},{4,68},{5,69},{6,70},{7,71},{8,72},{9,... | collective-permute-start | bytes 688136 | tf_op jit(solution)/shard_map/ppermute | solution.py:30
  45.1 13.1 %collective-permute-start.5 = (bf16[8,14336]{1,0:T(8,128)(2,1)S(1)}, bf16[8,14336]{1,0:T(8,128)(2,1)S(1)}, u32[]{:S(2)}, u32[]{:S(2)}) collective-permute-start(bf16[8,14336]{1,0:T(8,128)(2,1)S(1)} %fusion.76), channel_id=1, source_target_pairs={{0,64},{1,65},{2,66},{3,67},{4,68},{5,69},{6,70},{7,71},{8,72},{9,... | collective-permute-start | bytes 688136 | tf_op jit(solution)/shard_map/ppermute | solution.py:30
  51.8 5.3 %collective-permute-start.9 = (f32[1]{0:T(128)}, f32[1]{0:T(128)}, u32[]{:S(2)}, u32[]{:S(2)}) collective-permute-start(f32[1]{0:T(128)} %add.236), channel_id=1, source_target_pairs={{0,64},{8,72},{16,80},{24,88},{32,96},{40,104},{48,112},{56,120},{... | collective-permute-start | bytes 20 | tf_op jit(solution)/shard_map/ppermute | solution.py:153
  54.4 9.3 %collective-permute-start.14 = (bf16[8,14336]{1,0:T(8,128)(2,1)S(1)}, bf16[8,14336]{1,0:T(8,128)(2,1)S(1)}, u32[]{:S(2)}, u32[]{:S(2)}) collective-permute-start(bf16[8,14336]{1,0:T(8,128)(2,1)S(1)} %fusion.82), channel_id=1, source_target_pairs={{0,32},{1,33},{2,34},{3,35},{4,36},{5,37},{6,38},{7,39},{8,40},{9,... | collective-permute-start | bytes 688136 | tf_op jit(solution)/shard_map/ppermute | solution.py:30
  59.5 9.8 %collective-permute-start.10 = (bf16[8,14336]{1,0:T(8,128)(2,1)S(1)}, bf16[8,14336]{1,0:T(8,128)(2,1)S(1)}, u32[]{:S(2)}, u32[]{:S(2)}) collective-permute-start(bf16[8,14336]{1,0:T(8,128)(2,1)S(1)} %get-tuple-element.45), channel_id=1, source_target_pairs={{0,32},{1,33},{2,34},{3,35},{4,36},{5,37},{6,38},{7,39},{8,40},{9,... | collective-permute-start | bytes 688136 | tf_op jit(solution)/shard_map/ppermute | solution.py:30
  63.9 9.0 %collective-permute-start.15 = (bf16[8,14336]{1,0:T(8,128)(2,1)S(1)}, bf16[8,14336]{1,0:T(8,128)(2,1)S(1)}, u32[]{:S(2)}, u32[]{:S(2)}) collective-permute-start(bf16[8,14336]{1,0:T(8,128)(2,1)S(1)} %get-tuple-element.36), channel_id=1, source_target_pairs={{0,64},{1,65},{2,66},{3,67},{4,68},{5,69},{6,70},{7,71},{8,72},{9,... | collective-permute-start | bytes 688136 | tf_op jit(solution)/shard_map/ppermute | solution.py:30
  65.3 9.6 %collective-permute-start.16 = (bf16[8,14336]{1,0:T(8,128)(2,1)S(1)}, bf16[8,14336]{1,0:T(8,128)(2,1)S(1)}, u32[]{:S(2)}, u32[]{:S(2)}) collective-permute-start(bf16[8,14336]{1,0:T(8,128)(2,1)S(1)} %get-tuple-element.36), channel_id=1, source_target_pairs={{0,65},{1,64},{2,67},{3,66},{4,69},{5,68},{6,71},{7,70},{8,73},{9,... | collective-permute-start | bytes 688136 | tf_op jit(solution)/shard_map/ppermute | solution.py:30
  67.5 7.8 %collective-permute-start.17 = (bf16[8,14336]{1,0:T(8,128)(2,1)S(1)}, bf16[8,14336]{1,0:T(8,128)(2,1)S(1)}, u32[]{:S(2)}, u32[]{:S(2)}) collective-permute-start(bf16[8,14336]{1,0:T(8,128)(2,1)S(1)} %get-tuple-element.36), channel_id=1, source_target_pairs={{0,1},{1,0},{2,3},{3,2},{4,5},{5,4},{6,7},{7,6},{8,9},{9,8},{10,11... | collective-permute-start | bytes 688136 | tf_op jit(solution)/shard_map/ppermute | solution.py:30
  69.6 9.8 %collective-permute-start.11 = (bf16[8,14336]{1,0:T(8,128)(2,1)S(1)}, bf16[8,14336]{1,0:T(8,128)(2,1)S(1)}, u32[]{:S(2)}, u32[]{:S(2)}) collective-permute-start(bf16[8,14336]{1,0:T(8,128)(2,1)S(1)} %get-tuple-element.38), channel_id=1, source_target_pairs={{0,2},{1,3},{2,4},{3,5},{4,6},{5,7},{6,0},{7,1},{8,10},{9,11},{10,... | collective-permute-start | bytes 688136 | tf_op jit(solution)/shard_map/ppermute | solution.py:30
  71.3 8.5 %collective-permute-start.12 = (bf16[8,14336]{1,0:T(8,128)(2,1)S(1)}, bf16[8,14336]{1,0:T(8,128)(2,1)S(1)}, u32[]{:S(2)}, u32[]{:S(2)}) collective-permute-start(bf16[8,14336]{1,0:T(8,128)(2,1)S(1)} %get-tuple-element.38), channel_id=1, source_target_pairs={{0,6},{1,7},{2,0},{3,1},{4,2},{5,3},{6,4},{7,5},{8,14},{9,15},{10,... | collective-permute-start | bytes 688136 | tf_op jit(solution)/shard_map/ppermute | solution.py:30
  72.9 12.7 %collective-permute-start.13 = (bf16[8,14336]{1,0:T(8,128)(2,1)S(1)}, bf16[8,14336]{1,0:T(8,128)(2,1)S(1)}, u32[]{:S(2)}, u32[]{:S(2)}) collective-permute-start(bf16[8,14336]{1,0:T(8,128)(2,1)S(1)} %get-tuple-element.38), channel_id=1, source_target_pairs={{0,4},{1,5},{2,6},{3,7},{4,0},{5,1},{6,2},{7,3},{8,12},{9,13},{10,... | collective-permute-start | bytes 688136 | tf_op jit(solution)/shard_map/ppermute | solution.py:30
  75.4 22.9 %collective-permute-start.18 = (bf16[4,8,14336]{2,1,0:T(8,128)(2,1)S(1)}, bf16[4,8,14336]{2,1,0:T(8,128)(2,1)S(1)}, u32[]{:S(2)}, u32[]{:S(2)}) collective-permute-start(bf16[4,8,14336]{2,1,0:T(8,128)(2,1)S(1)} %bitcast_dynamic-update-slice_fusion.10), channel_id=1, source_target_pairs={{0,2},{1,3},{2,4},{3,5},{4,6},{5,7},{6,0},{7,1},{8,10},{9,11},{10,... | collective-permute-start | bytes 2752520 | tf_op jit(solution)/shard_map/ppermute | solution.py:30
  77.0 21.9 %collective-permute-start.19 = (bf16[4,8,14336]{2,1,0:T(8,128)(2,1)S(1)}, bf16[4,8,14336]{2,1,0:T(8,128)(2,1)S(1)}, u32[]{:S(2)}, u32[]{:S(2)}) collective-permute-start(bf16[4,8,14336]{2,1,0:T(8,128)(2,1)S(1)} %bitcast_dynamic-update-slice_fusion.10), channel_id=1, source_target_pairs={{0,6},{1,7},{2,0},{3,1},{4,2},{5,3},{6,4},{7,5},{8,14},{9,15},{10,... | collective-permute-start | bytes 2752520 | tf_op jit(solution)/shard_map/ppermute | solution.py:30
  85.6 18.1 %collective-permute-start.20 = (bf16[4,8,14336]{2,1,0:T(8,128)(2,1)S(1)}, bf16[4,8,14336]{2,1,0:T(8,128)(2,1)S(1)}, u32[]{:S(2)}, u32[]{:S(2)}) collective-permute-start(bf16[4,8,14336]{2,1,0:T(8,128)(2,1)S(1)} %bitcast_dynamic-update-slice_fusion.14), channel_id=1, source_target_pairs={{0,64},{1,65},{2,66},{3,67},{4,68},{5,69},{6,70},{7,71},{8,72},{9,... | collective-permute-start | bytes 2752520 | tf_op jit(solution)/shard_map/ppermute | solution.py:30
  86.7 18.6 %collective-permute-start.21 = (bf16[4,8,14336]{2,1,0:T(8,128)(2,1)S(1)}, bf16[4,8,14336]{2,1,0:T(8,128)(2,1)S(1)}, u32[]{:S(2)}, u32[]{:S(2)}) collective-permute-start(bf16[4,8,14336]{2,1,0:T(8,128)(2,1)S(1)} %bitcast_dynamic-update-slice_fusion.14), channel_id=1, source_target_pairs={{0,65},{1,64},{2,67},{3,66},{4,69},{5,68},{6,71},{7,70},{8,73},{9,... | collective-permute-start | bytes 2752520 | tf_op jit(solution)/shard_map/ppermute | solution.py:30
  98.4 11.2 %collective-permute-start.22 = (bf16[2,8,14336]{2,1,0:T(8,128)(2,1)S(1)}, bf16[2,8,14336]{2,1,0:T(8,128)(2,1)S(1)}, u32[]{:S(2)}, u32[]{:S(2)}) collective-permute-start(bf16[2,8,14336]{2,1,0:T(8,128)(2,1)S(1)} %slice.109), channel_id=1, source_target_pairs={{0,2},{1,3},{2,4},{3,5},{4,6},{5,7},{6,0},{7,1},{8,10},{9,11},{10,... | collective-permute-start | bytes 1376264 | tf_op jit(solution)/shard_map/ppermute | solution.py:30
  99.0 11.4 %collective-permute-start.23 = (bf16[2,8,14336]{2,1,0:T(8,128)(2,1)S(1)}, bf16[2,8,14336]{2,1,0:T(8,128)(2,1)S(1)}, u32[]{:S(2)}, u32[]{:S(2)}) collective-permute-start(bf16[2,8,14336]{2,1,0:T(8,128)(2,1)S(1)} %slice.110), channel_id=1, source_target_pairs={{0,6},{1,7},{2,0},{3,1},{4,2},{5,3},{6,4},{7,5},{8,14},{9,15},{10,... | collective-permute-start | bytes 1376264 | tf_op jit(solution)/shard_map/ppermute | solution.py:30
  103.8 11.5 %collective-permute-start.24 = (bf16[2,8,14336]{2,1,0:T(8,128)(2,1)S(1)}, bf16[2,8,14336]{2,1,0:T(8,128)(2,1)S(1)}, u32[]{:S(2)}, u32[]{:S(2)}) collective-permute-start(bf16[2,8,14336]{2,1,0:T(8,128)(2,1)S(1)} %slice.111), channel_id=1, source_target_pairs={{0,64},{1,65},{2,66},{3,67},{4,68},{5,69},{6,70},{7,71},{8,72},{9,... | collective-permute-start | bytes 1376264 | tf_op jit(solution)/shard_map/ppermute | solution.py:30
  105.4 10.7 %collective-permute-start.25 = (bf16[2,8,14336]{2,1,0:T(8,128)(2,1)S(1)}, bf16[2,8,14336]{2,1,0:T(8,128)(2,1)S(1)}, u32[]{:S(2)}, u32[]{:S(2)}) collective-permute-start(bf16[2,8,14336]{2,1,0:T(8,128)(2,1)S(1)} %slice.112), channel_id=1, source_target_pairs={{0,65},{1,64},{2,67},{3,66},{4,69},{5,68},{6,71},{7,70},{8,73},{9,... | collective-permute-start | bytes 1376264 | tf_op jit(solution)/shard_map/ppermute | solution.py:30
